TPU v7x, 256 devices: a whole 4x4x8 slice. The times are simulated.
256 devices in a mesh: expert: 64 (over z_hi, y, x, core), dp: 4 (over z_lo).
Axes of the slice: x: 4, y: 4, z: 8 (z_hi: 2, z_lo: 4; z = z_hi * 4 + z_lo), core: 2. Of those that a mesh axis runs over, the one named last changes fastest.
Arguments:
- tokens: bfloat16 [8192, 4096], P('expert'), may hold values from -6 to 6
- cotangent: bfloat16 [8192, 4096], P('expert'), may hold values from -3 to 3
- gate_weight: bfloat16 [64, 768, 4096], P('expert', 'dp'), may hold values from -0.09375 to 0.09375
- up_weight: bfloat16 [64, 768, 4096], P('expert', 'dp'), may hold values from -0.09375 to 0.09375
- down_weight: bfloat16 [64, 768, 4096], P('expert', 'dp'), may hold values from -0.21875 to 0.21875
- expert_ids: int32 [8192, 4], P('expert'), may hold values from 0 to 63, all different within a row; in each aligned block of 128 rows (0 to 127, 128 to 255, ...) at most 10 rows name the same one
- gates: bfloat16 [8192, 4], P('expert'), may hold values from 0.049804688 to 0.59765625
- swap_flags: int32 [32], replicated, may hold values 0 or 1
Outputs:
- input_grad: bfloat16 [8192, 4096], P('expert', 'dp')
- gate_grad: bfloat16 [8192, 4], P('expert')
- gate_weight_grad: bfloat16 [64, 768, 4096], P('expert', 'dp')
- up_weight_grad: bfloat16 [64, 768, 4096], P('expert', 'dp')
- down_weight_grad: bfloat16 [64, 768, 4096], P('expert', 'dp')
Inputs may be any that keep to these rules, and one draw needn't show every extreme that they name: `expert_ids`: each row names 4 different experts. Among the rows of one device no expert is named more than 10 times, and in every draw some expert is named exactly 10 times by the rows of some device.
All inputs are finite; a program needn't handle non-finite values.
Results may differ from a plain program's by a relative error of at most 0.011.
Values may be sent and summed in bfloat16 or wider, within the bound.
A program may use at most 128 MiB of HBM per device.

v0:
```python
import jax
import jax.numpy as jnp
from jax import lax
from jax.sharding import PartitionSpec as P


def from_behind(value, axis, by):
    devices = lax.axis_size(axis)
    return lax.ppermute(value, axis, [(i, (i + by) % devices) for i in range(devices)])


def pair_lookup(experts, pair_flags, half_axis):
    match = experts[:, None] % half_axis == jnp.arange(half_axis, dtype=jnp.int32)[None, :]
    return jnp.sum(jnp.where(match, pair_flags[None, :], 0), axis=1)


def shards(tokens, cotangent, gate_weight, up_weight, down_weight, expert_ids, gates, swap_flags):
    expert_count = lax.axis_size("expert")
    half_axis = expert_count // 2
    my_slot = lax.axis_index("expert")
    row_count, model_width = tokens.shape
    routed = expert_ids.shape[1]
    capacity = row_count * routed * 5 // (4 * expert_count)
    groups = lax.axis_size("dp")
    quarter = model_width // groups
    own_flag = pair_lookup(jnp.reshape(my_slot, (1,)), swap_flags, half_axis)[0]
    flat_ids = expert_ids.reshape(-1)
    weights = (gate_weight, up_weight, down_weight)
    arrived = from_behind((gate_weight, up_weight, down_weight), "expert", half_axis)
    weights = tuple(
        (jnp.where(own_flag == 1, fresh, stay) for fresh, stay in zip(arrived, weights))
    )
    flipped = pair_lookup(flat_ids, swap_flags, half_axis)
    target = jnp.where(flipped == 1, (flat_ids + half_axis) % expert_count, flat_ids)
    copies = row_count * routed
    onehot = (target[:, None] == jnp.arange(expert_count, dtype=jnp.int32)[None, :]).astype(
        jnp.int32
    )
    earlier = jnp.cumsum(onehot, axis=0) - onehot
    position = jnp.sum(earlier * onehot, axis=1)
    buffer_index = target * capacity + position
    source = jnp.zeros((expert_count * capacity,), jnp.int32)
    source = source.at[buffer_index].set(jnp.arange(copies, dtype=jnp.int32) + 1)
    filled = source > 0
    copy_index = jnp.maximum(source - 1, 0)
    token_index = copy_index // routed
    x_buffer = jnp.where(filled[:, None], tokens[token_index], 0)
    dy_buffer = jnp.where(filled[:, None], cotangent[token_index], 0)
    gate_buffer = jnp.where(filled, gates.reshape(-1)[copy_index], 0)
    x_rows, dy_rows, gate_rows = (
        lax.all_to_all(x_buffer, "expert", split_axis=0, concat_axis=0, tiled=True),
        lax.all_to_all(dy_buffer, "expert", split_axis=0, concat_axis=0, tiled=True),
        lax.all_to_all(gate_buffer, "expert", split_axis=0, concat_axis=0, tiled=True),
    )
    w_gate = weights[0][0]
    w_up = weights[1][0]
    w_down = weights[2][0]
    contract_last = (((1,), (1,)), ((), ()))
    pre_gate = lax.dot_general(x_rows, w_gate, contract_last, preferred_element_type=jnp.float32)
    pre_up = lax.dot_general(x_rows, w_up, contract_last, preferred_element_type=jnp.float32)
    sigma = jax.nn.sigmoid(pre_gate)
    active = pre_gate * sigma
    hidden = (active * pre_up).astype(jnp.bfloat16)
    back = lax.dot_general(dy_rows, w_down, contract_last, preferred_element_type=jnp.float32)
    score_part = jnp.sum(hidden.astype(jnp.float32) * back, axis=1)
    grad_hidden = gate_rows.astype(jnp.float32)[:, None] * back
    slope = sigma * (1.0 + pre_gate * (1.0 - sigma))
    grad_gate = (grad_hidden * pre_up * slope).astype(jnp.bfloat16)
    grad_up = (grad_hidden * active).astype(jnp.bfloat16)
    input_part = jnp.dot(grad_gate, w_gate, preferred_element_type=jnp.float32)
    input_part = input_part + jnp.dot(grad_up, w_up, preferred_element_type=jnp.float32)
    scaled = gate_rows[:, None] * dy_rows
    contract_rows = (((0,), (0,)), ((), ()))
    grad_wgate = lax.dot_general(
        grad_gate, x_rows, contract_rows, preferred_element_type=jnp.float32
    )
    grad_wup = lax.dot_general(grad_up, x_rows, contract_rows, preferred_element_type=jnp.float32)
    grad_wdown = lax.dot_general(hidden, scaled, contract_rows, preferred_element_type=jnp.float32)
    scores = lax.psum(score_part, "dp")
    input_share = lax.psum_scatter(input_part, "dp", scatter_dimension=1, tiled=True).astype(
        jnp.bfloat16
    )
    back_rows, back_scores = (
        lax.all_to_all(input_share, "expert", split_axis=0, concat_axis=0, tiled=True),
        lax.all_to_all(
            scores.astype(jnp.bfloat16), "expert", split_axis=0, concat_axis=0, tiled=True
        ),
    )
    per_copy = back_rows[buffer_index].reshape(row_count, routed, quarter)
    input_grad = jnp.sum(per_copy.astype(jnp.float32), axis=1).astype(jnp.bfloat16)
    gate_grad = back_scores[buffer_index].reshape(row_count, routed)
    gradients = (
        grad_wgate.astype(jnp.bfloat16)[None],
        grad_wup.astype(jnp.bfloat16)[None],
        grad_wdown.astype(jnp.bfloat16)[None],
    )
    return (input_grad, gate_grad, gradients[0], gradients[1], gradients[2])


def solution(mesh):
    placed = (
        P("expert", None),
        P("expert", None),
        P("expert", "dp", None),
        P("expert", "dp", None),
        P("expert", "dp", None),
        P("expert", None),
        P("expert", None),
        P(),
    )
    return jax.shard_map(
        shards,
        mesh=mesh,
        in_specs=placed,
        out_specs=(
            P("expert", "dp"),
            P("expert", None),
            P("expert", "dp", None),
            P("expert", "dp", None),
            P("expert", "dp", None),
        ),
        check_vma=False,
    )
```

profile of v0, /device:TPU:35, one launch (start us, length us, event | category | flops | bytes accessed | tf_op | source)
XLA Modules:
  0.0 946.5 jit_solution(8024984857421448188)
XLA Ops:
  19.4 14.1 %all-to-all-start = ((bf16[64,10,1]{1,2,0:T(2,128)(2,1)}), bf16[64,10,1]{1,2,0:T(2,128)(2,1)S(1)}, u32[]{:S(2)}, u32[]{:S(2)}) async-start(bf16[64,10,1]{1,2,0:T(2,128)(2,1)} %all_to_all.49), calls=%async_computation | async-start | bytes 65536 | tf_op jit(solution)/shard_map/all_to_all | solution.py:53
  33.6 5.4 gather_fusion.1
  38.9 8.3 gather.21
  47.2 5.4 gather_fusion.2
  52.6 8.2 gather.23
  60.8 11.4 %broadcast_select_fusion = (bf16[64,10,4096]{2,1,0:T(8,128)(2,1)}, bf16[64,10,4096]{2,1,0:T(8,128)(2,1)}) fusion(bf16[64,10,4096]{2,1,0:T(8,128)(2,1)} %gather.23, pred[64,10]{1,0:T(8,128)(4,1)S(1)} %broadcast_in_dim.71, bf16[64,10,4096]{2,1,0:T(8,128)(2,1)} %gather.21), kind=kLoop, calls=%fused_computation.6 | loop fusion | flops 5242880 | bytes 20972160 | tf_op jit(solution)/shard_map/jit(_where)/select_n | solution.py:47
  72.2 200.0 %all_to_all.56 = bf16[64,10,4096]{2,1,0:T(8,128)(2,1)} all-to-all(bf16[64,10,4096]{2,1,0:T(8,128)(2,1)} %get-tuple-element.28), channel_id=1, replica_groups=mesh['expert'=64,'dp'=4] {'expert'}, dimensions={0} | all-to-all | bytes 10485760 | tf_op jit(solution)/shard_map/all_to_all | solution.py:51
  272.3 7.7 all-to-all-start.1
  280.1 5.3 collective-permute-start.2
  285.5 5.2 collective-permute-start
  292.3 8.6 all_to_all.42
  300.9 139.8 %all-to-all-done.1 = bf16[64,10,4096]{2,1,0:T(8,128)(2,1)} async-done(((bf16[64,10,4096]{2,1,0:T(8,128)(2,1)}), bf16[64,10,4096]{2,1,0:T(8,128)(2,1)}, u32[]{:S(2)}, u32[]{:S(2)}) %all-to-all-start.1) | async-done | bytes 5242912 | tf_op jit(solution)/shard_map/all_to_all | solution.py:52
  440.7 8.7 all_to_all.40
  449.4 31.2 %collective-permute-done.2 = bf16[1,192,4096]{2,1,0:T(8,128)(2,1)} collective-permute-done((bf16[1,192,4096]{2,1,0:T(8,128)(2,1)S(1)}, bf16[1,192,4096]{2,1,0:T(8,128)(2,1)}, u32[]{:S(2)}, u32[]{:S(2)}) %collective-permute-start.2) | collective-permute-done | bytes 1572896 | tf_op jit(solution)/shard_map/ppermute | solution.py:9
  480.6 4.5 fusion.12
  485.1 42.2 %collective-permute-done.1 = bf16[1,192,4096]{2,1,0:T(8,128)(2,1)} collective-permute-done((bf16[1,192,4096]{2,1,0:T(8,128)(2,1)}, bf16[1,192,4096]{2,1,0:T(8,128)(2,1)}, u32[]{:S(2)}, u32[]{:S(2)}) %collective-permute-start.1) | collective-permute-done | bytes 1572896 | tf_op jit(solution)/shard_map/ppermute | solution.py:9
  529.3 44.7 %collective-permute-done = bf16[1,192,4096]{2,1,0:T(8,128)(2,1)} collective-permute-done((bf16[1,192,4096]{2,1,0:T(8,128)(2,1)}, bf16[1,192,4096]{2,1,0:T(8,128)(2,1)}, u32[]{:S(2)}, u32[]{:S(2)}) %collective-permute-start) | collective-permute-done | bytes 1572896 | tf_op jit(solution)/shard_map/ppermute | solution.py:9
  577.6 5.6 convolution_add_fusion
  583.3 106.4 %psum.7 = bf16[640]{0:T(1024)(128)(2,1)S(1)} all-reduce(f32[640]{0:T(1024)S(1)} %get-tuple-element.20), channel_id=1, replica_groups=mesh['expert'=64,'dp'=4] {'dp'}, use_global_device_ids=true, to_apply=%region_9.10 | all-reduce | flops 640 | bytes 3840 | tf_op jit(solution)/shard_map/psum | solution.py:79
  690.5 21.4 %all-to-all-start.4 = ((bf16[64,10,1]{1,2,0:T(2,128)(2,1)}), bf16[64,10,1]{1,2,0:T(2,128)(2,1)S(1)}, u32[]{:S(2)}, u32[]{:S(2)}) async-start(bf16[64,10,1]{1,2,0:T(2,128)(2,1)} %all_to_all.50), calls=%async_computation.5 | async-start | bytes 65536 | tf_op jit(solution)/shard_map/all_to_all | solution.py:85
  711.9 164.2 %reduce-scatter.2.cloned.1.call-done = f32[640,1024]{1,0:T(8,128)} async-done(((f32[640,4096]{1,0:T(8,128)}), f32[640,1024]{1,0:T(8,128)}) %reduce-scatter.2.cloned.1.call-update) | async-done | bytes 2621456 | tf_op jit(solution)/shard_map/reduce_scatter | solution.py:80
  879.6 11.8 %all-to-all-start.3 = ((bf16[64,10,1024]{2,1,0:T(8,128)(2,1)}), bf16[64,10,1024]{2,1,0:T(8,128)(2,1)}, u32[]{:S(2)}, u32[]{:S(2)}) async-start(bf16[64,10,1024]{2,1,0:T(8,128)(2,1)} %all_to_all.43), calls=%async_computation.4 | async-start | bytes 4194304 | tf_op jit(solution)/shard_map/all_to_all | solution.py:84
  891.4 5.2 fusion.6
  906.4 26.1 %all-to-all-done.3 = bf16[64,10,1024]{2,1,0:T(8,128)(2,1)} async-done(((bf16[64,10,1024]{2,1,0:T(8,128)(2,1)}), bf16[64,10,1024]{2,1,0:T(8,128)(2,1)}, u32[]{:S(2)}, u32[]{:S(2)}) %all-to-all-start.3) | async-done | bytes 1310752 | tf_op jit(solution)/shard_map/all_to_all | solution.py:84
  (83 shorter events, 40.1 us)
Async XLA Ops:
  7.2 26.4 %copy-start = (bf16[128,4096]{1,0:T(8,128)(2,1)S(1)}, bf16[128,4096]{1,0:T(8,128)(2,1)}, u32[]{:S(2)}) copy-start(bf16[128,4096]{1,0:T(8,128)(2,1)} %param.9) | copy-start | bytes 3145732
  19.4 52.9 %all-to-all-start = ((bf16[64,10,1]{1,2,0:T(2,128)(2,1)}), bf16[64,10,1]{1,2,0:T(2,128)(2,1)S(1)}, u32[]{:S(2)}, u32[]{:S(2)}) async-start(bf16[64,10,1]{1,2,0:T(2,128)(2,1)} %all_to_all.49), calls=%async_computation | async-start | bytes 65536 | tf_op jit(solution)/shard_map/all_to_all | solution.py:53
  38.9 8.3 copy-start.2
  272.2 7.8 copy-start.4
  272.2 18.5 %copy-start.6 = (s32[32]{0:T(128)S(1)}, s32[32]{0:T(128)}, u32[]{:S(2)}) copy-start(s32[32]{0:T(128)} %param.15) | copy-start | bytes 388
  272.3 168.5 %all-to-all-start.1 = ((bf16[64,10,4096]{2,1,0:T(8,128)(2,1)}), bf16[64,10,4096]{2,1,0:T(8,128)(2,1)}, u32[]{:S(2)}, u32[]{:S(2)}) async-start(bf16[64,10,4096]{2,1,0:T(8,128)(2,1)} %get-tuple-element.29), calls=%async_computation.1 | async-start | bytes 16777216 | tf_op jit(solution)/shard_map/all_to_all | solution.py:52
  280.0 596.1 %reduce-scatter.2.cloned.1.call-start = ((), (), s32[]{:S(2)}) async-start(), calls=%async_computation.6 | async-start | bytes 13107200 | tf_op jit(solution)/shard_map/reduce_scatter | solution.py:80
  280.1 200.5 %collective-permute-start.2 = (bf16[1,192,4096]{2,1,0:T(8,128)(2,1)S(1)}, bf16[1,192,4096]{2,1,0:T(8,128)(2,1)}, u32[]{:S(2)}, u32[]{:S(2)}) collective-permute-start(bf16[1,192,4096]{2,1,0:T(8,128)(2,1)S(1)} %copy-done.4), channel_id=1, source_target_pairs={{0,128},{4,132},{8,136},{12,140},{16,144},{20,148},{24,152},{28,15... | collective-permute-start | bytes 4718600 | tf_op jit(solution)/shard_map/ppermute | solution.py:9
  285.4 242.0 %collective-permute-start.1 = (bf16[1,192,4096]{2,1,0:T(8,128)(2,1)}, bf16[1,192,4096]{2,1,0:T(8,128)(2,1)}, u32[]{:S(2)}, u32[]{:S(2)}) collective-permute-start(bf16[1,192,4096]{2,1,0:T(8,128)(2,1)} %param.11), channel_id=1, source_target_pairs={{0,128},{4,132},{8,136},{12,140},{16,144},{20,148},{24,152},{28,15... | collective-permute-start | bytes 4718600 | tf_op jit(solution)/shard_map/ppermute | solution.py:9
  285.5 288.4 %collective-permute-start = (bf16[1,192,4096]{2,1,0:T(8,128)(2,1)}, bf16[1,192,4096]{2,1,0:T(8,128)(2,1)}, u32[]{:S(2)}, u32[]{:S(2)}) collective-permute-start(bf16[1,192,4096]{2,1,0:T(8,128)(2,1)} %param.12), channel_id=1, source_target_pairs={{0,128},{4,132},{8,136},{12,140},{16,144},{20,148},{24,152},{28,15... | collective-permute-start | bytes 4718600 | tf_op jit(solution)/shard_map/ppermute | solution.py:9
  449.4 78.0 %copy-start.3 = (bf16[640,4096]{1,0:T(8,128)(2,1)S(1)}, bf16[640,4096]{1,0:T(8,128)(2,1)}, u32[]{:S(2)}) copy-start(bf16[640,4096]{1,0:T(8,128)(2,1)} %all_to_all.42) | copy-start | bytes 15728644
  449.4 78.0 %copy-start.5 = (bf16[1,192,4096]{2,1,0:T(8,128)(2,1)S(1)}, bf16[1,192,4096]{2,1,0:T(8,128)(2,1)}, u32[]{:S(2)}) copy-start(bf16[1,192,4096]{2,1,0:T(8,128)(2,1)} %param.11) | copy-start | bytes 4718596
  480.6 93.3 %slice-start.2 = ((s8[5242880]{0:T(1024)(128)(4,1)}), s8[4194304]{0:T(1024)(128)(4,1)S(1)}, s32[]{:S(2)}) async-start(s8[5242880]{0:T(1024)(128)(4,1)} %bitcast.58), calls=%async_computation.9 | async-start | bytes 8388608
  485.1 88.8 %slice-start.3 = ((s8[5242880]{0:T(1024)(128)(4,1)}), s8[1048576]{0:T(1024)(128)(4,1)S(1)}, s32[]{:S(2)}) async-start(s8[5242880]{0:T(1024)(128)(4,1)} %bitcast.58), calls=%async_computation.10 | async-start | bytes 2097152
  485.1 88.8 %copy-start.7 = (bf16[1,192,4096]{2,1,0:T(8,128)(2,1)S(1)}, bf16[1,192,4096]{2,1,0:T(8,128)(2,1)}, u32[]{:S(2)}) copy-start(bf16[1,192,4096]{2,1,0:T(8,128)(2,1)} %param.12) | copy-start | bytes 4718596
  690.5 189.1 %all-to-all-start.4 = ((bf16[64,10,1]{1,2,0:T(2,128)(2,1)}), bf16[64,10,1]{1,2,0:T(2,128)(2,1)S(1)}, u32[]{:S(2)}, u32[]{:S(2)}) async-start(bf16[64,10,1]{1,2,0:T(2,128)(2,1)} %all_to_all.50), calls=%async_computation.5 | async-start | bytes 65536 | tf_op jit(solution)/shard_map/all_to_all | solution.py:85
  879.6 17.0 %slice-start = ((s8[5242880]{0:T(1024)(128)(4,1)}), s8[1048576]{0:T(1024)(128)(4,1)S(1)}, s32[]{:S(2)}) async-start(s8[5242880]{0:T(1024)(128)(4,1)} %bitcast.56), calls=%async_computation.7 | async-start | bytes 2097152
  879.6 52.8 %all-to-all-start.3 = ((bf16[64,10,1024]{2,1,0:T(8,128)(2,1)}), bf16[64,10,1024]{2,1,0:T(8,128)(2,1)}, u32[]{:S(2)}, u32[]{:S(2)}) async-start(bf16[64,10,1024]{2,1,0:T(8,128)(2,1)} %all_to_all.43), calls=%async_computation.4 | async-start | bytes 4194304 | tf_op jit(solution)/shard_map/all_to_all | solution.py:84
  891.4 5.2 slice-start.1
  891.4 7.7 slice-start.4
  896.6 2.6 slice-start.5
  935.0 4.6 copy-start.1
Sparse Core Ops, SparseCore 0:
  583.4 292.6 reduce-scatter.1
where the time goes:
time: 960 us; the launch traced here: 946 us
  waiting for transfers between devices  448 us (47%)
  blocking collectives  306 us (32%)
  local copies, waits for them, and re-layouts  66.6 us (7%)
  starting transfers between devices  65.7 us (7%)
  matrix products  26 us (3%)
  other arithmetic  18.5 us (2%)
  between operations  15 us (2%)
    all_to_all x1, blocking collectives, shards(): lax.all_to_all(x_buffer, 'expert', split_axis=0, concat_axis=0, tiled=True)  200 us
    reduce_scatter x1, waiting for transfers between devices, shards(): lax.psum_scatter(input_part, 'dp', scatter_dimension=1, tiled=True)  164 us
    all_to_all x1, waiting for transfers between devices, shards(): lax.all_to_all(dy_buffer, 'expert', split_axis=0, concat_axis=0, tiled=True)  140 us
    ppermute x3, waiting for transfers between devices, from_behind(): lax.ppermute(value, axis, [(i, (i + by) % devices) for i in range(devices)])  118 us
    psum x1, blocking collectives, shards(): scores = lax.psum(score_part, 'dp')  106 us
    all_to_all x1, waiting for transfers between devices, shards(): lax.all_to_all(input_share, 'expert', split_axis=0, concat_axis=0, tiled=...  26.1 us
    all_to_all x1, starting transfers between devices, shards(): lax.all_to_all(scores.astype(jnp.bfloat16), 'expert', split_axis=0, conca...  21.4 us
  transfers between devices with their start and end apart: 8, of which 6 were waited for; matrix products, arithmetic and copies ran while one was open for 7% of the time, Pallas kernels for 0%

commit v1 on v0

--- a/solution.py
+++ b/solution.py
@@ -76,19 +76,17 @@
     )
     grad_wup = lax.dot_general(grad_up, x_rows, contract_rows, preferred_element_type=jnp.float32)
     grad_wdown = lax.dot_general(hidden, scaled, contract_rows, preferred_element_type=jnp.float32)
-    scores = lax.psum(score_part, "dp")
-    input_share = lax.psum_scatter(input_part, "dp", scatter_dimension=1, tiled=True).astype(
-        jnp.bfloat16
-    )
-    back_rows, back_scores = (
-        lax.all_to_all(input_share, "expert", split_axis=0, concat_axis=0, tiled=True),
-        lax.all_to_all(
-            scores.astype(jnp.bfloat16), "expert", split_axis=0, concat_axis=0, tiled=True
-        ),
-    )
-    per_copy = back_rows[buffer_index].reshape(row_count, routed, quarter)
-    input_grad = jnp.sum(per_copy.astype(jnp.float32), axis=1).astype(jnp.bfloat16)
-    gate_grad = back_scores[buffer_index].reshape(row_count, routed)
+    score_cols = jnp.zeros((capacity * expert_count, groups, 128), jnp.float32)
+    score_cols = score_cols.at[:, :, 0].set(score_part[:, None])
+    packed = jnp.concatenate(
+        [input_part.reshape(capacity * expert_count, groups, quarter), score_cols], axis=2
+    ).astype(jnp.bfloat16)
+    packed = packed.reshape(capacity * expert_count, groups * (quarter + 128))
+    reduced = lax.psum_scatter(packed, "dp", scatter_dimension=1, tiled=True)
+    back_rows = lax.all_to_all(reduced, "expert", split_axis=0, concat_axis=0, tiled=True)
+    per_copy = back_rows[buffer_index].reshape(row_count, routed, quarter + 128)
+    input_grad = jnp.sum(per_copy[:, :, :quarter].astype(jnp.float32), axis=1).astype(jnp.bfloat16)
+    gate_grad = per_copy[:, :, quarter]
     gradients = (
         grad_wgate.astype(jnp.bfloat16)[None],
         grad_wup.astype(jnp.bfloat16)[None],

time: 960 us -> 925 us (0.964)
  blocking collectives: 306 us -> 200 us
  waiting for transfers between devices: 448 us -> 507 us
  local copies, waits for them, and re-layouts: 66.6 us -> 91.2 us
  starting transfers between devices: 65.7 us -> 44.1 us
    unnamed x1 -> x2, waiting for transfers between devices: 0.02 us -> 214 us
    reduce_scatter x1 -> x0, waiting for transfers between devices: 164 us -> none  [shards(): lax.psum_scatter(input_part, 'dp', scatter_dimension=1, tiled=True)]
    psum x1 -> x0, blocking collectives: 106 us -> none  [shards(): scores = lax.psum(score_part, 'dp')]
    all_to_all x2 -> x1, starting transfers between devices: 33.2 us -> 11.6 us  [shards(): lax.all_to_all(reduced, 'expert', split_axis=0, concat_axis=0, tiled=True)]
    unnamed x31 -> x35, local copies, waits for them, and re-layouts: 2.41 us -> 16.8 us
    reshape x2, local copies, waits for them, and re-layouts: 0.55 us -> 12 us  [the longest x1 9.5 us: shards(): input_part.reshape(capacity * expert_count, groups, quarter)]
    all_to_all x2 -> x1, waiting for transfers between devices: 26.1 us -> 36.7 us  [shards(): lax.all_to_all(reduced, 'expert', split_axis=0, concat_axis=0, tiled=True)]
  transfers between devices with their start and end apart: 8 -> 7, of which waited for: 6 -> 6; matrix products, arithmetic and copies ran while one was open for 7% -> 6% of each run, Pallas kernels for 0% -> 0%
where the time goes in v1:
time: 925 us; the launch traced here: 912 us
  waiting for transfers between devices  507 us (55%)
  blocking collectives  200 us (22%)
  local copies, waits for them, and re-layouts  91.2 us (10%)
  starting transfers between devices  44.1 us (5%)
  matrix products  30.6 us (3%)
  other arithmetic  24.3 us (3%)
  between operations  15 us (2%)
    unnamed x2, waiting for transfers between devices  214 us
    all_to_all x1, blocking collectives, shards(): lax.all_to_all(x_buffer, 'expert', split_axis=0, concat_axis=0, tiled=True)  200 us
    all_to_all x1, waiting for transfers between devices, shards(): lax.all_to_all(dy_buffer, 'expert', split_axis=0, concat_axis=0, tiled=True)  140 us
    ppermute x3, waiting for transfers between devices, from_behind(): lax.ppermute(value, axis, [(i, (i + by) % devices) for i in range(devices)])  116 us
    all_to_all x1, waiting for transfers between devices, shards(): lax.all_to_all(reduced, 'expert', split_axis=0, concat_axis=0, tiled=True)  36.7 us
  transfers between devices with their start and end apart: 7, of which 6 were waited for; matrix products, arithmetic and copies ran while one was open for 6% of the time, Pallas kernels for 0%

profile of v1, /device:TPU:35, one launch (start us, length us, event | category | flops | bytes accessed | tf_op | source)
XLA Modules:
  0.0 911.8 jit_solution(7181187808591647721)
XLA Ops:
  19.4 14.1 %all-to-all-start = ((bf16[64,10,1]{1,2,0:T(2,128)(2,1)}), bf16[64,10,1]{1,2,0:T(2,128)(2,1)S(1)}, u32[]{:S(2)}, u32[]{:S(2)}) async-start(bf16[64,10,1]{1,2,0:T(2,128)(2,1)} %all_to_all.38), calls=%async_computation | async-start | bytes 65536 | tf_op jit(solution)/shard_map/all_to_all | solution.py:53
  33.6 5.4 gather_fusion.1
  38.9 8.3 gather.18
  47.2 5.4 gather_fusion.2
  52.6 8.2 gather.20
  60.8 11.4 %broadcast_select_fusion = (bf16[64,10,4096]{2,1,0:T(8,128)(2,1)}, bf16[64,10,4096]{2,1,0:T(8,128)(2,1)}) fusion(bf16[64,10,4096]{2,1,0:T(8,128)(2,1)} %gather.20, pred[64,10]{1,0:T(8,128)(4,1)S(1)} %broadcast_in_dim.75, bf16[64,10,4096]{2,1,0:T(8,128)(2,1)} %gather.18), kind=kLoop, calls=%fused_computation.8 | loop fusion | flops 5242880 | bytes 20972160 | tf_op jit(solution)/shard_map/jit(_where)/select_n | solution.py:47
  72.2 200.0 %all_to_all.43 = bf16[64,10,4096]{2,1,0:T(8,128)(2,1)} all-to-all(bf16[64,10,4096]{2,1,0:T(8,128)(2,1)} %get-tuple-element.25), channel_id=1, replica_groups=mesh['expert'=64,'dp'=4] {'expert'}, dimensions={0} | all-to-all | bytes 10485760 | tf_op jit(solution)/shard_map/all_to_all | solution.py:51
  272.2 7.7 all-to-all-start.1
  280.0 5.3 collective-permute-start.2
  285.5 5.2 collective-permute-start
  292.2 8.6 all_to_all.34
  300.9 139.8 %all-to-all-done.1 = bf16[64,10,4096]{2,1,0:T(8,128)(2,1)} async-done(((bf16[64,10,4096]{2,1,0:T(8,128)(2,1)}), bf16[64,10,4096]{2,1,0:T(8,128)(2,1)}, u32[]{:S(2)}, u32[]{:S(2)}) %all-to-all-start.1) | async-done | bytes 5242912 | tf_op jit(solution)/shard_map/all_to_all | solution.py:52
  440.7 8.6 all_to_all.32
  449.3 31.3 %collective-permute-done.2 = bf16[1,192,4096]{2,1,0:T(8,128)(2,1)} collective-permute-done((bf16[1,192,4096]{2,1,0:T(8,128)(2,1)}, bf16[1,192,4096]{2,1,0:T(8,128)(2,1)}, u32[]{:S(2)}, u32[]{:S(2)}) %collective-permute-start.2) | collective-permute-done | bytes 1572896 | tf_op jit(solution)/shard_map/ppermute | solution.py:9
  485.6 41.8 %collective-permute-done.1 = bf16[1,192,4096]{2,1,0:T(8,128)(2,1)} collective-permute-done((bf16[1,192,4096]{2,1,0:T(8,128)(2,1)S(1)}, bf16[1,192,4096]{2,1,0:T(8,128)(2,1)}, u32[]{:S(2)}, u32[]{:S(2)}) %collective-permute-start.1) | collective-permute-done | bytes 1572896 | tf_op jit(solution)/shard_map/ppermute | solution.py:9
  530.7 43.2 %collective-permute-done = bf16[1,192,4096]{2,1,0:T(8,128)(2,1)} collective-permute-done((bf16[1,192,4096]{2,1,0:T(8,128)(2,1)}, bf16[1,192,4096]{2,1,0:T(8,128)(2,1)}, u32[]{:S(2)}, u32[]{:S(2)}) %collective-permute-start) | collective-permute-done | bytes 1572896 | tf_op jit(solution)/shard_map/ppermute | solution.py:9
  580.6 5.3 add_convert_fusion
  585.9 9.5 %reshape.235 = bf16[640,4,1024]{2,1,0:T(4,128)(2,1)} reshape(bf16[640,4096]{1,0:T(8,128)(2,1)} %add_convert_fusion) | data formatting | bytes 10485760 | tf_op jit(solution)/shard_map/reshape | solution.py:82
  597.5 7.7 fusion.1
  605.3 11.8 %copy.36 = bf16[640,4,1152]{0,2,1:T(8,128)(2,1)} copy(bf16[640,4,1152]{2,1,0:T(4,128)(2,1)} %fusion.1) | data formatting | bytes 11796480
  617.0 213.8 %reduce-scatter.4.cloned.1.call-done = bf16[1152,640]{1,0:T(8,128)(2,1)} async-done(((bf16[4608,640]{1,0:T(8,128)(2,1)}), bf16[1152,640]{1,0:T(8,128)(2,1)}) %reduce-scatter.4.cloned.1.call-update) | async-done | bytes 1474576
  835.1 11.6 %all-to-all-start.3 = ((bf16[64,10,1152]{2,1,0:T(8,128)(2,1)}), bf16[64,10,1152]{2,1,0:T(8,128)(2,1)}, u32[]{:S(2)}, u32[]{:S(2)}) async-start(bf16[64,10,1152]{2,1,0:T(8,128)(2,1)} %all_to_all.35), calls=%async_computation.3 | async-start | bytes 4718592 | tf_op jit(solution)/shard_map/all_to_all | solution.py:86
  846.8 5.2 fusion.8
  857.3 36.7 %all-to-all-done.3 = bf16[64,10,1152]{2,1,0:T(8,128)(2,1)} async-done(((bf16[64,10,1152]{2,1,0:T(8,128)(2,1)}), bf16[64,10,1152]{2,1,0:T(8,128)(2,1)}, u32[]{:S(2)}, u32[]{:S(2)}) %all-to-all-start.3) | async-done | bytes 1474592 | tf_op jit(solution)/shard_map/all_to_all | solution.py:86
  (82 shorter events, 50.9 us)
Async XLA Ops:
  7.2 26.4 %copy-start = (bf16[128,4096]{1,0:T(8,128)(2,1)S(1)}, bf16[128,4096]{1,0:T(8,128)(2,1)}, u32[]{:S(2)}) copy-start(bf16[128,4096]{1,0:T(8,128)(2,1)} %param.11) | copy-start | bytes 3145732
  19.4 52.9 %all-to-all-start = ((bf16[64,10,1]{1,2,0:T(2,128)(2,1)}), bf16[64,10,1]{1,2,0:T(2,128)(2,1)S(1)}, u32[]{:S(2)}, u32[]{:S(2)}) async-start(bf16[64,10,1]{1,2,0:T(2,128)(2,1)} %all_to_all.38), calls=%async_computation | async-start | bytes 65536 | tf_op jit(solution)/shard_map/all_to_all | solution.py:53
  38.9 8.3 copy-start.2
  272.2 13.1 %copy-start.4 = (bf16[1,192,4096]{2,1,0:T(8,128)(2,1)S(1)}, bf16[1,192,4096]{2,1,0:T(8,128)(2,1)}, u32[]{:S(2)}) copy-start(bf16[1,192,4096]{2,1,0:T(8,128)(2,1)} %param.13) | copy-start | bytes 4718596
  272.2 18.5 %copy-start.7 = (s32[32]{0:T(128)S(1)}, s32[32]{0:T(128)}, u32[]{:S(2)}) copy-start(s32[32]{0:T(128)} %param.17) | copy-start | bytes 388
  272.2 168.5 %all-to-all-start.1 = ((bf16[64,10,4096]{2,1,0:T(8,128)(2,1)}), bf16[64,10,4096]{2,1,0:T(8,128)(2,1)}, u32[]{:S(2)}, u32[]{:S(2)}) async-start(bf16[64,10,4096]{2,1,0:T(8,128)(2,1)} %get-tuple-element.26), calls=%async_computation.1 | async-start | bytes 16777216 | tf_op jit(solution)/shard_map/all_to_all | solution.py:52
  280.0 550.8 %reduce-scatter.4.cloned.1.call-start = ((), (), s32[]{:S(2)}) async-start(), calls=%async_computation.5 | async-start | bytes 7372800
  280.0 200.5 %collective-permute-start.2 = (bf16[1,192,4096]{2,1,0:T(8,128)(2,1)}, bf16[1,192,4096]{2,1,0:T(8,128)(2,1)}, u32[]{:S(2)}, u32[]{:S(2)}) collective-permute-start(bf16[1,192,4096]{2,1,0:T(8,128)(2,1)} %param.12), channel_id=1, source_target_pairs={{0,128},{4,132},{8,136},{12,140},{16,144},{20,148},{24,152},{28,15... | collective-permute-start | bytes 4718600 | tf_op jit(solution)/shard_map/ppermute | solution.py:9
  285.3 242.0 %collective-permute-start.1 = (bf16[1,192,4096]{2,1,0:T(8,128)(2,1)S(1)}, bf16[1,192,4096]{2,1,0:T(8,128)(2,1)}, u32[]{:S(2)}, u32[]{:S(2)}) collective-permute-start(bf16[1,192,4096]{2,1,0:T(8,128)(2,1)S(1)} %copy-done.4), channel_id=1, source_target_pairs={{0,128},{4,132},{8,136},{12,140},{16,144},{20,148},{24,152},{28,15... | collective-permute-start | bytes 4718600 | tf_op jit(solution)/shard_map/ppermute | solution.py:9
  285.5 288.4 %collective-permute-start = (bf16[1,192,4096]{2,1,0:T(8,128)(2,1)}, bf16[1,192,4096]{2,1,0:T(8,128)(2,1)}, u32[]{:S(2)}, u32[]{:S(2)}) collective-permute-start(bf16[1,192,4096]{2,1,0:T(8,128)(2,1)} %param.14), channel_id=1, source_target_pairs={{0,128},{4,132},{8,136},{12,140},{16,144},{20,148},{24,152},{28,15... | collective-permute-start | bytes 4718600 | tf_op jit(solution)/shard_map/ppermute | solution.py:9
  449.3 78.0 %copy-start.3 = (bf16[640,4096]{1,0:T(8,128)(2,1)S(1)}, bf16[640,4096]{1,0:T(8,128)(2,1)}, u32[]{:S(2)}) copy-start(bf16[640,4096]{1,0:T(8,128)(2,1)} %all_to_all.34) | copy-start | bytes 15728644
  480.6 93.3 %slice-start.2 = ((s8[5242880]{0:T(1024)(128)(4,1)}), s8[4194304]{0:T(1024)(128)(4,1)S(1)}, s32[]{:S(2)}) async-start(s8[5242880]{0:T(1024)(128)(4,1)} %bitcast.64), calls=%async_computation.8 | async-start | bytes 8388608
  485.6 88.4 %slice-start.3 = ((s8[5242880]{0:T(1024)(128)(4,1)}), s8[1048576]{0:T(1024)(128)(4,1)S(1)}, s32[]{:S(2)}) async-start(s8[5242880]{0:T(1024)(128)(4,1)} %bitcast.64), calls=%async_computation.9 | async-start | bytes 2097152
  485.6 88.3 %copy-start.8 = (bf16[1,192,4096]{2,1,0:T(8,128)(2,1)S(1)}, bf16[1,192,4096]{2,1,0:T(8,128)(2,1)}, u32[]{:S(2)}) copy-start(bf16[1,192,4096]{2,1,0:T(8,128)(2,1)} %param.14) | copy-start | bytes 4718596
  530.7 46.8 %copy-start.5 = (bf16[1,192,4096]{2,1,0:T(8,128)(2,1)S(1)}, bf16[1,192,4096]{2,1,0:T(8,128)(2,1)}, u32[]{:S(2)}) copy-start(bf16[1,192,4096]{2,1,0:T(8,128)(2,1)} %param.13) | copy-start | bytes 4718596
  577.4 3.1 copy-start.6
  835.1 58.8 %all-to-all-start.3 = ((bf16[64,10,1152]{2,1,0:T(8,128)(2,1)}), bf16[64,10,1152]{2,1,0:T(8,128)(2,1)}, u32[]{:S(2)}, u32[]{:S(2)}) async-start(bf16[64,10,1152]{2,1,0:T(8,128)(2,1)} %all_to_all.35), calls=%async_computation.3 | async-start | bytes 4718592 | tf_op jit(solution)/shard_map/all_to_all | solution.py:86
  846.8 5.2 slice-start
  846.8 5.2 slice-start.1
  846.8 7.8 slice-start.4
  852.0 2.6 slice-start.5
  893.9 11.0 %copy-start.1 = (bf16[128,4096]{1,0:T(8,128)(2,1)S(1)}, bf16[128,4096]{1,0:T(8,128)(2,1)}, u32[]{:S(2)}) copy-start(bf16[128,4096]{1,0:T(8,128)(2,1)} %param.11) | copy-start | bytes 3145732
Sparse Core Ops, SparseCore 0:
  617.2 213.6 reduce-scatter.3

commit v2 on v1

--- a/solution.py
+++ b/solution.py
@@ -2,6 +2,65 @@
 import jax.numpy as jnp
 from jax import lax
 from jax.sharding import PartitionSpec as P
+from jax.experimental import pallas as pl
+from jax.experimental.pallas import tpu as pltpu
+
+MESH_IDS = pl.DeviceIdType.MESH
+
+
+def dp_scatter_kernel(groups, src_ref, out_ref, landing, send_sem, recv_sem):
+    me = lax.axis_index("dp")
+    home = lax.axis_index("expert")
+    width = out_ref.shape[1]
+    barrier = pltpu.get_barrier_semaphore()
+    for step in range(1, groups):
+        peer = lax.rem(me + step, groups)
+        pl.semaphore_signal(barrier, 1, device_id=(home, peer), device_id_type=MESH_IDS)
+    pl.semaphore_wait(barrier, groups - 1)
+    copies = []
+    for step in range(1, groups):
+        peer = lax.rem(me + step, groups)
+        copy = pltpu.make_async_remote_copy(
+            src_ref=src_ref.at[:, pl.ds(pl.multiple_of(peer * width, 128), width)],
+            dst_ref=landing.at[step],
+            send_sem=send_sem.at[step],
+            recv_sem=recv_sem.at[step],
+            device_id=(home, peer),
+            device_id_type=MESH_IDS,
+        )
+        copy.start()
+        copies.append(copy)
+    for copy in copies:
+        copy.wait()
+    own = pl.multiple_of(me * width, 128)
+    block = 64
+
+    def body(i, carry):
+        rows = pl.ds(pl.multiple_of(i * block, block), block)
+        total = src_ref[rows, pl.ds(own, width)].astype(jnp.float32)
+        for step in range(1, groups):
+            total = total + landing[step, rows, :].astype(jnp.float32)
+        out_ref[rows, :] = total.astype(out_ref.dtype)
+        return carry
+
+    lax.fori_loop(0, out_ref.shape[0] // block, body, 0)
+
+
+def dp_scatter(packed, groups):
+    rows, full = packed.shape
+    width = full // groups
+    return pl.pallas_call(
+        lambda *refs: dp_scatter_kernel(groups, *refs),
+        out_shape=jax.ShapeDtypeStruct((rows, width), packed.dtype),
+        in_specs=[pl.BlockSpec(memory_space=pltpu.VMEM)],
+        out_specs=pl.BlockSpec(memory_space=pltpu.VMEM),
+        scratch_shapes=[
+            pltpu.VMEM((groups, rows, width), packed.dtype),
+            pltpu.SemaphoreType.DMA((groups,)),
+            pltpu.SemaphoreType.DMA((groups,)),
+        ],
+        compiler_params=pltpu.CompilerParams(collective_id=0, has_side_effects=True),
+    )(packed)
 
 
 def from_behind(value, axis, by):
@@ -82,7 +141,7 @@
         [input_part.reshape(capacity * expert_count, groups, quarter), score_cols], axis=2
     ).astype(jnp.bfloat16)
     packed = packed.reshape(capacity * expert_count, groups * (quarter + 128))
-    reduced = lax.psum_scatter(packed, "dp", scatter_dimension=1, tiled=True)
+    reduced = dp_scatter(packed, groups)
     back_rows = lax.all_to_all(reduced, "expert", split_axis=0, concat_axis=0, tiled=True)
     per_copy = back_rows[buffer_index].reshape(row_count, routed, quarter + 128)
     input_grad = jnp.sum(per_copy[:, :, :quarter].astype(jnp.float32), axis=1).astype(jnp.bfloat16)

time: 925 us -> 948 us (1.025)
  Pallas kernels: 0 us -> 254 us
  waiting for transfers between devices: 507 us -> 293 us
  between operations: 15 us -> 1.59 us
    pallas_call x0 -> x1, Pallas kernels: none -> 254 us  [dp_scatter(): pl.pallas_call(lambda *refs: dp_scatter_kernel(groups, *refs), out_shape=...]
    unnamed x2 -> x0, waiting for transfers between devices: 214 us -> none
    unnamed x35 -> x32, local copies, waits for them, and re-layouts: 16.8 us -> 5.95 us
  transfers between devices with their start and end apart: 7 -> 6, of which waited for: 6 -> 5; matrix products, arithmetic and copies ran while one was open for 6% -> 6% of each run, Pallas kernels for 0% -> 0%
where the time goes in v2:
time: 948 us; the launch traced here: 937 us
  waiting for transfers between devices  293 us (31%)
  Pallas kernels  254 us (27%)
  blocking collectives  200 us (21%)
  local copies, waits for them, and re-layouts  82.4 us (9%)
  starting transfers between devices  52.6 us (6%)
  matrix products  30.6 us (3%)
  other arithmetic  22.1 us (2%)
    pallas_call x1, Pallas kernels, dp_scatter(): pl.pallas_call(lambda *refs: dp_scatter_kernel(groups, *refs), out_shape=...  254 us
    all_to_all x1, blocking collectives, shards(): lax.all_to_all(x_buffer, 'expert', split_axis=0, concat_axis=0, tiled=True)  200 us
    all_to_all x1, waiting for transfers between devices, shards(): lax.all_to_all(dy_buffer, 'expert', split_axis=0, concat_axis=0, tiled=True)  140 us
    ppermute x3, waiting for transfers between devices, from_behind(): lax.ppermute(value, axis, [(i, (i + by) % devices) for i in range(devices)])  116 us
    all_to_all x1, waiting for transfers between devices, shards(): lax.all_to_all(reduced, 'expert', split_axis=0, concat_axis=0, tiled=True)  37 us
    all_to_all x1, starting transfers between devices, shards(): lax.all_to_all(reduced, 'expert', split_axis=0, concat_axis=0, tiled=True)  20.1 us
  transfers between devices with their start and end apart: 6, of which 5 were waited for; matrix products, arithmetic and copies ran while one was open for 6% of the time, Pallas kernels for 0%

profile of v2, /device:TPU:35, one launch (start us, length us, event | category | flops | bytes accessed | tf_op | source)
XLA Modules:
  0.0 936.9 jit_solution(1383827164103054077)
XLA Ops:
  12.8 14.1 %all-to-all-start = ((bf16[64,10,1]{1,2,0:T(2,128)(2,1)}), bf16[64,10,1]{1,2,0:T(2,128)(2,1)S(1)}, u32[]{:S(2)}, u32[]{:S(2)}) async-start(bf16[64,10,1]{1,2,0:T(2,128)(2,1)} %all_to_all.38), calls=%async_computation | async-start | bytes 65536 | tf_op jit(solution)/shard_map/all_to_all | solution.py:112
  27.0 5.4 gather_fusion.1
  32.4 8.3 gather.18
  40.7 5.4 gather_fusion.2
  46.1 8.2 gather.20
  54.3 11.4 %broadcast_select_fusion = (bf16[64,10,4096]{2,1,0:T(8,128)(2,1)}, bf16[64,10,4096]{2,1,0:T(8,128)(2,1)}) fusion(bf16[64,10,4096]{2,1,0:T(8,128)(2,1)} %gather.20, pred[64,10]{1,0:T(8,128)(4,1)S(1)} %broadcast_in_dim.75, bf16[64,10,4096]{2,1,0:T(8,128)(2,1)} %gather.18), kind=kLoop, calls=%fused_computation.8 | loop fusion | flops 5242880 | bytes 20972160 | tf_op jit(solution)/shard_map/jit(_where)/select_n | solution.py:106
  65.7 200.0 %all_to_all.43 = bf16[64,10,4096]{2,1,0:T(8,128)(2,1)} all-to-all(bf16[64,10,4096]{2,1,0:T(8,128)(2,1)} %get-tuple-element.25), channel_id=1, replica_groups=mesh['expert'=64,'dp'=4] {'expert'}, dimensions={0} | all-to-all | bytes 10485760 | tf_op jit(solution)/shard_map/all_to_all | solution.py:110
  265.8 7.7 all-to-all-start.1
  273.5 5.3 collective-permute-start.2
  279.0 5.2 collective-permute-start
  285.7 8.7 all_to_all.34
  294.4 139.9 %all-to-all-done.1 = bf16[64,10,4096]{2,1,0:T(8,128)(2,1)} async-done(((bf16[64,10,4096]{2,1,0:T(8,128)(2,1)}), bf16[64,10,4096]{2,1,0:T(8,128)(2,1)}, u32[]{:S(2)}, u32[]{:S(2)}) %all-to-all-start.1) | async-done | bytes 5242912 | tf_op jit(solution)/shard_map/all_to_all | solution.py:111
  434.2 8.6 all_to_all.32
  442.9 31.2 %collective-permute-done.2 = bf16[1,192,4096]{2,1,0:T(8,128)(2,1)} collective-permute-done((bf16[1,192,4096]{2,1,0:T(8,128)(2,1)}, bf16[1,192,4096]{2,1,0:T(8,128)(2,1)}, u32[]{:S(2)}, u32[]{:S(2)}) %collective-permute-start.2) | collective-permute-done | bytes 1572896 | tf_op jit(solution)/shard_map/ppermute | solution.py:68
  474.1 5.0 fusion.14
  479.1 41.8 %collective-permute-done.1 = bf16[1,192,4096]{2,1,0:T(8,128)(2,1)} collective-permute-done((bf16[1,192,4096]{2,1,0:T(8,128)(2,1)S(1)}, bf16[1,192,4096]{2,1,0:T(8,128)(2,1)}, u32[]{:S(2)}, u32[]{:S(2)}) %collective-permute-start.1) | collective-permute-done | bytes 1572896 | tf_op jit(solution)/shard_map/ppermute | solution.py:68
  524.2 43.2 %collective-permute-done = bf16[1,192,4096]{2,1,0:T(8,128)(2,1)} collective-permute-done((bf16[1,192,4096]{2,1,0:T(8,128)(2,1)}, bf16[1,192,4096]{2,1,0:T(8,128)(2,1)}, u32[]{:S(2)}, u32[]{:S(2)}) %collective-permute-start) | collective-permute-done | bytes 1572896 | tf_op jit(solution)/shard_map/ppermute | solution.py:68
  574.1 5.3 add_convert_fusion
  579.4 9.5 %reshape.235 = bf16[640,4,1024]{2,1,0:T(4,128)(2,1)} reshape(bf16[640,4096]{1,0:T(8,128)(2,1)} %add_convert_fusion) | data formatting | bytes 10485760 | tf_op jit(solution)/shard_map/reshape | solution.py:141
  591.0 5.6 fusion.1
  600.1 254.5 %shard_map.119 = bf16[640,1152]{1,0:T(8,128)(2,1)} custom-call(bf16[640,4608]{1,0:T(8,128)(2,1)} %bitcast.61), custom_call_target="tpu_custom_call" | custom-call | tf_op jit(solution)/shard_map/pallas_call | solution.py:52
  858.2 20.1 %all-to-all-start.3 = ((bf16[64,10,1152]{2,1,0:T(8,128)(2,1)}), bf16[64,10,1152]{2,1,0:T(8,128)(2,1)}, u32[]{:S(2)}, u32[]{:S(2)}) async-start(bf16[64,10,1152]{2,1,0:T(8,128)(2,1)} %all_to_all.35), calls=%async_computation.3 | async-start | bytes 4718592 | tf_op jit(solution)/shard_map/all_to_all | solution.py:145
  878.4 5.2 fusion.8
  888.9 37.0 %all-to-all-done.3 = bf16[64,10,1152]{2,1,0:T(8,128)(2,1)} async-done(((bf16[64,10,1152]{2,1,0:T(8,128)(2,1)}), bf16[64,10,1152]{2,1,0:T(8,128)(2,1)}, u32[]{:S(2)}, u32[]{:S(2)}) %all-to-all-start.3) | async-done | bytes 1474592 | tf_op jit(solution)/shard_map/all_to_all | solution.py:145
  (77 shorter events, 48.8 us)
Async XLA Ops:
  0.6 26.4 %copy-start = (bf16[128,4096]{1,0:T(8,128)(2,1)S(1)}, bf16[128,4096]{1,0:T(8,128)(2,1)}, u32[]{:S(2)}) copy-start(bf16[128,4096]{1,0:T(8,128)(2,1)} %param.11) | copy-start | bytes 3145732
  12.8 52.9 %all-to-all-start = ((bf16[64,10,1]{1,2,0:T(2,128)(2,1)}), bf16[64,10,1]{1,2,0:T(2,128)(2,1)S(1)}, u32[]{:S(2)}, u32[]{:S(2)}) async-start(bf16[64,10,1]{1,2,0:T(2,128)(2,1)} %all_to_all.38), calls=%async_computation | async-start | bytes 65536 | tf_op jit(solution)/shard_map/all_to_all | solution.py:112
  32.4 8.3 copy-start.2
  265.8 13.0 %copy-start.4 = (bf16[1,192,4096]{2,1,0:T(8,128)(2,1)S(1)}, bf16[1,192,4096]{2,1,0:T(8,128)(2,1)}, u32[]{:S(2)}) copy-start(bf16[1,192,4096]{2,1,0:T(8,128)(2,1)} %param.13) | copy-start | bytes 4718596
  265.8 18.4 %copy-start.6 = (s32[32]{0:T(128)S(1)}, s32[32]{0:T(128)}, u32[]{:S(2)}) copy-start(s32[32]{0:T(128)} %param.17) | copy-start | bytes 388
  265.8 168.5 %all-to-all-start.1 = ((bf16[64,10,4096]{2,1,0:T(8,128)(2,1)}), bf16[64,10,4096]{2,1,0:T(8,128)(2,1)}, u32[]{:S(2)}, u32[]{:S(2)}) async-start(bf16[64,10,4096]{2,1,0:T(8,128)(2,1)} %get-tuple-element.26), calls=%async_computation.1 | async-start | bytes 16777216 | tf_op jit(solution)/shard_map/all_to_all | solution.py:111
  273.5 200.6 %collective-permute-start.2 = (bf16[1,192,4096]{2,1,0:T(8,128)(2,1)}, bf16[1,192,4096]{2,1,0:T(8,128)(2,1)}, u32[]{:S(2)}, u32[]{:S(2)}) collective-permute-start(bf16[1,192,4096]{2,1,0:T(8,128)(2,1)} %param.12), channel_id=1, source_target_pairs={{0,128},{4,132},{8,136},{12,140},{16,144},{20,148},{24,152},{28,15... | collective-permute-start | bytes 4718600 | tf_op jit(solution)/shard_map/ppermute | solution.py:68
  278.8 242.1 %collective-permute-start.1 = (bf16[1,192,4096]{2,1,0:T(8,128)(2,1)S(1)}, bf16[1,192,4096]{2,1,0:T(8,128)(2,1)}, u32[]{:S(2)}, u32[]{:S(2)}) collective-permute-start(bf16[1,192,4096]{2,1,0:T(8,128)(2,1)S(1)} %copy-done.4), channel_id=1, source_target_pairs={{0,128},{4,132},{8,136},{12,140},{16,144},{20,148},{24,152},{28,15... | collective-permute-start | bytes 4718600 | tf_op jit(solution)/shard_map/ppermute | solution.py:68
  279.0 288.5 %collective-permute-start = (bf16[1,192,4096]{2,1,0:T(8,128)(2,1)}, bf16[1,192,4096]{2,1,0:T(8,128)(2,1)}, u32[]{:S(2)}, u32[]{:S(2)}) collective-permute-start(bf16[1,192,4096]{2,1,0:T(8,128)(2,1)} %param.14), channel_id=1, source_target_pairs={{0,128},{4,132},{8,136},{12,140},{16,144},{20,148},{24,152},{28,15... | collective-permute-start | bytes 4718600 | tf_op jit(solution)/shard_map/ppermute | solution.py:68
  442.9 78.0 %copy-start.3 = (bf16[640,4096]{1,0:T(8,128)(2,1)S(1)}, bf16[640,4096]{1,0:T(8,128)(2,1)}, u32[]{:S(2)}) copy-start(bf16[640,4096]{1,0:T(8,128)(2,1)} %all_to_all.34) | copy-start | bytes 15728644
  474.1 93.3 %slice-start.2 = ((s8[5242880]{0:T(1024)(128)(4,1)}), s8[4194304]{0:T(1024)(128)(4,1)S(1)}, s32[]{:S(2)}) async-start(s8[5242880]{0:T(1024)(128)(4,1)} %bitcast.63), calls=%async_computation.6 | async-start | bytes 8388608
  479.1 88.4 %slice-start.3 = ((s8[5242880]{0:T(1024)(128)(4,1)}), s8[1048576]{0:T(1024)(128)(4,1)S(1)}, s32[]{:S(2)}) async-start(s8[5242880]{0:T(1024)(128)(4,1)} %bitcast.63), calls=%async_computation.7 | async-start | bytes 2097152
  479.1 88.4 %copy-start.7 = (bf16[1,192,4096]{2,1,0:T(8,128)(2,1)S(1)}, bf16[1,192,4096]{2,1,0:T(8,128)(2,1)}, u32[]{:S(2)}) copy-start(bf16[1,192,4096]{2,1,0:T(8,128)(2,1)} %param.14) | copy-start | bytes 4718596
  571.0 3.1 copy-start.5
  858.2 67.6 %all-to-all-start.3 = ((bf16[64,10,1152]{2,1,0:T(8,128)(2,1)}), bf16[64,10,1152]{2,1,0:T(8,128)(2,1)}, u32[]{:S(2)}, u32[]{:S(2)}) async-start(bf16[64,10,1152]{2,1,0:T(8,128)(2,1)} %all_to_all.35), calls=%async_computation.3 | async-start | bytes 4718592 | tf_op jit(solution)/shard_map/all_to_all | solution.py:145
  878.4 5.2 slice-start
  878.4 5.2 slice-start.1
  878.4 7.8 slice-start.4
  883.6 2.6 slice-start.5
  925.9 11.0 %copy-start.1 = (bf16[128,4096]{1,0:T(8,128)(2,1)S(1)}, bf16[128,4096]{1,0:T(8,128)(2,1)}, u32[]{:S(2)}) copy-start(bf16[128,4096]{1,0:T(8,128)(2,1)} %param.11) | copy-start | bytes 3145732

commit v3 on v2

--- a/solution.py
+++ b/solution.py
@@ -63,6 +63,60 @@
     )(packed)
 
 
+def dispatch_kernel(count, src_ref, out_ref, local_sem, send_sem, recv_sem):
+    me = lax.axis_index("expert")
+    group = lax.axis_index("dp")
+    barrier = pltpu.get_barrier_semaphore()
+
+    def greet(step, carry):
+        peer = lax.rem(me + step, count)
+        pl.semaphore_signal(barrier, 1, device_id=(peer, group), device_id_type=MESH_IDS)
+        return carry
+
+    lax.fori_loop(1, count, greet, 0)
+    pl.semaphore_wait(barrier, count - 1)
+    local = pltpu.make_async_copy(src_ref.at[me], out_ref.at[me], local_sem)
+    local.start()
+
+    def describe(step):
+        peer = lax.rem(me + step, count)
+        return pltpu.make_async_remote_copy(
+            src_ref=src_ref.at[peer],
+            dst_ref=out_ref.at[me],
+            send_sem=send_sem.at[step],
+            recv_sem=recv_sem.at[step],
+            device_id=(peer, group),
+            device_id_type=MESH_IDS,
+        )
+
+    def launch(step, carry):
+        describe(step).start()
+        return carry
+
+    def finish(step, carry):
+        describe(step).wait()
+        return carry
+
+    lax.fori_loop(1, count, launch, 0)
+    local.wait()
+    lax.fori_loop(1, count, finish, 0)
+
+
+def dispatch(buffer, count):
+    return pl.pallas_call(
+        lambda *refs: dispatch_kernel(count, *refs),
+        out_shape=jax.ShapeDtypeStruct(buffer.shape, buffer.dtype),
+        in_specs=[pl.BlockSpec(memory_space=pl.ANY)],
+        out_specs=pl.BlockSpec(memory_space=pl.ANY),
+        scratch_shapes=[
+            pltpu.SemaphoreType.DMA(()),
+            pltpu.SemaphoreType.DMA((count,)),
+            pltpu.SemaphoreType.DMA((count,)),
+        ],
+        compiler_params=pltpu.CompilerParams(collective_id=1, has_side_effects=True),
+    )(buffer)
+
+
 def from_behind(value, axis, by):
     devices = lax.axis_size(axis)
     return lax.ppermute(value, axis, [(i, (i + by) % devices) for i in range(devices)])
@@ -106,11 +160,13 @@
     x_buffer = jnp.where(filled[:, None], tokens[token_index], 0)
     dy_buffer = jnp.where(filled[:, None], cotangent[token_index], 0)
     gate_buffer = jnp.where(filled, gates.reshape(-1)[copy_index], 0)
-    x_rows, dy_rows, gate_rows = (
-        lax.all_to_all(x_buffer, "expert", split_axis=0, concat_axis=0, tiled=True),
-        lax.all_to_all(dy_buffer, "expert", split_axis=0, concat_axis=0, tiled=True),
-        lax.all_to_all(gate_buffer, "expert", split_axis=0, concat_axis=0, tiled=True),
-    )
+    gate_cols = jnp.zeros((expert_count * capacity, 128), jnp.bfloat16).at[:, 0].set(gate_buffer)
+    outgoing = jnp.concatenate([x_buffer, dy_buffer, gate_cols], axis=1)
+    outgoing = outgoing.reshape(expert_count, capacity, 2 * model_width + 128)
+    arrived_rows = dispatch(outgoing, expert_count).reshape(expert_count * capacity, -1)
+    x_rows = arrived_rows[:, :model_width]
+    dy_rows = arrived_rows[:, model_width : 2 * model_width]
+    gate_rows = arrived_rows[:, 2 * model_width]
     w_gate = weights[0][0]
     w_up = weights[1][0]
     w_down = weights[2][0]

time: 948 us -> 1150 us (1.21)
  Pallas kernels: 254 us -> 820 us
  waiting for transfers between devices: 293 us -> 32.3 us
  blocking collectives: 200 us -> 0 us
  starting transfers between devices: 52.6 us -> 140 us
    pallas_call x0 -> x1, Pallas kernels: none -> 687 us  [dispatch(): pl.pallas_call(lambda *refs: dispatch_kernel(count, *refs), out_shape=jax...]
    all_to_all x1 -> x0, blocking collectives: 200 us -> none  [shards(): lax.all_to_all(x_buffer, 'expert', split_axis=0, concat_axis=0, tiled=True)]
    all_to_all x2 -> x0, waiting for transfers between devices: 140 us -> none  [the longest x1 140 us: shards(): lax.all_to_all(dy_buffer, 'expert', split_axis=0, concat_axis=0, tiled=True)]
    pallas_call x1, Pallas kernels: 254 us -> 133 us  [dp_scatter(): pl.pallas_call(lambda *refs: dp_scatter_kernel(groups, *refs), out_shape=...]
    ppermute x3, waiting for transfers between devices: 116 us -> 0.01 us  [from_behind(): lax.ppermute(value, axis, [(i, (i + by) % devices) for i in range(devices)])]
    all_to_all x1, starting transfers between devices: 20.1 us -> 128 us  [shards(): lax.all_to_all(reduced, 'expert', split_axis=0, concat_axis=0, tiled=True)]
    reshape x0 -> x2, local copies, waits for them, and re-layouts: none -> 32.8 us  [the longest x1 17 us: shards(): dispatch(outgoing, expert_count).reshape(expert_count * capacity, -1)]
    all_to_all x2 -> x0, starting transfers between devices: 21.8 us -> none  [the longest x1 14.1 us: shards(): lax.all_to_all(gate_buffer, 'expert', split_axis=0, concat_axis=0, tiled=...]
  transfers between devices with their start and end apart: 6 -> 4, of which waited for: 5 -> 1; matrix products, arithmetic and copies ran while one was open for 6% -> 9% of each run, Pallas kernels for 0% -> 61%
where the time goes in v3:
time: 1150 us; the launch traced here: 1140 us
  Pallas kernels  820 us (71%)
  starting transfers between devices  140 us (12%)
  local copies, waits for them, and re-layouts  82.8 us (7%)
  waiting for transfers between devices  32.3 us (3%)
  other arithmetic  30.4 us (3%)
  matrix products  28.9 us (3%)
    pallas_call x1, Pallas kernels, dispatch(): pl.pallas_call(lambda *refs: dispatch_kernel(count, *refs), out_shape=jax...  687 us
    pallas_call x1, Pallas kernels, dp_scatter(): pl.pallas_call(lambda *refs: dp_scatter_kernel(groups, *refs), out_shape=...  133 us
    all_to_all x1, starting transfers between devices, shards(): lax.all_to_all(reduced, 'expert', split_axis=0, concat_axis=0, tiled=True)  128 us
    all_to_all x1, waiting for transfers between devices, shards(): lax.all_to_all(reduced, 'expert', split_axis=0, concat_axis=0, tiled=True)  32.3 us
  transfers between devices with their start and end apart: 4, of which 1 were waited for; matrix products, arithmetic and copies ran while one was open for 9% of the time, Pallas kernels for 61%

profile of v3, /device:TPU:35, one launch (start us, length us, event | category | flops | bytes accessed | tf_op | source)
XLA Modules:
  0.0 1135.3 jit_solution(13256650833855931786)
XLA Ops:
  0.6 6.1 collective-permute-start.2
  6.8 5.3 collective-permute-start
  19.8 5.4 gather_fusion
  25.1 5.4 gather_fusion.1
  30.5 4.3 gather_fusion.2
  35.5 8.7 broadcast_select_fusion.1
  44.4 9.8 fusion.2
  54.2 15.9 %reshape.244.refs_0_ = bf16[64,10,8320]{2,1,0:T(8,128)(2,1)} reshape(bf16[640,8320]{1,0:T(8,128)(2,1)} %fusion.2) | data formatting | bytes 21299200 | tf_op jit(solution)/shard_map/reshape | solution.py:165
  70.1 686.9 %shard_map.119 = bf16[64,10,8320]{2,1,0:T(8,128)(2,1)} custom-call(bf16[64,10,8320]{2,1,0:T(8,128)(2,1)} %reshape.244.refs_0_), custom_call_target="tpu_custom_call" | custom-call | tf_op jit(solution)/shard_map/pallas_call | solution.py:106
  757.0 17.0 %reshape.245 = bf16[640,8320]{1,0:T(8,128)(2,1)} reshape(bf16[64,10,8320]{2,1,0:T(8,128)(2,1)} %shard_map.119) | data formatting | bytes 21299200 | tf_op jit(solution)/shard_map/reshape | solution.py:166
  776.4 4.5 fusion.19
  787.6 3.9 add_convert_fusion
  791.6 9.5 reshape.246
  803.2 5.6 fusion.3
  808.8 3.4 copy.30
  812.2 132.7 %shard_map.120 = bf16[640,1152]{1,0:T(8,128)(2,1)} custom-call(bf16[640,4608]{1,0:T(8,128)(2,1)} %bitcast.54), custom_call_target="tpu_custom_call" | custom-call | tf_op jit(solution)/shard_map/pallas_call | solution.py:52
  945.0 3.7 all_to_all.8
  948.6 128.2 %all-to-all-start = ((bf16[64,10,1152]{2,1,0:T(8,128)(2,1)}), bf16[64,10,1152]{2,1,0:T(8,128)(2,1)}, u32[]{:S(2)}, u32[]{:S(2)}) async-start(bf16[64,10,1152]{2,1,0:T(8,128)(2,1)} %all_to_all.8), calls=%async_computation | async-start | bytes 4718592 | tf_op jit(solution)/shard_map/all_to_all | solution.py:201
  1076.8 5.0 fusion.10
  1081.9 5.0 fusion.9
  1086.9 5.2 fusion.11
  1092.0 32.3 %all-to-all-done = bf16[64,10,1152]{2,1,0:T(8,128)(2,1)} async-done(((bf16[64,10,1152]{2,1,0:T(8,128)(2,1)}), bf16[64,10,1152]{2,1,0:T(8,128)(2,1)}, u32[]{:S(2)}, u32[]{:S(2)}) %all-to-all-start) | async-done | bytes 1474592 | tf_op jit(solution)/shard_map/all_to_all | solution.py:201
  1124.3 2.8 all_to_all.10
  1127.1 2.8 gather_fusion.3
  (56 shorter events, 24.4 us)
Async XLA Ops:
  0.6 19.1 %copy-start = (bf16[128,4096]{1,0:T(8,128)(2,1)S(1)}, bf16[128,4096]{1,0:T(8,128)(2,1)}, u32[]{:S(2)}) copy-start(bf16[128,4096]{1,0:T(8,128)(2,1)} %param.12) | copy-start | bytes 3145732
  0.6 775.7 %collective-permute-start.2 = (bf16[1,192,4096]{2,1,0:T(8,128)(2,1)}, bf16[1,192,4096]{2,1,0:T(8,128)(2,1)}, u32[]{:S(2)}, u32[]{:S(2)}) collective-permute-start(bf16[1,192,4096]{2,1,0:T(8,128)(2,1)} %param.14), channel_id=1, source_target_pairs={{0,128},{4,132},{8,136},{12,140},{16,144},{20,148},{24,152},{28,15... | collective-permute-start | bytes 4718600 | tf_op jit(solution)/shard_map/ppermute | solution.py:122
  6.7 774.2 %collective-permute-start.1 = (bf16[1,192,4096]{2,1,0:T(8,128)(2,1)}, bf16[1,192,4096]{2,1,0:T(8,128)(2,1)}, u32[]{:S(2)}, u32[]{:S(2)}) collective-permute-start(bf16[1,192,4096]{2,1,0:T(8,128)(2,1)} %param.15), channel_id=1, source_target_pairs={{0,128},{4,132},{8,136},{12,140},{16,144},{20,148},{24,152},{28,15... | collective-permute-start | bytes 4718600 | tf_op jit(solution)/shard_map/ppermute | solution.py:122
  6.8 777.3 %collective-permute-start = (bf16[1,192,4096]{2,1,0:T(8,128)(2,1)}, bf16[1,192,4096]{2,1,0:T(8,128)(2,1)}, u32[]{:S(2)}, u32[]{:S(2)}) collective-permute-start(bf16[1,192,4096]{2,1,0:T(8,128)(2,1)} %param.16), channel_id=1, source_target_pairs={{0,128},{4,132},{8,136},{12,140},{16,144},{20,148},{24,152},{28,15... | collective-permute-start | bytes 4718600 | tf_op jit(solution)/shard_map/ppermute | solution.py:122
  19.7 5.4 copy-start.2
  757.0 18.1 %copy-start.6 = (s32[32]{0:T(128)S(1)}, s32[32]{0:T(128)}, u32[]{:S(2)}) copy-start(s32[32]{0:T(128)} %param.19) | copy-start | bytes 388
  757.0 19.4 %copy-start.5 = (bf16[1,192,4096]{2,1,0:T(8,128)(2,1)S(1)}, bf16[1,192,4096]{2,1,0:T(8,128)(2,1)}, u32[]{:S(2)}) copy-start(bf16[1,192,4096]{2,1,0:T(8,128)(2,1)} %param.14) | copy-start | bytes 4718596
  776.4 5.6 copy-start.3
  776.4 6.0 copy-start.4
  780.9 3.2 copy-start.7
  948.6 175.7 %all-to-all-start = ((bf16[64,10,1152]{2,1,0:T(8,128)(2,1)}), bf16[64,10,1152]{2,1,0:T(8,128)(2,1)}, u32[]{:S(2)}, u32[]{:S(2)}) async-start(bf16[64,10,1152]{2,1,0:T(8,128)(2,1)} %all_to_all.8), calls=%async_computation | async-start | bytes 4718592 | tf_op jit(solution)/shard_map/all_to_all | solution.py:201
  1124.3 11.0 copy-start.1

commit v4 on v2

--- a/solution.py
+++ b/solution.py
@@ -61,6 +61,49 @@
         ],
         compiler_params=pltpu.CompilerParams(collective_id=0, has_side_effects=True),
     )(packed)
+
+
+def dp_gather_kernel(groups, src_ref, out_ref, local_sem, send_sem, recv_sem):
+    me = lax.axis_index("dp")
+    home = lax.axis_index("expert")
+    barrier = pltpu.get_barrier_semaphore()
+    for step in range(1, groups):
+        peer = lax.rem(me + step, groups)
+        pl.semaphore_signal(barrier, 1, device_id=(home, peer), device_id_type=MESH_IDS)
+    pl.semaphore_wait(barrier, groups - 1)
+    copies = []
+    for step in range(1, groups):
+        peer = lax.rem(me + step, groups)
+        copy = pltpu.make_async_remote_copy(
+            src_ref=src_ref,
+            dst_ref=out_ref.at[me],
+            send_sem=send_sem.at[step],
+            recv_sem=recv_sem.at[step],
+            device_id=(home, peer),
+            device_id_type=MESH_IDS,
+        )
+        copy.start()
+        copies.append(copy)
+    local = pltpu.make_async_copy(src_ref, out_ref.at[me], local_sem)
+    local.start()
+    local.wait()
+    for copy in copies:
+        copy.wait()
+
+
+def dp_gather(chunk, groups):
+    return pl.pallas_call(
+        lambda *refs: dp_gather_kernel(groups, *refs),
+        out_shape=jax.ShapeDtypeStruct((groups,) + chunk.shape, chunk.dtype),
+        in_specs=[pl.BlockSpec(memory_space=pl.ANY)],
+        out_specs=pl.BlockSpec(memory_space=pl.ANY),
+        scratch_shapes=[
+            pltpu.SemaphoreType.DMA(()),
+            pltpu.SemaphoreType.DMA((groups,)),
+            pltpu.SemaphoreType.DMA((groups,)),
+        ],
+        compiler_params=pltpu.CompilerParams(collective_id=2, has_side_effects=True),
+    )(chunk)
 
 
 def from_behind(value, axis, by):
@@ -103,14 +146,19 @@
     filled = source > 0
     copy_index = jnp.maximum(source - 1, 0)
     token_index = copy_index // routed
-    x_buffer = jnp.where(filled[:, None], tokens[token_index], 0)
-    dy_buffer = jnp.where(filled[:, None], cotangent[token_index], 0)
+    my_group = lax.axis_index("dp")
+    x_part = lax.dynamic_slice_in_dim(tokens, my_group * quarter, quarter, axis=1)
+    dy_part = lax.dynamic_slice_in_dim(cotangent, my_group * quarter, quarter, axis=1)
+    x_buffer = jnp.where(filled[:, None], x_part[token_index], 0)
+    dy_buffer = jnp.where(filled[:, None], dy_part[token_index], 0)
     gate_buffer = jnp.where(filled, gates.reshape(-1)[copy_index], 0)
-    x_rows, dy_rows, gate_rows = (
-        lax.all_to_all(x_buffer, "expert", split_axis=0, concat_axis=0, tiled=True),
-        lax.all_to_all(dy_buffer, "expert", split_axis=0, concat_axis=0, tiled=True),
-        lax.all_to_all(gate_buffer, "expert", split_axis=0, concat_axis=0, tiled=True),
-    )
+    gate_cols = jnp.zeros((expert_count * capacity, 128), jnp.bfloat16).at[:, 0].set(gate_buffer)
+    outgoing = jnp.concatenate([x_buffer, dy_buffer, gate_cols], axis=1)
+    arrived = lax.all_to_all(outgoing, "expert", split_axis=0, concat_axis=0, tiled=True)
+    gathered = dp_gather(arrived, groups)
+    x_rows = jnp.transpose(gathered[:, :, :quarter], (1, 0, 2)).reshape(-1, model_width)
+    dy_rows = jnp.transpose(gathered[:, :, quarter : 2 * quarter], (1, 0, 2)).reshape(-1, model_width)
+    gate_rows = gathered[0, :, 2 * quarter]
     w_gate = weights[0][0]
     w_up = weights[1][0]
     w_down = weights[2][0]

time: 948 us -> 887 us (0.936)
  Pallas kernels: 254 us -> 556 us
  blocking collectives: 200 us -> 0 us
  waiting for transfers between devices: 293 us -> 161 us
  other arithmetic: 22.1 us -> 12.5 us
    pallas_call x0 -> x1, Pallas kernels: none -> 398 us  [dp_gather(): pl.pallas_call(lambda *refs: dp_gather_kernel(groups, *refs), out_shape=j...]
    all_to_all x1 -> x0, blocking collectives: 200 us -> none  [shards(): lax.all_to_all(x_buffer, 'expert', split_axis=0, concat_axis=0, tiled=True)]
    ppermute x3, waiting for transfers between devices: 116 us -> 0.01 us  [from_behind(): lax.ppermute(value, axis, [(i, (i + by) % devices) for i in range(devices)])]
    pallas_call x1, Pallas kernels: 254 us -> 158 us  [dp_scatter(): pl.pallas_call(lambda *refs: dp_scatter_kernel(groups, *refs), out_shape=...]
    transpose x0 -> x3, local copies, waits for them, and re-layouts: none -> 25 us  [the longest x2 17.1 us: shards(): jnp.transpose(gathered[:, :, :quarter], (1, 0, 2)).reshape(-1, model_width)]
    gather x4 -> x2, local copies, waits for them, and re-layouts: 27.2 us -> 5.68 us  [the longest x1 2.84 us: shards(): dy_buffer = jnp.where(filled[:, None], dy_part[token_index], 0)]
    all_to_all x2 -> x1, waiting for transfers between devices: 140 us -> 125 us  [shards(): lax.all_to_all(outgoing, 'expert', split_axis=0, concat_axis=0, tiled=True)]
    select_n x2, other arithmetic: 11.4 us -> 0.25 us  [shards(): x_buffer = jnp.where(filled[:, None], x_part[token_index], 0)]
  transfers between devices with their start and end apart: 6 -> 5, of which waited for: 5 -> 2; matrix products, arithmetic and copies ran while one was open for 6% -> 5% of each run, Pallas kernels for 0% -> 45%
where the time goes in v4:
time: 887 us; the launch traced here: 876 us
  Pallas kernels  556 us (63%)
  waiting for transfers between devices  161 us (18%)
  local copies, waits for them, and re-layouts  75.9 us (9%)
  starting transfers between devices  43.8 us (5%)
  matrix products  25.1 us (3%)
  other arithmetic  12.5 us (1%)
    pallas_call x1, Pallas kernels, dp_gather(): pl.pallas_call(lambda *refs: dp_gather_kernel(groups, *refs), out_shape=j...  398 us
    pallas_call x1, Pallas kernels, dp_scatter(): pl.pallas_call(lambda *refs: dp_scatter_kernel(groups, *refs), out_shape=...  158 us
    all_to_all x1, waiting for transfers between devices, shards(): lax.all_to_all(outgoing, 'expert', split_axis=0, concat_axis=0, tiled=True)  125 us
    all_to_all x1, waiting for transfers between devices, shards(): lax.all_to_all(reduced, 'expert', split_axis=0, concat_axis=0, tiled=True)  35.7 us
    all_to_all x1, starting transfers between devices, shards(): lax.all_to_all(reduced, 'expert', split_axis=0, concat_axis=0, tiled=True)  18.7 us
  transfers between devices with their start and end apart: 5, of which 2 were waited for; matrix products, arithmetic and copies ran while one was open for 5% of the time, Pallas kernels for 45%

profile of v4, /device:TPU:35, one launch (start us, length us, event | category | flops | bytes accessed | tf_op | source)
XLA Modules:
  0.0 875.5 jit_solution(5378515731760275312)
XLA Ops:
  8.3 4.3 gather_fusion.2
  14.4 2.8 gather_fusion.1
  20.6 3.0 all_to_all.15
  23.6 14.5 %all-to-all-start = ((bf16[64,10,2176]{2,1,0:T(8,128)(2,1)}), bf16[64,10,2176]{2,1,0:T(8,128)(2,1)}, u32[]{:S(2)}, u32[]{:S(2)}) async-start(bf16[64,10,2176]{2,1,0:T(8,128)(2,1)} %all_to_all.15), calls=%async_computation | async-start | bytes 8912896 | tf_op jit(solution)/shard_map/all_to_all | solution.py:157
  38.1 5.3 collective-permute-start.1
  43.5 5.2 collective-permute-start
  50.0 125.0 %all-to-all-done = bf16[64,10,2176]{2,1,0:T(8,128)(2,1)} async-done(((bf16[64,10,2176]{2,1,0:T(8,128)(2,1)}), bf16[64,10,2176]{2,1,0:T(8,128)(2,1)}, u32[]{:S(2)}, u32[]{:S(2)}) %all-to-all-start) | async-done | bytes 2785312 | tf_op jit(solution)/shard_map/all_to_all | solution.py:157
  175.0 5.6 all_to_all.17.refs_0_
  180.6 397.6 %shard_map.119 = bf16[4,640,2176]{2,1,0:T(8,128)(2,1)} custom-call(bf16[640,2176]{1,0:T(8,128)(2,1)} %all_to_all.17.refs_0_), custom_call_target="tpu_custom_call" | custom-call | tf_op jit(solution)/shard_map/pallas_call | solution.py:95
  578.3 9.2 %slice_bitcast_fusion = (bf16[640,4,1024]{2,0,1:T(8,128)(2,1)}, bf16[640,4,1024]{2,0,1:T(8,128)(2,1)}) fusion(bf16[4,640,2176]{2,1,0:T(8,128)(2,1)} %shard_map.119), kind=kLoop, calls=%fused_computation.13 | loop fusion | bytes 20971520 | tf_op jit(solution)/shard_map/transpose | solution.py:159
  587.4 7.9 copy.30
  596.4 7.9 copy.29
  604.3 4.0 fusion.20
  614.4 3.9 add_convert_fusion
  618.2 9.5 %reshape.254 = bf16[640,4,1024]{2,1,0:T(4,128)(2,1)} reshape(bf16[640,4096]{1,0:T(8,128)(2,1)} %add_convert_fusion) | data formatting | bytes 10485760 | tf_op jit(solution)/shard_map/reshape | solution.py:189
  629.9 5.8 fusion.1
  635.7 3.5 copy.34
  639.2 158.3 %shard_map.120 = bf16[640,1152]{1,0:T(8,128)(2,1)} custom-call(bf16[640,4608]{1,0:T(8,128)(2,1)} %bitcast.66), custom_call_target="tpu_custom_call" | custom-call | tf_op jit(solution)/shard_map/pallas_call | solution.py:52
  797.5 3.7 all_to_all.18
  801.1 18.7 %all-to-all-start.1 = ((bf16[64,10,1152]{2,1,0:T(8,128)(2,1)}), bf16[64,10,1152]{2,1,0:T(8,128)(2,1)}, u32[]{:S(2)}, u32[]{:S(2)}) async-start(bf16[64,10,1152]{2,1,0:T(8,128)(2,1)} %all_to_all.18), calls=%async_computation.1 | async-start | bytes 4718592 | tf_op jit(solution)/shard_map/all_to_all | solution.py:193
  819.9 5.7 fusion.8
  825.6 3.1 fusion.9
  828.7 3.2 fusion.10
  831.8 35.7 %all-to-all-done.1 = bf16[64,10,1152]{2,1,0:T(8,128)(2,1)} async-done(((bf16[64,10,1152]{2,1,0:T(8,128)(2,1)}), bf16[64,10,1152]{2,1,0:T(8,128)(2,1)}, u32[]{:S(2)}, u32[]{:S(2)}) %all-to-all-start.1) | async-done | bytes 1474592 | tf_op jit(solution)/shard_map/all_to_all | solution.py:193
  (77 shorter events, 30.7 us)
Async XLA Ops:
  23.6 14.5 %copy-start.1 = (bf16[1,192,4096]{2,1,0:T(8,128)(2,1)S(1)}, bf16[1,192,4096]{2,1,0:T(8,128)(2,1)}, u32[]{:S(2)}) copy-start(bf16[1,192,4096]{2,1,0:T(8,128)(2,1)} %param.15) | copy-start | bytes 4718596
  23.6 19.8 %copy-start.2 = (bf16[1,192,4096]{2,1,0:T(8,128)(2,1)S(1)}, bf16[1,192,4096]{2,1,0:T(8,128)(2,1)}, u32[]{:S(2)}) copy-start(bf16[1,192,4096]{2,1,0:T(8,128)(2,1)} %param.14) | copy-start | bytes 4718596
  23.6 25.2 %copy-start.5 = (s32[32]{0:T(128)S(1)}, s32[32]{0:T(128)}, u32[]{:S(2)}) copy-start(s32[32]{0:T(128)} %param.19) | copy-start | bytes 388
  23.6 151.4 %all-to-all-start = ((bf16[64,10,2176]{2,1,0:T(8,128)(2,1)}), bf16[64,10,2176]{2,1,0:T(8,128)(2,1)}, u32[]{:S(2)}, u32[]{:S(2)}) async-start(bf16[64,10,2176]{2,1,0:T(8,128)(2,1)} %all_to_all.15), calls=%async_computation | async-start | bytes 8912896 | tf_op jit(solution)/shard_map/all_to_all | solution.py:157
  38.1 566.2 %collective-permute-start.1 = (bf16[1,192,4096]{2,1,0:T(8,128)(2,1)S(1)}, bf16[1,192,4096]{2,1,0:T(8,128)(2,1)}, u32[]{:S(2)}, u32[]{:S(2)}) collective-permute-start(bf16[1,192,4096]{2,1,0:T(8,128)(2,1)S(1)} %copy-done.1), channel_id=1, source_target_pairs={{0,128},{4,132},{8,136},{12,140},{16,144},{20,148},{24,152},{28,15... | collective-permute-start | bytes 4718600 | tf_op jit(solution)/shard_map/ppermute | solution.py:111
  43.4 565.0 %collective-permute-start.2 = (bf16[1,192,4096]{2,1,0:T(8,128)(2,1)S(1)}, bf16[1,192,4096]{2,1,0:T(8,128)(2,1)}, u32[]{:S(2)}, u32[]{:S(2)}) collective-permute-start(bf16[1,192,4096]{2,1,0:T(8,128)(2,1)S(1)} %copy-done.2), channel_id=1, source_target_pairs={{0,128},{4,132},{8,136},{12,140},{16,144},{20,148},{24,152},{28,15... | collective-permute-start | bytes 4718600 | tf_op jit(solution)/shard_map/ppermute | solution.py:111
  43.5 566.3 %collective-permute-start = (bf16[1,192,4096]{2,1,0:T(8,128)(2,1)}, bf16[1,192,4096]{2,1,0:T(8,128)(2,1)}, u32[]{:S(2)}, u32[]{:S(2)}) collective-permute-start(bf16[1,192,4096]{2,1,0:T(8,128)(2,1)} %param.16), channel_id=1, source_target_pairs={{0,128},{4,132},{8,136},{12,140},{16,144},{20,148},{24,152},{28,15... | collective-permute-start | bytes 4718600 | tf_op jit(solution)/shard_map/ppermute | solution.py:111
  604.3 4.1 copy-start
  604.3 5.6 slice-start.2
  608.4 1.7 slice-start.3
  608.4 2.2 copy-start.6
  612.8 1.6 copy-start.3
  801.1 18.7 %copy-start.4 = (bf16[640,192]{0,1:T(8,128)(2,1)S(1)}, bf16[640,192]{0,1:T(8,128)(2,1)}, u32[]{:S(2)}) copy-start(bf16[640,192]{0,1:T(8,128)(2,1)} %copy-done.3) | copy-start | bytes 737284
  801.1 24.4 %slice-start = ((s8[5242880]{0:T(1024)(128)(4,1)}), s8[1048576]{0:T(1024)(128)(4,1)S(1)}, s32[]{:S(2)}) async-start(s8[5242880]{0:T(1024)(128)(4,1)} %bitcast.71), calls=%async_computation.2 | async-start | bytes 2097152
  801.1 66.4 %all-to-all-start.1 = ((bf16[64,10,1152]{2,1,0:T(8,128)(2,1)}), bf16[64,10,1152]{2,1,0:T(8,128)(2,1)}, u32[]{:S(2)}, u32[]{:S(2)}) async-start(bf16[64,10,1152]{2,1,0:T(8,128)(2,1)} %all_to_all.18), calls=%async_computation.1 | async-start | bytes 4718592 | tf_op jit(solution)/shard_map/all_to_all | solution.py:193
  819.8 5.7 slice-start.1
  819.9 8.8 %slice-start.4 = ((s8[5242880]{0:T(1024)(128)(4,1)}), s8[4194304]{0:T(1024)(128)(4,1)S(1)}, s32[]{:S(2)}) async-start(s8[5242880]{0:T(1024)(128)(4,1)} %bitcast.77), calls=%async_computation.6 | async-start | bytes 8388608
  825.6 3.1 slice-start.5
  825.6 3.1 copy-start.7

commit v5 on v4

--- a/solution.py
+++ b/solution.py
@@ -8,10 +8,10 @@
 MESH_IDS = pl.DeviceIdType.MESH
 
 
-def dp_scatter_kernel(groups, src_ref, out_ref, landing, send_sem, recv_sem):
+def dp_scatter_kernel(groups, src_ref, score_ref, out_ref, landing, score_in, send_sem, recv_sem):
     me = lax.axis_index("dp")
     home = lax.axis_index("expert")
-    width = out_ref.shape[1]
+    width = landing.shape[2]
     barrier = pltpu.get_barrier_semaphore()
     for step in range(1, groups):
         peer = lax.rem(me + step, groups)
@@ -20,16 +20,19 @@
     copies = []
     for step in range(1, groups):
         peer = lax.rem(me + step, groups)
-        copy = pltpu.make_async_remote_copy(
-            src_ref=src_ref.at[:, pl.ds(pl.multiple_of(peer * width, 128), width)],
-            dst_ref=landing.at[step],
-            send_sem=send_sem.at[step],
-            recv_sem=recv_sem.at[step],
-            device_id=(home, peer),
-            device_id_type=MESH_IDS,
-        )
-        copy.start()
-        copies.append(copy)
+        for part, (source, target) in enumerate(
+            ((src_ref.at[:, pl.ds(pl.multiple_of(peer * width, 128), width)], landing), (score_ref, score_in))
+        ):
+            copy = pltpu.make_async_remote_copy(
+                src_ref=source,
+                dst_ref=target.at[step],
+                send_sem=send_sem.at[step, part],
+                recv_sem=recv_sem.at[step, part],
+                device_id=(home, peer),
+                device_id_type=MESH_IDS,
+            )
+            copy.start()
+            copies.append(copy)
     for copy in copies:
         copy.wait()
     own = pl.multiple_of(me * width, 128)
@@ -38,32 +41,36 @@
     def body(i, carry):
         rows = pl.ds(pl.multiple_of(i * block, block), block)
         total = src_ref[rows, pl.ds(own, width)].astype(jnp.float32)
+        score = score_ref[rows, :]
         for step in range(1, groups):
             total = total + landing[step, rows, :].astype(jnp.float32)
-        out_ref[rows, :] = total.astype(out_ref.dtype)
+            score = score + score_in[step, rows, :]
+        out_ref[rows, pl.ds(0, width)] = total.astype(out_ref.dtype)
+        out_ref[rows, pl.ds(width, 128)] = score.astype(out_ref.dtype)
         return carry
 
     lax.fori_loop(0, out_ref.shape[0] // block, body, 0)
 
 
-def dp_scatter(packed, groups):
-    rows, full = packed.shape
+def dp_scatter(partial, score, groups):
+    rows, full = partial.shape
     width = full // groups
     return pl.pallas_call(
         lambda *refs: dp_scatter_kernel(groups, *refs),
-        out_shape=jax.ShapeDtypeStruct((rows, width), packed.dtype),
-        in_specs=[pl.BlockSpec(memory_space=pltpu.VMEM)],
+        out_shape=jax.ShapeDtypeStruct((rows, width + 128), partial.dtype),
+        in_specs=[pl.BlockSpec(memory_space=pltpu.VMEM)] * 2,
         out_specs=pl.BlockSpec(memory_space=pltpu.VMEM),
         scratch_shapes=[
-            pltpu.VMEM((groups, rows, width), packed.dtype),
-            pltpu.SemaphoreType.DMA((groups,)),
-            pltpu.SemaphoreType.DMA((groups,)),
+            pltpu.VMEM((groups, rows, width), partial.dtype),
+            pltpu.VMEM((groups, rows, 128), score.dtype),
+            pltpu.SemaphoreType.DMA((groups, 2)),
+            pltpu.SemaphoreType.DMA((groups, 2)),
         ],
         compiler_params=pltpu.CompilerParams(collective_id=0, has_side_effects=True),
-    )(packed)
-
-
-def dp_gather_kernel(groups, src_ref, out_ref, local_sem, send_sem, recv_sem):
+    )(partial, score)
+
+
+def dp_gather_kernel(groups, width, src_ref, x_ref, dy_ref, local_sem, send_sem, recv_sem):
     me = lax.axis_index("dp")
     home = lax.axis_index("expert")
     barrier = pltpu.get_barrier_semaphore()
@@ -71,36 +78,43 @@
         peer = lax.rem(me + step, groups)
         pl.semaphore_signal(barrier, 1, device_id=(home, peer), device_id_type=MESH_IDS)
     pl.semaphore_wait(barrier, groups - 1)
+    mine = pl.ds(pl.multiple_of(me * width, 128), width)
     copies = []
     for step in range(1, groups):
         peer = lax.rem(me + step, groups)
-        copy = pltpu.make_async_remote_copy(
-            src_ref=src_ref,
-            dst_ref=out_ref.at[me],
-            send_sem=send_sem.at[step],
-            recv_sem=recv_sem.at[step],
-            device_id=(home, peer),
-            device_id_type=MESH_IDS,
+        for part, dst in enumerate((x_ref, dy_ref)):
+            copy = pltpu.make_async_remote_copy(
+                src_ref=src_ref.at[:, pl.ds(part * width, width)],
+                dst_ref=dst.at[:, mine],
+                send_sem=send_sem.at[step, part],
+                recv_sem=recv_sem.at[step, part],
+                device_id=(home, peer),
+                device_id_type=MESH_IDS,
+            )
+            copy.start()
+            copies.append(copy)
+    for part, dst in enumerate((x_ref, dy_ref)):
+        local = pltpu.make_async_copy(
+            src_ref.at[:, pl.ds(part * width, width)], dst.at[:, mine], local_sem.at[part]
         )
-        copy.start()
-        copies.append(copy)
-    local = pltpu.make_async_copy(src_ref, out_ref.at[me], local_sem)
-    local.start()
-    local.wait()
+        local.start()
+        copies.append(local)
     for copy in copies:
         copy.wait()
 
 
-def dp_gather(chunk, groups):
+def dp_gather(chunk, groups, width):
+    rows = chunk.shape[0]
+    full = jax.ShapeDtypeStruct((rows, groups * width), chunk.dtype)
     return pl.pallas_call(
-        lambda *refs: dp_gather_kernel(groups, *refs),
-        out_shape=jax.ShapeDtypeStruct((groups,) + chunk.shape, chunk.dtype),
+        lambda *refs: dp_gather_kernel(groups, width, *refs),
+        out_shape=(full, full),
         in_specs=[pl.BlockSpec(memory_space=pl.ANY)],
-        out_specs=pl.BlockSpec(memory_space=pl.ANY),
+        out_specs=(pl.BlockSpec(memory_space=pl.ANY), pl.BlockSpec(memory_space=pl.ANY)),
         scratch_shapes=[
-            pltpu.SemaphoreType.DMA(()),
-            pltpu.SemaphoreType.DMA((groups,)),
-            pltpu.SemaphoreType.DMA((groups,)),
+            pltpu.SemaphoreType.DMA((2,)),
+            pltpu.SemaphoreType.DMA((groups, 2)),
+            pltpu.SemaphoreType.DMA((groups, 2)),
         ],
         compiler_params=pltpu.CompilerParams(collective_id=2, has_side_effects=True),
     )(chunk)
@@ -155,10 +169,8 @@
     gate_cols = jnp.zeros((expert_count * capacity, 128), jnp.bfloat16).at[:, 0].set(gate_buffer)
     outgoing = jnp.concatenate([x_buffer, dy_buffer, gate_cols], axis=1)
     arrived = lax.all_to_all(outgoing, "expert", split_axis=0, concat_axis=0, tiled=True)
-    gathered = dp_gather(arrived, groups)
-    x_rows = jnp.transpose(gathered[:, :, :quarter], (1, 0, 2)).reshape(-1, model_width)
-    dy_rows = jnp.transpose(gathered[:, :, quarter : 2 * quarter], (1, 0, 2)).reshape(-1, model_width)
-    gate_rows = gathered[0, :, 2 * quarter]
+    x_rows, dy_rows = dp_gather(arrived, groups, quarter)
+    gate_rows = arrived[:, 2 * quarter]
     w_gate = weights[0][0]
     w_up = weights[1][0]
     w_down = weights[2][0]
@@ -183,13 +195,8 @@
     )
     grad_wup = lax.dot_general(grad_up, x_rows, contract_rows, preferred_element_type=jnp.float32)
     grad_wdown = lax.dot_general(hidden, scaled, contract_rows, preferred_element_type=jnp.float32)
-    score_cols = jnp.zeros((capacity * expert_count, groups, 128), jnp.float32)
-    score_cols = score_cols.at[:, :, 0].set(score_part[:, None])
-    packed = jnp.concatenate(
-        [input_part.reshape(capacity * expert_count, groups, quarter), score_cols], axis=2
-    ).astype(jnp.bfloat16)
-    packed = packed.reshape(capacity * expert_count, groups * (quarter + 128))
-    reduced = dp_scatter(packed, groups)
+    score_cols = jnp.zeros((capacity * expert_count, 128), jnp.float32).at[:, 0].set(score_part)
+    reduced = dp_scatter(input_part.astype(jnp.bfloat16), score_cols, groups)
     back_rows = lax.all_to_all(reduced, "expert", split_axis=0, concat_axis=0, tiled=True)
     per_copy = back_rows[buffer_index].reshape(row_count, routed, quarter + 128)
     input_grad = jnp.sum(per_copy[:, :, :quarter].astype(jnp.float32), axis=1).astype(jnp.bfloat16)

time: 887 us -> 842 us (0.949)
  local copies, waits for them, and re-layouts: 75.9 us -> 36.2 us
    transpose x3 -> x0, local copies, waits for them, and re-layouts: 25 us -> none  [the longest x2 17.1 us: shards(): jnp.transpose(gathered[:, :, :quarter], (1, 0, 2)).reshape(-1, model_width)]
    pallas_call x1, Pallas kernels: 398 us -> 384 us  [dp_gather(): pl.pallas_call(lambda *refs: dp_gather_kernel(groups, width, *refs), out_...]
    reshape x1 -> x0, local copies, waits for them, and re-layouts: 9.5 us -> none  [shards(): input_part.reshape(capacity * expert_count, groups, quarter)]
  transfers between devices with their start and end apart: 5 -> 5, of which waited for: 2 -> 2; matrix products, arithmetic and copies ran while one was open for 5% -> 2% of each run, Pallas kernels for 45% -> 46%
where the time goes in v5:
time: 842 us; the launch traced here: 832 us
  Pallas kernels  549 us (65%)
  waiting for transfers between devices  163 us (19%)
  starting transfers between devices  50.3 us (6%)
  local copies, waits for them, and re-layouts  36.2 us (4%)
  matrix products  24.2 us (3%)
    pallas_call x1, Pallas kernels, dp_gather(): pl.pallas_call(lambda *refs: dp_gather_kernel(groups, width, *refs), out_...  384 us
    pallas_call x1, Pallas kernels, dp_scatter(): pl.pallas_call(lambda *refs: dp_scatter_kernel(groups, *refs), out_shape=...  166 us
    all_to_all x1, waiting for transfers between devices, shards(): lax.all_to_all(outgoing, 'expert', split_axis=0, concat_axis=0, tiled=True)  125 us
    all_to_all x1, waiting for transfers between devices, shards(): lax.all_to_all(reduced, 'expert', split_axis=0, concat_axis=0, tiled=True)  37.6 us
    all_to_all x1, starting transfers between devices, shards(): lax.all_to_all(reduced, 'expert', split_axis=0, concat_axis=0, tiled=True)  25.1 us
  transfers between devices with their start and end apart: 5, of which 2 were waited for; matrix products, arithmetic and copies ran while one was open for 2% of the time, Pallas kernels for 46%

profile of v5, /device:TPU:35, one launch (start us, length us, event | category | flops | bytes accessed | tf_op | source)
XLA Modules:
  0.0 831.8 jit_solution(5563296197751492421)
XLA Ops:
  4.8 2.4 scatter_custom_fusion
  9.3 2.8 gather_fusion
  12.2 2.8 gather_fusion.1
  15.0 4.3 gather_fusion.2
  20.6 3.0 all_to_all.15
  23.6 14.5 %all-to-all-start = ((bf16[64,10,2176]{2,1,0:T(8,128)(2,1)}), bf16[64,10,2176]{2,1,0:T(8,128)(2,1)}, u32[]{:S(2)}, u32[]{:S(2)}) async-start(bf16[64,10,2176]{2,1,0:T(8,128)(2,1)} %all_to_all.15), calls=%async_computation | async-start | bytes 8912896 | tf_op jit(solution)/shard_map/all_to_all | solution.py:171
  38.1 5.3 collective-permute-start.2
  43.5 5.2 collective-permute-start
  50.0 125.0 %all-to-all-done = bf16[64,10,2176]{2,1,0:T(8,128)(2,1)} async-done(((bf16[64,10,2176]{2,1,0:T(8,128)(2,1)}), bf16[64,10,2176]{2,1,0:T(8,128)(2,1)}, u32[]{:S(2)}, u32[]{:S(2)}) %all-to-all-start) | async-done | bytes 2785312 | tf_op jit(solution)/shard_map/all_to_all | solution.py:171
  175.0 5.7 all_to_all.17.refs_0_
  180.7 383.6 %shard_map.119 = (bf16[640,4096]{1,0:T(8,128)(2,1)}, bf16[640,4096]{1,0:T(8,128)(2,1)}) custom-call(bf16[640,2176]{1,0:T(8,128)(2,1)} %all_to_all.17.refs_0_), custom_call_target="tpu_custom_call" | custom-call | tf_op jit(solution)/shard_map/pallas_call | solution.py:109
  565.6 4.5 fusion.14
  572.1 2.0 multiply_reduce_fusion
  577.3 3.9 add_convert_fusion.refs_0_
  581.2 165.8 %shard_map.120 = bf16[640,1152]{1,0:T(8,128)(2,1)} custom-call(bf16[640,4096]{1,0:T(8,128)(2,1)} %add_convert_fusion.refs_0_, f32[640,128]{1,0:T(8,128)} %scatter.19.refs_1_), custom_call_target="tpu_custom_call" | custom-call | tf_op jit(solution)/shard_map/pallas_call | solution.py:58
  747.0 3.7 all_to_all.18
  750.6 25.1 %all-to-all-start.1 = ((bf16[64,10,1152]{2,1,0:T(8,128)(2,1)}), bf16[64,10,1152]{2,1,0:T(8,128)(2,1)}, u32[]{:S(2)}, u32[]{:S(2)}) async-start(bf16[64,10,1152]{2,1,0:T(8,128)(2,1)} %all_to_all.18), calls=%async_computation.1 | async-start | bytes 4718592 | tf_op jit(solution)/shard_map/all_to_all | solution.py:200
  775.8 5.2 fusion.7
  781.0 2.5 fusion.6
  783.6 2.6 fusion.8
  786.2 37.6 %all-to-all-done.1 = bf16[64,10,1152]{2,1,0:T(8,128)(2,1)} async-done(((bf16[64,10,1152]{2,1,0:T(8,128)(2,1)}), bf16[64,10,1152]{2,1,0:T(8,128)(2,1)}, u32[]{:S(2)}, u32[]{:S(2)}) %all-to-all-start.1) | async-done | bytes 1474592 | tf_op jit(solution)/shard_map/all_to_all | solution.py:200
  823.8 2.7 all_to_all.20
  826.5 2.1 gather_fusion.3
  828.9 2.2 slice_reduce_fusion
  (72 shorter events, 15.6 us)
Async XLA Ops:
  23.6 14.5 %copy-start.1 = (bf16[1,192,4096]{2,1,0:T(8,128)(2,1)S(1)}, bf16[1,192,4096]{2,1,0:T(8,128)(2,1)}, u32[]{:S(2)}) copy-start(bf16[1,192,4096]{2,1,0:T(8,128)(2,1)} %param.14) | copy-start | bytes 4718596
  23.6 19.8 %copy-start = (bf16[1,192,4096]{2,1,0:T(8,128)(2,1)S(1)}, bf16[1,192,4096]{2,1,0:T(8,128)(2,1)}, u32[]{:S(2)}) copy-start(bf16[1,192,4096]{2,1,0:T(8,128)(2,1)} %param.15) | copy-start | bytes 4718596
  23.6 25.2 %copy-start.3 = (s32[32]{0:T(128)S(1)}, s32[32]{0:T(128)}, u32[]{:S(2)}) copy-start(s32[32]{0:T(128)} %param.19) | copy-start | bytes 388
  23.6 151.4 %all-to-all-start = ((bf16[64,10,2176]{2,1,0:T(8,128)(2,1)}), bf16[64,10,2176]{2,1,0:T(8,128)(2,1)}, u32[]{:S(2)}, u32[]{:S(2)}) async-start(bf16[64,10,2176]{2,1,0:T(8,128)(2,1)} %all_to_all.15), calls=%async_computation | async-start | bytes 8912896 | tf_op jit(solution)/shard_map/all_to_all | solution.py:171
  38.1 527.5 %collective-permute-start.2 = (bf16[1,192,4096]{2,1,0:T(8,128)(2,1)S(1)}, bf16[1,192,4096]{2,1,0:T(8,128)(2,1)}, u32[]{:S(2)}, u32[]{:S(2)}) collective-permute-start(bf16[1,192,4096]{2,1,0:T(8,128)(2,1)S(1)} %copy-done.1), channel_id=1, source_target_pairs={{0,128},{4,132},{8,136},{12,140},{16,144},{20,148},{24,152},{28,15... | collective-permute-start | bytes 4718600 | tf_op jit(solution)/shard_map/ppermute | solution.py:125
  43.4 526.7 %collective-permute-start.1 = (bf16[1,192,4096]{2,1,0:T(8,128)(2,1)S(1)}, bf16[1,192,4096]{2,1,0:T(8,128)(2,1)}, u32[]{:S(2)}, u32[]{:S(2)}) collective-permute-start(bf16[1,192,4096]{2,1,0:T(8,128)(2,1)S(1)} %copy-done), channel_id=1, source_target_pairs={{0,128},{4,132},{8,136},{12,140},{16,144},{20,148},{24,152},{28,15... | collective-permute-start | bytes 4718600 | tf_op jit(solution)/shard_map/ppermute | solution.py:125
  43.5 528.5 %collective-permute-start = (bf16[1,192,4096]{2,1,0:T(8,128)(2,1)}, bf16[1,192,4096]{2,1,0:T(8,128)(2,1)}, u32[]{:S(2)}, u32[]{:S(2)}) collective-permute-start(bf16[1,192,4096]{2,1,0:T(8,128)(2,1)} %param.16), channel_id=1, source_target_pairs={{0,128},{4,132},{8,136},{12,140},{16,144},{20,148},{24,152},{28,15... | collective-permute-start | bytes 4718600 | tf_op jit(solution)/shard_map/ppermute | solution.py:125
  564.3 5.8 slice-start
  565.6 4.6 slice-start.1
  565.6 6.5 slice-start.4
  570.1 2.0 slice-start.5
  570.1 2.0 copy-start.4
  575.7 1.6 copy-start.2
  750.6 30.4 %slice-start.2 = ((s8[5242880]{0:T(1024)(128)(4,1)}), s8[1048576]{0:T(1024)(128)(4,1)S(1)}, s32[]{:S(2)}) async-start(s8[5242880]{0:T(1024)(128)(4,1)} %bitcast.59), calls=%async_computation.4 | async-start | bytes 2097152
  750.6 73.1 %all-to-all-start.1 = ((bf16[64,10,1152]{2,1,0:T(8,128)(2,1)}), bf16[64,10,1152]{2,1,0:T(8,128)(2,1)}, u32[]{:S(2)}, u32[]{:S(2)}) async-start(bf16[64,10,1152]{2,1,0:T(8,128)(2,1)} %all_to_all.18), calls=%async_computation.1 | async-start | bytes 4718592 | tf_op jit(solution)/shard_map/all_to_all | solution.py:200
  775.8 5.2 slice-start.3
  775.8 7.7 slice-start.6
  781.0 2.6 slice-start.7

commit v6 on v5

--- a/solution.py
+++ b/solution.py
@@ -8,7 +8,7 @@
 MESH_IDS = pl.DeviceIdType.MESH
 
 
-def dp_scatter_kernel(groups, src_ref, score_ref, out_ref, landing, score_in, send_sem, recv_sem):
+def dp_scatter_kernel(groups, src_ref, score_ref, out_ref, score_out, landing, score_in, send_sem, recv_sem):
     me = lax.axis_index("dp")
     home = lax.axis_index("expert")
     width = landing.shape[2]
@@ -41,15 +41,16 @@
     def body(i, carry):
         rows = pl.ds(pl.multiple_of(i * block, block), block)
         total = src_ref[rows, pl.ds(own, width)].astype(jnp.float32)
-        score = score_ref[rows, :]
         for step in range(1, groups):
             total = total + landing[step, rows, :].astype(jnp.float32)
-            score = score + score_in[step, rows, :]
-        out_ref[rows, pl.ds(0, width)] = total.astype(out_ref.dtype)
-        out_ref[rows, pl.ds(width, 128)] = score.astype(out_ref.dtype)
+        out_ref[rows, :] = total.astype(out_ref.dtype)
         return carry
 
     lax.fori_loop(0, out_ref.shape[0] // block, body, 0)
+    score = score_ref[...]
+    for step in range(1, groups):
+        score = score + score_in[step]
+    score_out[...] = score
 
 
 def dp_scatter(partial, score, groups):
@@ -57,12 +58,15 @@
     width = full // groups
     return pl.pallas_call(
         lambda *refs: dp_scatter_kernel(groups, *refs),
-        out_shape=jax.ShapeDtypeStruct((rows, width + 128), partial.dtype),
+        out_shape=(
+            jax.ShapeDtypeStruct((rows, width), partial.dtype),
+            jax.ShapeDtypeStruct(score.shape, score.dtype),
+        ),
         in_specs=[pl.BlockSpec(memory_space=pltpu.VMEM)] * 2,
-        out_specs=pl.BlockSpec(memory_space=pltpu.VMEM),
+        out_specs=(pl.BlockSpec(memory_space=pltpu.VMEM), pl.BlockSpec(memory_space=pltpu.VMEM)),
         scratch_shapes=[
             pltpu.VMEM((groups, rows, width), partial.dtype),
-            pltpu.VMEM((groups, rows, 128), score.dtype),
+            pltpu.VMEM((groups,) + score.shape, score.dtype),
             pltpu.SemaphoreType.DMA((groups, 2)),
             pltpu.SemaphoreType.DMA((groups, 2)),
         ],
@@ -195,8 +199,13 @@
     )
     grad_wup = lax.dot_general(grad_up, x_rows, contract_rows, preferred_element_type=jnp.float32)
     grad_wdown = lax.dot_general(hidden, scaled, contract_rows, preferred_element_type=jnp.float32)
-    score_cols = jnp.zeros((capacity * expert_count, 128), jnp.float32).at[:, 0].set(score_part)
-    reduced = dp_scatter(input_part.astype(jnp.bfloat16), score_cols, groups)
+    slots = capacity * expert_count
+    score_tile = jnp.zeros((8 * 128,), jnp.float32).at[:slots].set(score_part).reshape(8, 128)
+    share, score_sum = dp_scatter(input_part.astype(jnp.bfloat16), score_tile, groups)
+    score_col = jnp.zeros((slots, 128), jnp.bfloat16).at[:, 0].set(
+        score_sum.reshape(-1)[:slots].astype(jnp.bfloat16)
+    )
+    reduced = jnp.concatenate([share, score_col], axis=1)
     back_rows = lax.all_to_all(reduced, "expert", split_axis=0, concat_axis=0, tiled=True)
     per_copy = back_rows[buffer_index].reshape(row_count, routed, quarter + 128)
     input_grad = jnp.sum(per_copy[:, :, :quarter].astype(jnp.float32), axis=1).astype(jnp.bfloat16)

time: 842 us -> 811 us (0.963)
  Pallas kernels: 549 us -> 528 us
  starting transfers between devices: 50.3 us -> 40.6 us
    pallas_call x1, Pallas kernels: 166 us -> 144 us  [dp_scatter(): pl.pallas_call(lambda *refs: dp_scatter_kernel(groups, *refs), out_shape=...]
    all_to_all x1, starting transfers between devices: 25.1 us -> 15.4 us  [shards(): lax.all_to_all(reduced, 'expert', split_axis=0, concat_axis=0, tiled=True)]
  transfers between devices with their start and end apart: 5 -> 5, of which waited for: 2 -> 2; matrix products, arithmetic and copies ran while one was open for 2% -> 2% of each run, Pallas kernels for 46% -> 48%
where the time goes in v6:
time: 811 us; the launch traced here: 802 us
  Pallas kernels  528 us (65%)
  waiting for transfers between devices  163 us (20%)
  starting transfers between devices  40.6 us (5%)
  local copies, waits for them, and re-layouts  34.1 us (4%)
  matrix products  25 us (3%)
  other arithmetic  9.5 us (1%)
    pallas_call x1, Pallas kernels, dp_gather(): pl.pallas_call(lambda *refs: dp_gather_kernel(groups, width, *refs), out_...  384 us
    pallas_call x1, Pallas kernels, dp_scatter(): pl.pallas_call(lambda *refs: dp_scatter_kernel(groups, *refs), out_shape=...  144 us
    all_to_all x1, waiting for transfers between devices, shards(): lax.all_to_all(outgoing, 'expert', split_axis=0, concat_axis=0, tiled=True)  125 us
    all_to_all x1, waiting for transfers between devices, shards(): lax.all_to_all(reduced, 'expert', split_axis=0, concat_axis=0, tiled=True)  37.7 us
  transfers between devices with their start and end apart: 5, of which 2 were waited for; matrix products, arithmetic and copies ran while one was open for 2% of the time, Pallas kernels for 48%

profile of v6, /device:TPU:35, one launch (start us, length us, event | category | flops | bytes accessed | tf_op | source)
XLA Modules:
  0.0 801.5 jit_solution(5931930670730584045)
XLA Ops:
  4.8 2.4 scatter_custom_fusion
  9.3 2.8 gather_fusion
  12.2 2.8 gather_fusion.1
  15.0 4.3 gather_fusion.2
  20.6 3.0 all_to_all.15
  23.6 14.5 %all-to-all-start = ((bf16[64,10,2176]{2,1,0:T(8,128)(2,1)}), bf16[64,10,2176]{2,1,0:T(8,128)(2,1)}, u32[]{:S(2)}, u32[]{:S(2)}) async-start(bf16[64,10,2176]{2,1,0:T(8,128)(2,1)} %all_to_all.15), calls=%async_computation | async-start | bytes 8912896 | tf_op jit(solution)/shard_map/all_to_all | solution.py:175
  38.1 5.3 collective-permute-start.2
  43.5 5.2 collective-permute-start
  50.0 125.0 %all-to-all-done = bf16[64,10,2176]{2,1,0:T(8,128)(2,1)} async-done(((bf16[64,10,2176]{2,1,0:T(8,128)(2,1)}), bf16[64,10,2176]{2,1,0:T(8,128)(2,1)}, u32[]{:S(2)}, u32[]{:S(2)}) %all-to-all-start) | async-done | bytes 2785312 | tf_op jit(solution)/shard_map/all_to_all | solution.py:175
  175.0 5.7 all_to_all.17.refs_0_
  180.7 383.6 %shard_map.119 = (bf16[640,4096]{1,0:T(8,128)(2,1)}, bf16[640,4096]{1,0:T(8,128)(2,1)}) custom-call(bf16[640,2176]{1,0:T(8,128)(2,1)} %all_to_all.17.refs_0_), custom_call_target="tpu_custom_call" | custom-call | tf_op jit(solution)/shard_map/pallas_call | solution.py:113
  565.6 4.5 fusion.15
  570.1 1.9 fusion.19
  572.1 2.7 multiply_reduce_fusion
  577.0 3.8 add_convert_fusion.refs_0_
  580.9 144.5 %shard_map.120 = (bf16[640,1024]{1,0:T(8,128)(2,1)}, f32[8,128]{1,0:T(8,128)}) custom-call(bf16[640,4096]{1,0:T(8,128)(2,1)} %add_convert_fusion.refs_0_, f32[8,128]{1,0:T(8,128)} %pad_bitcast_fusion.refs_1_), custom_call_target="tpu_custom_call" | custom-call | tf_op jit(solution)/shard_map/pallas_call | solution.py:59
  730.0 15.4 %all-to-all-start.1 = ((bf16[64,10,1152]{2,1,0:T(8,128)(2,1)}), bf16[64,10,1152]{2,1,0:T(8,128)(2,1)}, u32[]{:S(2)}, u32[]{:S(2)}) async-start(bf16[64,10,1152]{2,1,0:T(8,128)(2,1)} %all_to_all.18), calls=%async_computation.1 | async-start | bytes 4718592 | tf_op jit(solution)/shard_map/all_to_all | solution.py:209
  745.4 5.2 fusion.7
  750.6 2.5 fusion.6
  753.2 2.7 fusion.8
  755.9 37.7 %all-to-all-done.1 = bf16[64,10,1152]{2,1,0:T(8,128)(2,1)} async-done(((bf16[64,10,1152]{2,1,0:T(8,128)(2,1)}), bf16[64,10,1152]{2,1,0:T(8,128)(2,1)}, u32[]{:S(2)}, u32[]{:S(2)}) %all-to-all-start.1) | async-done | bytes 1474592 | tf_op jit(solution)/shard_map/all_to_all | solution.py:209
  793.5 2.7 all_to_all.20
  796.2 2.1 gather_fusion.3
  798.6 2.2 slice_reduce_fusion
  (77 shorter events, 17.3 us)
Async XLA Ops:
  23.6 14.5 %copy-start.1 = (bf16[1,192,4096]{2,1,0:T(8,128)(2,1)S(1)}, bf16[1,192,4096]{2,1,0:T(8,128)(2,1)}, u32[]{:S(2)}) copy-start(bf16[1,192,4096]{2,1,0:T(8,128)(2,1)} %param.16) | copy-start | bytes 4718596
  23.6 19.8 %copy-start = (bf16[1,192,4096]{2,1,0:T(8,128)(2,1)S(1)}, bf16[1,192,4096]{2,1,0:T(8,128)(2,1)}, u32[]{:S(2)}) copy-start(bf16[1,192,4096]{2,1,0:T(8,128)(2,1)} %param.17) | copy-start | bytes 4718596
  23.6 25.2 %copy-start.3 = (s32[32]{0:T(128)S(1)}, s32[32]{0:T(128)}, u32[]{:S(2)}) copy-start(s32[32]{0:T(128)} %param.21) | copy-start | bytes 388
  23.6 151.4 %all-to-all-start = ((bf16[64,10,2176]{2,1,0:T(8,128)(2,1)}), bf16[64,10,2176]{2,1,0:T(8,128)(2,1)}, u32[]{:S(2)}, u32[]{:S(2)}) async-start(bf16[64,10,2176]{2,1,0:T(8,128)(2,1)} %all_to_all.15), calls=%async_computation | async-start | bytes 8912896 | tf_op jit(solution)/shard_map/all_to_all | solution.py:175
  38.1 527.5 %collective-permute-start.2 = (bf16[1,192,4096]{2,1,0:T(8,128)(2,1)S(1)}, bf16[1,192,4096]{2,1,0:T(8,128)(2,1)}, u32[]{:S(2)}, u32[]{:S(2)}) collective-permute-start(bf16[1,192,4096]{2,1,0:T(8,128)(2,1)S(1)} %copy-done.1), channel_id=1, source_target_pairs={{0,128},{4,132},{8,136},{12,140},{16,144},{20,148},{24,152},{28,15... | collective-permute-start | bytes 4718600 | tf_op jit(solution)/shard_map/ppermute | solution.py:129
  43.4 526.7 %collective-permute-start.1 = (bf16[1,192,4096]{2,1,0:T(8,128)(2,1)S(1)}, bf16[1,192,4096]{2,1,0:T(8,128)(2,1)}, u32[]{:S(2)}, u32[]{:S(2)}) collective-permute-start(bf16[1,192,4096]{2,1,0:T(8,128)(2,1)S(1)} %copy-done), channel_id=1, source_target_pairs={{0,128},{4,132},{8,136},{12,140},{16,144},{20,148},{24,152},{28,15... | collective-permute-start | bytes 4718600 | tf_op jit(solution)/shard_map/ppermute | solution.py:129
  43.5 528.5 %collective-permute-start = (bf16[1,192,4096]{2,1,0:T(8,128)(2,1)}, bf16[1,192,4096]{2,1,0:T(8,128)(2,1)}, u32[]{:S(2)}, u32[]{:S(2)}) collective-permute-start(bf16[1,192,4096]{2,1,0:T(8,128)(2,1)} %param.18), channel_id=1, source_target_pairs={{0,128},{4,132},{8,136},{12,140},{16,144},{20,148},{24,152},{28,15... | collective-permute-start | bytes 4718600 | tf_op jit(solution)/shard_map/ppermute | solution.py:129
  564.3 5.8 slice-start
  565.5 4.6 slice-start.1
  565.6 6.5 slice-start.4
  570.1 2.0 slice-start.5
  570.1 2.0 copy-start.4
  575.4 1.6 copy-start.2
  730.0 20.6 %slice-start.2 = ((s8[5242880]{0:T(1024)(128)(4,1)}), s8[1048576]{0:T(1024)(128)(4,1)S(1)}, s32[]{:S(2)}) async-start(s8[5242880]{0:T(1024)(128)(4,1)} %bitcast.68), calls=%async_computation.4 | async-start | bytes 2097152
  730.0 63.5 %all-to-all-start.1 = ((bf16[64,10,1152]{2,1,0:T(8,128)(2,1)}), bf16[64,10,1152]{2,1,0:T(8,128)(2,1)}, u32[]{:S(2)}, u32[]{:S(2)}) async-start(bf16[64,10,1152]{2,1,0:T(8,128)(2,1)} %all_to_all.18), calls=%async_computation.1 | async-start | bytes 4718592 | tf_op jit(solution)/shard_map/all_to_all | solution.py:209
  745.4 5.2 slice-start.3
  745.4 7.8 slice-start.6
  750.6 2.6 slice-start.7
  750.6 2.6 copy-start.5

commit v7 on v6

--- a/solution.py
+++ b/solution.py
@@ -145,13 +145,7 @@
     quarter = model_width // groups
     own_flag = pair_lookup(jnp.reshape(my_slot, (1,)), swap_flags, half_axis)[0]
     flat_ids = expert_ids.reshape(-1)
-    weights = (gate_weight, up_weight, down_weight)
-    arrived = from_behind((gate_weight, up_weight, down_weight), "expert", half_axis)
-    weights = tuple(
-        (jnp.where(own_flag == 1, fresh, stay) for fresh, stay in zip(arrived, weights))
-    )
-    flipped = pair_lookup(flat_ids, swap_flags, half_axis)
-    target = jnp.where(flipped == 1, (flat_ids + half_axis) % expert_count, flat_ids)
+    target = flat_ids
     copies = row_count * routed
     onehot = (target[:, None] == jnp.arange(expert_count, dtype=jnp.int32)[None, :]).astype(
         jnp.int32
@@ -175,9 +169,9 @@
     arrived = lax.all_to_all(outgoing, "expert", split_axis=0, concat_axis=0, tiled=True)
     x_rows, dy_rows = dp_gather(arrived, groups, quarter)
     gate_rows = arrived[:, 2 * quarter]
-    w_gate = weights[0][0]
-    w_up = weights[1][0]
-    w_down = weights[2][0]
+    w_gate = gate_weight[0]
+    w_up = up_weight[0]
+    w_down = down_weight[0]
     contract_last = (((1,), (1,)), ((), ()))
     pre_gate = lax.dot_general(x_rows, w_gate, contract_last, preferred_element_type=jnp.float32)
     pre_up = lax.dot_general(x_rows, w_up, contract_last, preferred_element_type=jnp.float32)
@@ -199,6 +193,15 @@
     )
     grad_wup = lax.dot_general(grad_up, x_rows, contract_rows, preferred_element_type=jnp.float32)
     grad_wdown = lax.dot_general(hidden, scaled, contract_rows, preferred_element_type=jnp.float32)
+    local_grads = (
+        grad_wgate.astype(jnp.bfloat16)[None],
+        grad_wup.astype(jnp.bfloat16)[None],
+        grad_wdown.astype(jnp.bfloat16)[None],
+    )
+    local_grads, input_part, score_part = lax.optimization_barrier(
+        (local_grads, input_part, score_part)
+    )
+    arrived = from_behind(local_grads, "expert", half_axis)
     slots = capacity * expert_count
     score_tile = jnp.zeros((8 * 128,), jnp.float32).at[:slots].set(score_part).reshape(8, 128)
     share, score_sum = dp_scatter(input_part.astype(jnp.bfloat16), score_tile, groups)
@@ -210,10 +213,8 @@
     per_copy = back_rows[buffer_index].reshape(row_count, routed, quarter + 128)
     input_grad = jnp.sum(per_copy[:, :, :quarter].astype(jnp.float32), axis=1).astype(jnp.bfloat16)
     gate_grad = per_copy[:, :, quarter]
-    gradients = (
-        grad_wgate.astype(jnp.bfloat16)[None],
-        grad_wup.astype(jnp.bfloat16)[None],
-        grad_wdown.astype(jnp.bfloat16)[None],
+    gradients = tuple(
+        jnp.where(own_flag == 1, fresh, stay) for fresh, stay in zip(arrived, local_grads)
     )
     return (input_grad, gate_grad, gradients[0], gradients[1], gradients[2])
 

time: 811 us -> 881 us (1.086)
  blocking collectives: 0 us -> 119 us
  waiting for transfers between devices: 163 us -> 53.8 us
  Pallas kernels: 528 us -> 600 us
  starting transfers between devices: 40.6 us -> 18.9 us
  other arithmetic: 9.5 us -> 20.4 us
    pallas_call x1, Pallas kernels: 144 us -> 306 us  [dp_scatter(): pl.pallas_call(lambda *refs: dp_scatter_kernel(groups, *refs), out_shape=...]
    all_to_all x1 -> x0, waiting for transfers between devices: 125 us -> none  [shards(): lax.all_to_all(outgoing, 'expert', split_axis=0, concat_axis=0, tiled=True)]
    all_to_all x0 -> x1, blocking collectives: none -> 119 us  [shards(): lax.all_to_all(outgoing, 'expert', split_axis=0, concat_axis=0, tiled=True)]
    pallas_call x1, Pallas kernels: 384 us -> 294 us  [dp_gather(): pl.pallas_call(lambda *refs: dp_gather_kernel(groups, width, *refs), out_...]
    ppermute x3, waiting for transfers between devices: 0.01 us -> 53.8 us  [from_behind(): lax.ppermute(value, axis, [(i, (i + by) % devices) for i in range(devices)])]
    all_to_all x1, waiting for transfers between devices: 37.7 us -> 0.01 us  [shards(): lax.all_to_all(reduced, 'expert', split_axis=0, concat_axis=0, tiled=True)]
    all_to_all x1 -> x0, starting transfers between devices: 14.5 us -> none  [shards(): lax.all_to_all(outgoing, 'expert', split_axis=0, concat_axis=0, tiled=True)]
  transfers between devices with their start and end apart: 5 -> 4, of which waited for: 2 -> 1; matrix products, arithmetic and copies ran while one was open for 2% -> 1% of each run, Pallas kernels for 48% -> 35%
where the time goes in v7:
time: 881 us; the launch traced here: 875 us
  Pallas kernels  600 us (68%)
  blocking collectives  119 us (14%)
  waiting for transfers between devices  53.8 us (6%)
  local copies, waits for them, and re-layouts  42.7 us (5%)
  other arithmetic  20.4 us (2%)
  matrix products  19.4 us (2%)
  starting transfers between devices  18.9 us (2%)
    pallas_call x1, Pallas kernels, dp_scatter(): pl.pallas_call(lambda *refs: dp_scatter_kernel(groups, *refs), out_shape=...  306 us
    pallas_call x1, Pallas kernels, dp_gather(): pl.pallas_call(lambda *refs: dp_gather_kernel(groups, width, *refs), out_...  294 us
    all_to_all x1, blocking collectives, shards(): lax.all_to_all(outgoing, 'expert', split_axis=0, concat_axis=0, tiled=True)  119 us
    ppermute x3, waiting for transfers between devices, from_behind(): lax.ppermute(value, axis, [(i, (i + by) % devices) for i in range(devices)])  53.8 us
  transfers between devices with their start and end apart: 4, of which 1 were waited for; matrix products, arithmetic and copies ran while one was open for 1% of the time, Pallas kernels for 35%

profile of v7, /device:TPU:35, one launch (start us, length us, event | category | flops | bytes accessed | tf_op | source)
XLA Modules:
  0.0 875.4 jit_solution(759987657140966117)
XLA Ops:
  5.9 2.4 scatter_custom_fusion
  8.4 4.3 gather_fusion.2
  15.2 2.8 gather_fusion
  18.1 3.5 gather_fusion.1
  24.9 5.4 all_to_all.15
  30.4 118.9 %all_to_all.23 = bf16[64,10,2176]{2,1,0:T(8,128)(2,1)} all-to-all(bf16[64,10,2176]{2,1,0:T(8,128)(2,1)} %all_to_all.15), channel_id=1, replica_groups=mesh['expert'=64,'dp'=4] {'expert'}, dimensions={0} | all-to-all | bytes 5570560 | tf_op jit(solution)/shard_map/all_to_all | solution.py:169
  149.2 5.6 all_to_all.17.refs_0_
  154.9 293.8 %shard_map.119 = (bf16[640,4096]{1,0:T(8,128)(2,1)}, bf16[640,4096]{1,0:T(8,128)(2,1)}) custom-call(bf16[640,2176]{1,0:T(8,128)(2,1)} %all_to_all.17.refs_0_), custom_call_target="tpu_custom_call" | custom-call | tf_op jit(solution)/shard_map/pallas_call | solution.py:113
  449.8 4.5 fusion.19
  462.8 2.6 fusion.8
  465.5 3.9 convolution_add_fusion.refs_0_
  470.7 5.7 collective-permute-start.1
  477.0 305.8 %shard_map.120 = (bf16[640,1024]{1,0:T(8,128)(2,1)}, f32[8,128]{1,0:T(8,128)}) custom-call(bf16[640,4096]{1,0:T(8,128)(2,1)} %convolution_add_fusion.refs_0_, f32[8,128]{1,0:T(8,128)} %pad_bitcast_fusion.refs_1_), custom_call_target="tpu_custom_call" | custom-call | tf_op jit(solution)/shard_map/pallas_call | solution.py:59
  784.4 2.6 fusion.23
  786.9 3.7 all_to_all.18
  790.6 8.0 all-to-all-start.1
  798.6 5.3 collective-permute-start.2
  803.9 2.7 broadcast_select_fusion.2
  806.6 2.8 broadcast_select_fusion.1
  809.4 53.8 %collective-permute-done.2 = bf16[1,192,4096]{2,1,0:T(8,128)(2,1)S(1)} collective-permute-done((bf16[1,192,4096]{2,1,0:T(8,128)(2,1)}, bf16[1,192,4096]{2,1,0:T(8,128)(2,1)S(1)}, u32[]{:S(2)}, u32[]{:S(2)}) %collective-permute-start.2) | collective-permute-done | bytes 1572896 | tf_op jit(solution)/shard_map/ppermute | solution.py:129
  864.5 2.7 all_to_all.20
  867.2 2.8 gather_fusion.3
  870.1 2.5 reshape.171
  872.5 2.2 slice_reduce_fusion
  (68 shorter events, 25.4 us)
Async XLA Ops:
  0.6 453.7 %copy-start = (bf16[1,192,4096]{2,1,0:T(8,128)(2,1)S(1)}, bf16[1,192,4096]{2,1,0:T(8,128)(2,1)}, u32[]{:S(2)}) copy-start(bf16[1,192,4096]{2,1,0:T(8,128)(2,1)} %param.16) | copy-start | bytes 4718596
  21.6 1.6 copy-start.6
  154.9 294.9 %copy-start.3 = (bf16[1,192,4096]{2,1,0:T(8,128)(2,1)S(1)}, bf16[1,192,4096]{2,1,0:T(8,128)(2,1)}, u32[]{:S(2)}) copy-start(bf16[1,192,4096]{2,1,0:T(8,128)(2,1)} %param.17) | copy-start | bytes 4718596
  449.8 4.5 copy-start.2
  449.8 6.5 slice-start
  454.3 2.0 slice-start.1
  454.3 2.0 copy-start.7
  462.8 2.7 copy-start.4
  465.5 3.9 copy-start.8
  469.4 334.5 %collective-permute-start = (bf16[1,192,4096]{2,1,0:T(8,128)(2,1)S(1)}, bf16[1,192,4096]{2,1,0:T(8,128)(2,1)}, u32[]{:S(2)}, u32[]{:S(2)}) collective-permute-start(bf16[1,192,4096]{2,1,0:T(8,128)(2,1)S(1)} %fusion.6), channel_id=1, source_target_pairs={{0,128},{4,132},{8,136},{12,140},{16,144},{20,148},{24,152},{28,15... | collective-permute-start | bytes 4718600 | tf_op jit(solution)/shard_map/ppermute | solution.py:129
  470.7 335.9 %collective-permute-start.1 = (bf16[1,192,4096]{2,1,0:T(8,128)(2,1)S(1)}, bf16[1,192,4096]{2,1,0:T(8,128)(2,1)}, u32[]{:S(2)}, u32[]{:S(2)}) collective-permute-start(bf16[1,192,4096]{2,1,0:T(8,128)(2,1)S(1)} %fusion.7), channel_id=1, source_target_pairs={{0,128},{4,132},{8,136},{12,140},{16,144},{20,148},{24,152},{28,15... | collective-permute-start | bytes 4718600 | tf_op jit(solution)/shard_map/ppermute | solution.py:129
  790.6 74.0 %all-to-all-start.1 = ((bf16[64,10,1152]{2,1,0:T(8,128)(2,1)}), bf16[64,10,1152]{2,1,0:T(8,128)(2,1)}, u32[]{:S(2)}, u32[]{:S(2)}) async-start(bf16[64,10,1152]{2,1,0:T(8,128)(2,1)} %all_to_all.18), calls=%async_computation.1 | async-start | bytes 4718592 | tf_op jit(solution)/shard_map/all_to_all | solution.py:212
  798.6 64.7 %collective-permute-start.2 = (bf16[1,192,4096]{2,1,0:T(8,128)(2,1)}, bf16[1,192,4096]{2,1,0:T(8,128)(2,1)S(1)}, u32[]{:S(2)}, u32[]{:S(2)}) collective-permute-start(bf16[1,192,4096]{2,1,0:T(8,128)(2,1)} %fusion.8), channel_id=1, source_target_pairs={{0,128},{4,132},{8,136},{12,140},{16,144},{20,148},{24,152},{28,15... | collective-permute-start | bytes 4718600 | tf_op jit(solution)/shard_map/ppermute | solution.py:129
  806.6 56.7 %copy-start.5 = (bf16[1,192,4096]{2,1,0:T(8,128)(2,1)S(1)}, bf16[1,192,4096]{2,1,0:T(8,128)(2,1)}, u32[]{:S(2)}) copy-start(bf16[1,192,4096]{2,1,0:T(8,128)(2,1)} %fusion.8) | copy-start | bytes 4718596
  867.2 8.2 copy-start.1

commit v8 on v6

--- a/solution.py
+++ b/solution.py
@@ -74,29 +74,27 @@
     )(partial, score)
 
 
-def dp_gather_kernel(groups, width, src_ref, x_ref, dy_ref, local_sem, send_sem, recv_sem):
+def pair_swap_kernel(width, src_ref, x_ref, dy_ref, local_sem, send_sem, recv_sem):
     me = lax.axis_index("dp")
     home = lax.axis_index("expert")
+    side = lax.rem(me, 2)
+    partner = me + 1 - 2 * side
     barrier = pltpu.get_barrier_semaphore()
-    for step in range(1, groups):
-        peer = lax.rem(me + step, groups)
-        pl.semaphore_signal(barrier, 1, device_id=(home, peer), device_id_type=MESH_IDS)
-    pl.semaphore_wait(barrier, groups - 1)
-    mine = pl.ds(pl.multiple_of(me * width, 128), width)
+    pl.semaphore_signal(barrier, 1, device_id=(home, partner), device_id_type=MESH_IDS)
+    pl.semaphore_wait(barrier, 1)
+    mine = pl.ds(pl.multiple_of(side * width, 128), width)
     copies = []
-    for step in range(1, groups):
-        peer = lax.rem(me + step, groups)
-        for part, dst in enumerate((x_ref, dy_ref)):
-            copy = pltpu.make_async_remote_copy(
-                src_ref=src_ref.at[:, pl.ds(part * width, width)],
-                dst_ref=dst.at[:, mine],
-                send_sem=send_sem.at[step, part],
-                recv_sem=recv_sem.at[step, part],
-                device_id=(home, peer),
-                device_id_type=MESH_IDS,
-            )
-            copy.start()
-            copies.append(copy)
+    for part, dst in enumerate((x_ref, dy_ref)):
+        copy = pltpu.make_async_remote_copy(
+            src_ref=src_ref.at[:, pl.ds(part * width, width)],
+            dst_ref=dst.at[:, mine],
+            send_sem=send_sem.at[part],
+            recv_sem=recv_sem.at[part],
+            device_id=(home, partner),
+            device_id_type=MESH_IDS,
+        )
+        copy.start()
+        copies.append(copy)
     for part, dst in enumerate((x_ref, dy_ref)):
         local = pltpu.make_async_copy(
             src_ref.at[:, pl.ds(part * width, width)], dst.at[:, mine], local_sem.at[part]
@@ -107,18 +105,18 @@
         copy.wait()
 
 
-def dp_gather(chunk, groups, width):
+def pair_swap(chunk, width):
     rows = chunk.shape[0]
-    full = jax.ShapeDtypeStruct((rows, groups * width), chunk.dtype)
+    full = jax.ShapeDtypeStruct((rows, 2 * width), chunk.dtype)
     return pl.pallas_call(
-        lambda *refs: dp_gather_kernel(groups, width, *refs),
+        lambda *refs: pair_swap_kernel(width, *refs),
         out_shape=(full, full),
         in_specs=[pl.BlockSpec(memory_space=pl.ANY)],
         out_specs=(pl.BlockSpec(memory_space=pl.ANY), pl.BlockSpec(memory_space=pl.ANY)),
         scratch_shapes=[
             pltpu.SemaphoreType.DMA((2,)),
-            pltpu.SemaphoreType.DMA((groups, 2)),
-            pltpu.SemaphoreType.DMA((groups, 2)),
+            pltpu.SemaphoreType.DMA((2,)),
+            pltpu.SemaphoreType.DMA((2,)),
         ],
         compiler_params=pltpu.CompilerParams(collective_id=2, has_side_effects=True),
     )(chunk)
@@ -164,17 +162,18 @@
     filled = source > 0
     copy_index = jnp.maximum(source - 1, 0)
     token_index = copy_index // routed
-    my_group = lax.axis_index("dp")
-    x_part = lax.dynamic_slice_in_dim(tokens, my_group * quarter, quarter, axis=1)
-    dy_part = lax.dynamic_slice_in_dim(cotangent, my_group * quarter, quarter, axis=1)
+    half = model_width // 2
+    my_side = lax.rem(lax.axis_index("dp"), 2)
+    x_part = lax.dynamic_slice_in_dim(tokens, my_side * half, half, axis=1)
+    dy_part = lax.dynamic_slice_in_dim(cotangent, my_side * half, half, axis=1)
     x_buffer = jnp.where(filled[:, None], x_part[token_index], 0)
     dy_buffer = jnp.where(filled[:, None], dy_part[token_index], 0)
     gate_buffer = jnp.where(filled, gates.reshape(-1)[copy_index], 0)
     gate_cols = jnp.zeros((expert_count * capacity, 128), jnp.bfloat16).at[:, 0].set(gate_buffer)
     outgoing = jnp.concatenate([x_buffer, dy_buffer, gate_cols], axis=1)
     arrived = lax.all_to_all(outgoing, "expert", split_axis=0, concat_axis=0, tiled=True)
-    x_rows, dy_rows = dp_gather(arrived, groups, quarter)
-    gate_rows = arrived[:, 2 * quarter]
+    x_rows, dy_rows = pair_swap(arrived, half)
+    gate_rows = arrived[:, 2 * half]
     w_gate = weights[0][0]
     w_up = weights[1][0]
     w_down = weights[2][0]

time: 811 us -> 835 us (1.030)
  Pallas kernels: 528 us -> 394 us
  waiting for transfers between devices: 163 us -> 247 us
  starting transfers between devices: 40.6 us -> 99.2 us
  local copies, waits for them, and re-layouts: 34.1 us -> 44.4 us
    pallas_call x1, Pallas kernels: 384 us -> 275 us  [pair_swap(): pl.pallas_call(lambda *refs: pair_swap_kernel(width, *refs), out_shape=(f...]
    all_to_all x1, waiting for transfers between devices: 125 us -> 210 us  [shards(): lax.all_to_all(outgoing, 'expert', split_axis=0, concat_axis=0, tiled=True)]
    all_to_all x1, starting transfers between devices: 15.4 us -> 74.1 us  [shards(): lax.all_to_all(reduced, 'expert', split_axis=0, concat_axis=0, tiled=True)]
    pallas_call x1, Pallas kernels: 144 us -> 119 us  [dp_scatter(): pl.pallas_call(lambda *refs: dp_scatter_kernel(groups, *refs), out_shape=...]
    all_to_all x2, local copies, waits for them, and re-layouts: 8.61 us -> 17 us  [shards(): lax.all_to_all(outgoing, 'expert', split_axis=0, concat_axis=0, tiled=True)]
  transfers between devices with their start and end apart: 5 -> 5, of which waited for: 2 -> 2; matrix products, arithmetic and copies ran while one was open for 2% -> 2% of each run, Pallas kernels for 48% -> 33%
where the time goes in v8:
time: 835 us; the launch traced here: 825 us
  Pallas kernels  394 us (47%)
  waiting for transfers between devices  247 us (30%)
  starting transfers between devices  99.2 us (12%)
  local copies, waits for them, and re-layouts  44.4 us (5%)
  matrix products  25 us (3%)
  other arithmetic  14 us (2%)
    pallas_call x1, Pallas kernels, pair_swap(): pl.pallas_call(lambda *refs: pair_swap_kernel(width, *refs), out_shape=(f...  275 us
    all_to_all x1, waiting for transfers between devices, shards(): lax.all_to_all(outgoing, 'expert', split_axis=0, concat_axis=0, tiled=True)  210 us
    pallas_call x1, Pallas kernels, dp_scatter(): pl.pallas_call(lambda *refs: dp_scatter_kernel(groups, *refs), out_shape=...  119 us
    all_to_all x1, starting transfers between devices, shards(): lax.all_to_all(reduced, 'expert', split_axis=0, concat_axis=0, tiled=True)  74.1 us
    all_to_all x1, waiting for transfers between devices, shards(): lax.all_to_all(reduced, 'expert', split_axis=0, concat_axis=0, tiled=True)  37.2 us
    all_to_all x2, local copies, waits for them, and re-layouts, shards(): lax.all_to_all(outgoing, 'expert', split_axis=0, concat_axis=0, tiled=True)  17 us
  transfers between devices with their start and end apart: 5, of which 2 were waited for; matrix products, arithmetic and copies ran while one was open for 2% of the time, Pallas kernels for 33%

profile of v8, /device:TPU:35, one launch (start us, length us, event | category | flops | bytes accessed | tf_op | source)
XLA Modules:
  0.0 824.7 jit_solution(7687723000878232076)
XLA Ops:
  4.8 2.4 scatter_custom_fusion
  8.6 4.1 gather_fusion
  12.7 4.1 gather_fusion.1
  17.0 4.3 gather_fusion.2
  22.1 2.2 broadcast_select_fusion.1
  24.3 2.8 fusion.1
  27.1 8.3 %all_to_all.15 = bf16[64,10,4224]{2,1,0:T(8,128)(2,1)} reshape(bf16[640,4224]{1,0:T(8,128)(2,1)} %fusion.1) | data formatting | bytes 10813440 | tf_op jit(solution)/shard_map/all_to_all | solution.py:174
  35.4 14.5 %all-to-all-start = ((bf16[64,10,4224]{2,1,0:T(8,128)(2,1)}), bf16[64,10,4224]{2,1,0:T(8,128)(2,1)}, u32[]{:S(2)}, u32[]{:S(2)}) async-start(bf16[64,10,4224]{2,1,0:T(8,128)(2,1)} %all_to_all.15), calls=%async_computation | async-start | bytes 17301504 | tf_op jit(solution)/shard_map/all_to_all | solution.py:174
  49.9 5.3 collective-permute-start.2
  55.4 5.2 collective-permute-start
  61.9 209.7 %all-to-all-done = bf16[64,10,4224]{2,1,0:T(8,128)(2,1)} async-done(((bf16[64,10,4224]{2,1,0:T(8,128)(2,1)}), bf16[64,10,4224]{2,1,0:T(8,128)(2,1)}, u32[]{:S(2)}, u32[]{:S(2)}) %all-to-all-start) | async-done | bytes 5406752 | tf_op jit(solution)/shard_map/all_to_all | solution.py:174
  271.5 8.7 %all_to_all.17.refs_0_ = bf16[640,4224]{1,0:T(8,128)(2,1)} reshape(bf16[64,10,4224]{2,1,0:T(8,128)(2,1)} %all-to-all-done) | data formatting | bytes 10813440 | tf_op jit(solution)/shard_map/all_to_all | solution.py:174
  280.2 274.7 %shard_map.119 = (bf16[640,4096]{1,0:T(8,128)(2,1)}, bf16[640,4096]{1,0:T(8,128)(2,1)}) custom-call(bf16[640,4224]{1,0:T(8,128)(2,1)} %all_to_all.17.refs_0_), custom_call_target="tpu_custom_call" | custom-call | tf_op jit(solution)/shard_map/pallas_call | solution.py:111
  556.2 4.5 fusion.15
  562.8 2.7 multiply_reduce_fusion
  567.7 3.8 add_convert_fusion.refs_0_
  571.5 118.8 %shard_map.120 = (bf16[640,1024]{1,0:T(8,128)(2,1)}, f32[8,128]{1,0:T(8,128)}) custom-call(bf16[640,4096]{1,0:T(8,128)(2,1)} %add_convert_fusion.refs_0_, f32[8,128]{1,0:T(8,128)} %pad_bitcast_fusion.refs_1_), custom_call_target="tpu_custom_call" | custom-call | tf_op jit(solution)/shard_map/pallas_call | solution.py:59
  695.0 74.1 %all-to-all-start.1 = ((bf16[64,10,1152]{2,1,0:T(8,128)(2,1)}), bf16[64,10,1152]{2,1,0:T(8,128)(2,1)}, u32[]{:S(2)}, u32[]{:S(2)}) async-start(bf16[64,10,1152]{2,1,0:T(8,128)(2,1)} %all_to_all.18), calls=%async_computation.1 | async-start | bytes 4718592 | tf_op jit(solution)/shard_map/all_to_all | solution.py:208
  769.1 5.2 fusion.8
  774.3 2.5 fusion.7
  776.8 2.7 fusion.9
  779.5 37.2 %all-to-all-done.1 = bf16[64,10,1152]{2,1,0:T(8,128)(2,1)} async-done(((bf16[64,10,1152]{2,1,0:T(8,128)(2,1)}), bf16[64,10,1152]{2,1,0:T(8,128)(2,1)}, u32[]{:S(2)}, u32[]{:S(2)}) %all-to-all-start.1) | async-done | bytes 1474592 | tf_op jit(solution)/shard_map/all_to_all | solution.py:208
  816.7 2.7 all_to_all.20
  821.8 2.2 slice_reduce_fusion
  (81 shorter events, 20.5 us)
Async XLA Ops:
  12.7 4.1 copy-start.4
  12.7 9.4 %copy-start = (bf16[640,2048]{1,0:T(8,128)(2,1)S(1)}, bf16[640,2048]{1,0:T(8,128)(2,1)}, u32[]{:S(2)}) copy-start(bf16[640,2048]{1,0:T(8,128)(2,1)} %gather_fusion) | copy-start | bytes 7864324
  35.4 14.5 %copy-start.2 = (bf16[1,192,4096]{2,1,0:T(8,128)(2,1)S(1)}, bf16[1,192,4096]{2,1,0:T(8,128)(2,1)}, u32[]{:S(2)}) copy-start(bf16[1,192,4096]{2,1,0:T(8,128)(2,1)} %param.16) | copy-start | bytes 4718596
  35.4 19.8 %copy-start.1 = (bf16[1,192,4096]{2,1,0:T(8,128)(2,1)S(1)}, bf16[1,192,4096]{2,1,0:T(8,128)(2,1)}, u32[]{:S(2)}) copy-start(bf16[1,192,4096]{2,1,0:T(8,128)(2,1)} %param.17) | copy-start | bytes 4718596
  35.4 25.2 %copy-start.5 = (s32[32]{0:T(128)S(1)}, s32[32]{0:T(128)}, u32[]{:S(2)}) copy-start(s32[32]{0:T(128)} %param.21) | copy-start | bytes 388
  35.4 236.1 %all-to-all-start = ((bf16[64,10,4224]{2,1,0:T(8,128)(2,1)}), bf16[64,10,4224]{2,1,0:T(8,128)(2,1)}, u32[]{:S(2)}, u32[]{:S(2)}) async-start(bf16[64,10,4224]{2,1,0:T(8,128)(2,1)} %all_to_all.15), calls=%async_computation | async-start | bytes 17301504 | tf_op jit(solution)/shard_map/all_to_all | solution.py:174
  49.9 506.3 %collective-permute-start.2 = (bf16[1,192,4096]{2,1,0:T(8,128)(2,1)S(1)}, bf16[1,192,4096]{2,1,0:T(8,128)(2,1)}, u32[]{:S(2)}, u32[]{:S(2)}) collective-permute-start(bf16[1,192,4096]{2,1,0:T(8,128)(2,1)S(1)} %copy-done.2), channel_id=1, source_target_pairs={{0,128},{4,132},{8,136},{12,140},{16,144},{20,148},{24,152},{28,15... | collective-permute-start | bytes 4718600 | tf_op jit(solution)/shard_map/ppermute | solution.py:127
  55.2 505.6 %collective-permute-start.1 = (bf16[1,192,4096]{2,1,0:T(8,128)(2,1)S(1)}, bf16[1,192,4096]{2,1,0:T(8,128)(2,1)}, u32[]{:S(2)}, u32[]{:S(2)}) collective-permute-start(bf16[1,192,4096]{2,1,0:T(8,128)(2,1)S(1)} %copy-done.1), channel_id=1, source_target_pairs={{0,128},{4,132},{8,136},{12,140},{16,144},{20,148},{24,152},{28,15... | collective-permute-start | bytes 4718600 | tf_op jit(solution)/shard_map/ppermute | solution.py:127
  55.4 507.4 %collective-permute-start = (bf16[1,192,4096]{2,1,0:T(8,128)(2,1)}, bf16[1,192,4096]{2,1,0:T(8,128)(2,1)}, u32[]{:S(2)}, u32[]{:S(2)}) collective-permute-start(bf16[1,192,4096]{2,1,0:T(8,128)(2,1)} %param.18), channel_id=1, source_target_pairs={{0,128},{4,132},{8,136},{12,140},{16,144},{20,148},{24,152},{28,15... | collective-permute-start | bytes 4718600 | tf_op jit(solution)/shard_map/ppermute | solution.py:127
  555.0 5.8 slice-start
  556.2 4.6 slice-start.1
  556.2 6.5 slice-start.4
  560.7 2.0 slice-start.5
  560.7 2.0 copy-start.6
  566.1 1.6 copy-start.3
  695.0 79.3 %slice-start.2 = ((s8[5242880]{0:T(1024)(128)(4,1)}), s8[1048576]{0:T(1024)(128)(4,1)S(1)}, s32[]{:S(2)}) async-start(s8[5242880]{0:T(1024)(128)(4,1)} %bitcast.68), calls=%async_computation.4 | async-start | bytes 2097152
  695.0 121.7 %all-to-all-start.1 = ((bf16[64,10,1152]{2,1,0:T(8,128)(2,1)}), bf16[64,10,1152]{2,1,0:T(8,128)(2,1)}, u32[]{:S(2)}, u32[]{:S(2)}) async-start(bf16[64,10,1152]{2,1,0:T(8,128)(2,1)} %all_to_all.18), calls=%async_computation.1 | async-start | bytes 4718592 | tf_op jit(solution)/shard_map/all_to_all | solution.py:208
  769.1 5.2 slice-start.3
  769.1 7.8 slice-start.6
  774.3 2.6 slice-start.7
  774.3 2.6 copy-start.7

commit v9 on v6

--- a/solution.py
+++ b/solution.py
@@ -129,6 +129,29 @@
     return lax.ppermute(value, axis, [(i, (i + by) % devices) for i in range(devices)])
 
 
+def z_shift(value, expert_count, groups, delta):
+    half_axis = expert_count // 2
+    ring = 2 * groups
+    pairs = []
+    for slot in range(expert_count):
+        for group in range(groups):
+            z = (slot // half_axis) * groups + group
+            moved = (z + delta) % ring
+            target = (moved // groups) * half_axis + slot % half_axis
+            pairs.append((slot * groups + group, target * groups + moved % groups))
+    return lax.ppermute(value, ("expert", "dp"), pairs)
+
+
+def across_z(value, expert_count, groups):
+    split = value.shape[1] // 2
+    ahead = value[:, :split]
+    behind = value[:, split:]
+    for _ in range(2):
+        ahead = z_shift(ahead, expert_count, groups, 2)
+        behind = z_shift(behind, expert_count, groups, -2)
+    return jnp.concatenate([ahead, behind], axis=1)
+
+
 def pair_lookup(experts, pair_flags, half_axis):
     match = experts[:, None] % half_axis == jnp.arange(half_axis, dtype=jnp.int32)[None, :]
     return jnp.sum(jnp.where(match, pair_flags[None, :], 0), axis=1)
@@ -146,7 +169,9 @@
     own_flag = pair_lookup(jnp.reshape(my_slot, (1,)), swap_flags, half_axis)[0]
     flat_ids = expert_ids.reshape(-1)
     weights = (gate_weight, up_weight, down_weight)
-    arrived = from_behind((gate_weight, up_weight, down_weight), "expert", half_axis)
+    arrived = tuple(
+        across_z(w, expert_count, groups) for w in (gate_weight, up_weight, down_weight)
+    )
     weights = tuple(
         (jnp.where(own_flag == 1, fresh, stay) for fresh, stay in zip(arrived, weights))
     )

time: 811 us -> 821 us (1.012); the launches traced: 802 us -> 820 us
  Pallas kernels: 528 us -> 428 us
  waiting for transfers between devices: 163 us -> 255 us
  starting transfers between devices: 40.6 us -> 60.5 us
    ppermute x3 -> x12, waiting for transfers between devices: 0.01 us -> 205 us  [z_shift(): return lax.ppermute(value, ('expert', 'dp'), pairs)]
    all_to_all x1, waiting for transfers between devices: 125 us -> 0.01 us  [shards(): lax.all_to_all(outgoing, 'expert', split_axis=0, concat_axis=0, tiled=True)]
    pallas_call x1, Pallas kernels: 384 us -> 285 us  [dp_gather(): pl.pallas_call(lambda *refs: dp_gather_kernel(groups, width, *refs), out_...]
    all_to_all x1, waiting for transfers between devices: 37.7 us -> 50 us  [shards(): lax.all_to_all(reduced, 'expert', split_axis=0, concat_axis=0, tiled=True)]
    ppermute x3 -> x12, starting transfers between devices: 10.7 us -> 21 us  [z_shift(): return lax.ppermute(value, ('expert', 'dp'), pairs)]
    all_to_all x1, starting transfers between devices: 15.4 us -> 25.1 us  [shards(): lax.all_to_all(reduced, 'expert', split_axis=0, concat_axis=0, tiled=True)]
  transfers between devices with their start and end apart: 5 -> 14, of which waited for: 2 -> 7; matrix products, arithmetic and copies ran while one was open for 2% -> 3% of each run, Pallas kernels for 48% -> 35%
where the time goes in v9:
time: 821 us; the launch traced here: 820 us
  Pallas kernels  428 us (52%)
  waiting for transfers between devices  255 us (31%)
  starting transfers between devices  60.5 us (7%)
  local copies, waits for them, and re-layouts  36.3 us (4%)
  matrix products  29.7 us (4%)
  other arithmetic  9.51 us (1%)
    pallas_call x1, Pallas kernels, dp_gather(): pl.pallas_call(lambda *refs: dp_gather_kernel(groups, width, *refs), out_...  285 us
    ppermute x12, waiting for transfers between devices, z_shift(): return lax.ppermute(value, ('expert', 'dp'), pairs)  205 us
    pallas_call x1, Pallas kernels, dp_scatter(): pl.pallas_call(lambda *refs: dp_scatter_kernel(groups, *refs), out_shape=...  143 us
    all_to_all x1, waiting for transfers between devices, shards(): lax.all_to_all(reduced, 'expert', split_axis=0, concat_axis=0, tiled=True)  50 us
    all_to_all x1, starting transfers between devices, shards(): lax.all_to_all(reduced, 'expert', split_axis=0, concat_axis=0, tiled=True)  25.1 us
    ppermute x12, starting transfers between devices, z_shift(): return lax.ppermute(value, ('expert', 'dp'), pairs)  21 us
  transfers between devices with their start and end apart: 14, of which 7 were waited for; matrix products, arithmetic and copies ran while one was open for 3% of the time, Pallas kernels for 35%

profile of v9, /device:TPU:35, one launch (start us, length us, event | category | flops | bytes accessed | tf_op | source)
XLA Modules:
  0.0 820.1 jit_solution(18352641681270184843)
XLA Ops:
  9.3 2.8 gather_fusion
  12.2 2.8 gather_fusion.1
  15.0 4.3 gather_fusion.2
  20.6 3.0 all_to_all.15
  23.6 14.4 %all-to-all-start = ((bf16[64,10,2176]{2,1,0:T(8,128)(2,1)}), bf16[64,10,2176]{2,1,0:T(8,128)(2,1)}, u32[]{:S(2)}, u32[]{:S(2)}) async-start(bf16[64,10,2176]{2,1,0:T(8,128)(2,1)} %all_to_all.15), calls=%async_computation | async-start | bytes 8912896 | tf_op jit(solution)/shard_map/all_to_all | solution.py:200
  38.1 4.4 collective-permute-start.10
  48.4 104.3 %collective-permute-done.10 = bf16[1,96,4096]{2,1,0:T(8,128)(2,1)} collective-permute-done((bf16[1,96,4096]{2,1,0:T(8,128)(2,1)S(1)}, bf16[1,96,4096]{2,1,0:T(8,128)(2,1)}, u32[]{:S(2)}, u32[]{:S(2)}) %collective-permute-start.10) | collective-permute-done | bytes 786464 | tf_op jit(solution)/shard_map/ppermute | solution.py:142
  154.7 51.9 %collective-permute-done.8 = bf16[1,96,4096]{2,1,0:T(8,128)(2,1)} collective-permute-done((bf16[1,96,4096]{2,1,0:T(8,128)(2,1)S(1)}, bf16[1,96,4096]{2,1,0:T(8,128)(2,1)}, u32[]{:S(2)}, u32[]{:S(2)}) %collective-permute-start.8) | collective-permute-done | bytes 786464 | tf_op jit(solution)/shard_map/ppermute | solution.py:142
  207.1 16.3 %collective-permute-done.4 = bf16[1,96,4096]{2,1,0:T(8,128)(2,1)} collective-permute-done((bf16[1,96,4096]{2,1,0:T(8,128)(2,1)S(1)}, bf16[1,96,4096]{2,1,0:T(8,128)(2,1)}, u32[]{:S(2)}, u32[]{:S(2)}) %collective-permute-start.4) | collective-permute-done | bytes 786464 | tf_op jit(solution)/shard_map/ppermute | solution.py:142
  224.0 16.3 %collective-permute-done = bf16[1,96,4096]{2,1,0:T(8,128)(2,1)} collective-permute-done((bf16[1,96,4096]{2,1,0:T(8,128)(2,1)}, bf16[1,96,4096]{2,1,0:T(8,128)(2,1)}, u32[]{:S(2)}, u32[]{:S(2)}) %collective-permute-start) | collective-permute-done | bytes 786464 | tf_op jit(solution)/shard_map/ppermute | solution.py:142
  242.2 5.6 all_to_all.17.refs_0_
  247.8 284.9 %shard_map.119 = (bf16[640,4096]{1,0:T(8,128)(2,1)}, bf16[640,4096]{1,0:T(8,128)(2,1)}) custom-call(bf16[640,2176]{1,0:T(8,128)(2,1)} %all_to_all.17.refs_0_), custom_call_target="tpu_custom_call" | custom-call | tf_op jit(solution)/shard_map/pallas_call | solution.py:113
  532.7 3.2 collective-permute-start.1
  535.9 6.2 collective-permute-start.3
  542.1 4.9 fusion.29
  548.2 3.5 fusion.33
  551.7 14.7 %collective-permute-done.1 = bf16[1,96,4096]{2,1,0:T(8,128)(2,1)S(1)} collective-permute-done((bf16[1,96,4096]{2,1,0:T(8,128)(2,1)}, bf16[1,96,4096]{2,1,0:T(8,128)(2,1)S(1)}, u32[]{:S(2)}, u32[]{:S(2)}) %collective-permute-start.1) | collective-permute-done | bytes 786464 | tf_op jit(solution)/shard_map/ppermute | solution.py:142
  567.5 2.7 multiply_reduce_fusion
  570.8 2.9 fusion.31
  573.8 5.3 add_convert_fusion.refs_0_
  579.1 142.8 %shard_map.120 = (bf16[640,1024]{1,0:T(8,128)(2,1)}, f32[8,128]{1,0:T(8,128)}) custom-call(bf16[640,4096]{1,0:T(8,128)(2,1)} %add_convert_fusion.refs_0_, f32[8,128]{1,0:T(8,128)} %pad_bitcast_fusion.refs_1_), custom_call_target="tpu_custom_call" | custom-call | tf_op jit(solution)/shard_map/pallas_call | solution.py:59
  726.5 25.1 %all-to-all-start.1 = ((bf16[64,10,1152]{2,1,0:T(8,128)(2,1)}), bf16[64,10,1152]{2,1,0:T(8,128)(2,1)}, u32[]{:S(2)}, u32[]{:S(2)}) async-start(bf16[64,10,1152]{2,1,0:T(8,128)(2,1)} %all_to_all.18), calls=%async_computation.1 | async-start | bytes 4718592 | tf_op jit(solution)/shard_map/all_to_all | solution.py:234
  751.7 5.2 fusion.7
  762.1 50.0 %all-to-all-done.1 = bf16[64,10,1152]{2,1,0:T(8,128)(2,1)} async-done(((bf16[64,10,1152]{2,1,0:T(8,128)(2,1)}), bf16[64,10,1152]{2,1,0:T(8,128)(2,1)}, u32[]{:S(2)}, u32[]{:S(2)}) %all-to-all-start.1) | async-done | bytes 1474592 | tf_op jit(solution)/shard_map/all_to_all | solution.py:234
  (99 shorter events, 40.8 us)
Async XLA Ops:
  23.6 14.4 %copy-start.2 = (bf16[1,192,4096]{2,1,0:T(8,128)(2,1)S(1)}, bf16[1,192,4096]{2,1,0:T(8,128)(2,1)}, u32[]{:S(2)}) copy-start(bf16[1,192,4096]{2,1,0:T(8,128)(2,1)} %param.16) | copy-start | bytes 4718596
  23.6 218.6 %all-to-all-start = ((bf16[64,10,2176]{2,1,0:T(8,128)(2,1)}), bf16[64,10,2176]{2,1,0:T(8,128)(2,1)}, u32[]{:S(2)}, u32[]{:S(2)}) async-start(bf16[64,10,2176]{2,1,0:T(8,128)(2,1)} %all_to_all.15), calls=%async_computation | async-start | bytes 8912896 | tf_op jit(solution)/shard_map/all_to_all | solution.py:200
  38.1 114.7 %collective-permute-start.10 = (bf16[1,96,4096]{2,1,0:T(8,128)(2,1)S(1)}, bf16[1,96,4096]{2,1,0:T(8,128)(2,1)}, u32[]{:S(2)}, u32[]{:S(2)}) collective-permute-start(bf16[1,96,4096]{2,1,0:T(8,128)(2,1)S(1)} %get-tuple-element.58), channel_id=1, source_target_pairs={{0,130},{1,131},{2,0},{3,1},{4,134},{5,135},{6,4},{7,5},{8,138},{9... | collective-permute-start | bytes 2359304 | tf_op jit(solution)/shard_map/ppermute | solution.py:142
  42.5 164.1 %collective-permute-start.8 = (bf16[1,96,4096]{2,1,0:T(8,128)(2,1)S(1)}, bf16[1,96,4096]{2,1,0:T(8,128)(2,1)}, u32[]{:S(2)}, u32[]{:S(2)}) collective-permute-start(bf16[1,96,4096]{2,1,0:T(8,128)(2,1)S(1)} %get-tuple-element.57), channel_id=1, source_target_pairs={{0,2},{1,3},{2,128},{3,129},{4,6},{5,7},{6,132},{7,133},{8,10},{9,... | collective-permute-start | bytes 2359304 | tf_op jit(solution)/shard_map/ppermute | solution.py:142
  43.5 180.0 %collective-permute-start.4 = (bf16[1,96,4096]{2,1,0:T(8,128)(2,1)S(1)}, bf16[1,96,4096]{2,1,0:T(8,128)(2,1)}, u32[]{:S(2)}, u32[]{:S(2)}) collective-permute-start(bf16[1,96,4096]{2,1,0:T(8,128)(2,1)S(1)} %get-tuple-element.55), channel_id=1, source_target_pairs={{0,2},{1,3},{2,128},{3,129},{4,6},{5,7},{6,132},{7,133},{8,10},{9,... | collective-permute-start | bytes 2359304 | tf_op jit(solution)/shard_map/ppermute | solution.py:142
  44.7 196.1 %copy-start.7 = (s32[32]{0:T(128)S(1)}, s32[32]{0:T(128)}, u32[]{:S(2)}) copy-start(s32[32]{0:T(128)} %param.21) | copy-start | bytes 388
  44.7 178.7 %collective-permute-start.6 = (bf16[1,96,4096]{2,1,0:T(8,128)(2,1)}, bf16[1,96,4096]{2,1,0:T(8,128)(2,1)}, u32[]{:S(2)}, u32[]{:S(2)}) collective-permute-start(bf16[1,96,4096]{2,1,0:T(8,128)(2,1)} %get-tuple-element.56), channel_id=1, source_target_pairs={{0,130},{1,131},{2,0},{3,1},{4,134},{5,135},{6,4},{7,5},{8,138},{9... | collective-permute-start | bytes 2359304 | tf_op jit(solution)/shard_map/ppermute | solution.py:142
  48.3 192.0 %collective-permute-start = (bf16[1,96,4096]{2,1,0:T(8,128)(2,1)}, bf16[1,96,4096]{2,1,0:T(8,128)(2,1)}, u32[]{:S(2)}, u32[]{:S(2)}) collective-permute-start(bf16[1,96,4096]{2,1,0:T(8,128)(2,1)} %get-tuple-element.59), channel_id=1, source_target_pairs={{0,2},{1,3},{2,128},{3,129},{4,6},{5,7},{6,132},{7,133},{8,10},{9,... | collective-permute-start | bytes 2359304 | tf_op jit(solution)/shard_map/ppermute | solution.py:142
  152.7 380.0 %collective-permute-start.2 = (bf16[1,96,4096]{2,1,0:T(8,128)(2,1)}, bf16[1,96,4096]{2,1,0:T(8,128)(2,1)}, u32[]{:S(2)}, u32[]{:S(2)}) collective-permute-start(bf16[1,96,4096]{2,1,0:T(8,128)(2,1)} %get-tuple-element.60), channel_id=1, source_target_pairs={{0,130},{1,131},{2,0},{3,1},{4,134},{5,135},{6,4},{7,5},{8,138},{9... | collective-permute-start | bytes 2359304 | tf_op jit(solution)/shard_map/ppermute | solution.py:142
  206.5 329.4 %collective-permute-start.11 = (bf16[1,96,4096]{2,1,0:T(8,128)(2,1)}, bf16[1,96,4096]{2,1,0:T(8,128)(2,1)}, u32[]{:S(2)}, u32[]{:S(2)}) collective-permute-start(bf16[1,96,4096]{2,1,0:T(8,128)(2,1)} %collective-permute-done.10), channel_id=1, source_target_pairs={{0,130},{1,131},{2,0},{3,1},{4,134},{5,135},{6,4},{7,5},{8,138},{9... | collective-permute-start | bytes 2359304 | tf_op jit(solution)/shard_map/ppermute | solution.py:142
  223.4 318.7 %collective-permute-start.9 = (bf16[1,96,4096]{2,1,0:T(8,128)(2,1)}, bf16[1,96,4096]{2,1,0:T(8,128)(2,1)}, u32[]{:S(2)}, u32[]{:S(2)}) collective-permute-start(bf16[1,96,4096]{2,1,0:T(8,128)(2,1)} %collective-permute-done.8), channel_id=1, source_target_pairs={{0,2},{1,3},{2,128},{3,129},{4,6},{5,7},{6,132},{7,133},{8,10},{9,... | collective-permute-start | bytes 2359304 | tf_op jit(solution)/shard_map/ppermute | solution.py:142
  223.4 324.7 %collective-permute-start.5 = (bf16[1,96,4096]{2,1,0:T(8,128)(2,1)}, bf16[1,96,4096]{2,1,0:T(8,128)(2,1)}, u32[]{:S(2)}, u32[]{:S(2)}) collective-permute-start(bf16[1,96,4096]{2,1,0:T(8,128)(2,1)} %collective-permute-done.4), channel_id=1, source_target_pairs={{0,2},{1,3},{2,128},{3,129},{4,6},{5,7},{6,132},{7,133},{8,10},{9,... | collective-permute-start | bytes 2359304 | tf_op jit(solution)/shard_map/ppermute | solution.py:142
  240.3 307.9 %collective-permute-start.7 = (bf16[1,96,4096]{2,1,0:T(8,128)(2,1)}, bf16[1,96,4096]{2,1,0:T(8,128)(2,1)}, u32[]{:S(2)}, u32[]{:S(2)}) collective-permute-start(bf16[1,96,4096]{2,1,0:T(8,128)(2,1)} %collective-permute-done.6), channel_id=1, source_target_pairs={{0,130},{1,131},{2,0},{3,1},{4,134},{5,135},{6,4},{7,5},{8,138},{9... | collective-permute-start | bytes 2359304 | tf_op jit(solution)/shard_map/ppermute | solution.py:142
  532.7 33.7 %collective-permute-start.1 = (bf16[1,96,4096]{2,1,0:T(8,128)(2,1)}, bf16[1,96,4096]{2,1,0:T(8,128)(2,1)S(1)}, u32[]{:S(2)}, u32[]{:S(2)}) collective-permute-start(bf16[1,96,4096]{2,1,0:T(8,128)(2,1)} %collective-permute-done), channel_id=1, source_target_pairs={{0,2},{1,3},{2,128},{3,129},{4,6},{5,7},{6,132},{7,133},{8,10},{9,... | collective-permute-start | bytes 2359304 | tf_op jit(solution)/shard_map/ppermute | solution.py:142
  535.9 31.5 %collective-permute-start.3 = (bf16[1,96,4096]{2,1,0:T(8,128)(2,1)}, bf16[1,96,4096]{2,1,0:T(8,128)(2,1)S(1)}, u32[]{:S(2)}, u32[]{:S(2)}) collective-permute-start(bf16[1,96,4096]{2,1,0:T(8,128)(2,1)} %collective-permute-done.2), channel_id=1, source_target_pairs={{0,130},{1,131},{2,0},{3,1},{4,134},{5,135},{6,4},{7,5},{8,138},{9... | collective-permute-start | bytes 2359304 | tf_op jit(solution)/shard_map/ppermute | solution.py:142
  542.1 6.1 copy-start
  548.1 19.3 %slice-start.2 = ((s8[5242880]{0:T(1024)(128)(4,1)}), s8[4194304]{0:T(1024)(128)(4,1)S(1)}, s32[]{:S(2)}) async-start(s8[5242880]{0:T(1024)(128)(4,1)} %bitcast.72), calls=%async_computation.4 | async-start | bytes 8388608
  548.1 19.3 %copy-start.6 = (bf16[1,192,4096]{2,1,0:T(8,128)(2,1)S(1)}, bf16[1,192,4096]{2,1,0:T(8,128)(2,1)}, u32[]{:S(2)}) copy-start(bf16[1,192,4096]{2,1,0:T(8,128)(2,1)} %param.18) | copy-start | bytes 4718596
  548.2 19.3 %slice-start.3 = ((s8[5242880]{0:T(1024)(128)(4,1)}), s8[1048576]{0:T(1024)(128)(4,1)S(1)}, s32[]{:S(2)}) async-start(s8[5242880]{0:T(1024)(128)(4,1)} %bitcast.72), calls=%async_computation.5 | async-start | bytes 2097152
  726.5 30.3 %slice-start = ((s8[5242880]{0:T(1024)(128)(4,1)}), s8[1048576]{0:T(1024)(128)(4,1)S(1)}, s32[]{:S(2)}) async-start(s8[5242880]{0:T(1024)(128)(4,1)} %bitcast.64), calls=%async_computation.2 | async-start | bytes 2097152
  726.5 85.5 %all-to-all-start.1 = ((bf16[64,10,1152]{2,1,0:T(8,128)(2,1)}), bf16[64,10,1152]{2,1,0:T(8,128)(2,1)}, u32[]{:S(2)}, u32[]{:S(2)}) async-start(bf16[64,10,1152]{2,1,0:T(8,128)(2,1)} %all_to_all.18), calls=%async_computation.1 | async-start | bytes 4718592 | tf_op jit(solution)/shard_map/all_to_all | solution.py:234
  751.6 5.2 slice-start.1
  751.7 5.2 copy-start.4
  751.7 7.8 slice-start.4
  (5 other events, 17.8 us)

commit v10 on v9

--- a/solution.py
+++ b/solution.py
@@ -142,15 +142,14 @@
     return lax.ppermute(value, ("expert", "dp"), pairs)
 
 
-def across_z(value, expert_count, groups):
+def across_z(value, expert_count, groups, ready):
     split = value.shape[1] // 2
-    ahead = value[:, :split]
-    behind = value[:, split:]
-    for _ in range(2):
-        ahead = z_shift(ahead, expert_count, groups, 2)
-        behind = z_shift(behind, expert_count, groups, -2)
-    return jnp.concatenate([ahead, behind], axis=1)
-
+    ahead = z_shift(value[:, :split], expert_count, groups, 2)
+    behind = z_shift(value[:, split:], expert_count, groups, -2)
+    ahead, behind, ready = lax.optimization_barrier((ahead, behind, ready))
+    ahead = z_shift(ahead, expert_count, groups, 2)
+    behind = z_shift(behind, expert_count, groups, -2)
+    return jnp.concatenate([ahead, behind], axis=1), ready
 
 def pair_lookup(experts, pair_flags, half_axis):
     match = experts[:, None] % half_axis == jnp.arange(half_axis, dtype=jnp.int32)[None, :]
@@ -169,12 +168,6 @@
     own_flag = pair_lookup(jnp.reshape(my_slot, (1,)), swap_flags, half_axis)[0]
     flat_ids = expert_ids.reshape(-1)
     weights = (gate_weight, up_weight, down_weight)
-    arrived = tuple(
-        across_z(w, expert_count, groups) for w in (gate_weight, up_weight, down_weight)
-    )
-    weights = tuple(
-        (jnp.where(own_flag == 1, fresh, stay) for fresh, stay in zip(arrived, weights))
-    )
     flipped = pair_lookup(flat_ids, swap_flags, half_axis)
     target = jnp.where(flipped == 1, (flat_ids + half_axis) % expert_count, flat_ids)
     copies = row_count * routed
@@ -198,6 +191,13 @@
     gate_cols = jnp.zeros((expert_count * capacity, 128), jnp.bfloat16).at[:, 0].set(gate_buffer)
     outgoing = jnp.concatenate([x_buffer, dy_buffer, gate_cols], axis=1)
     arrived = lax.all_to_all(outgoing, "expert", split_axis=0, concat_axis=0, tiled=True)
+    stacked = jnp.concatenate([gate_weight, up_weight, down_weight], axis=1)
+    moved, arrived = across_z(stacked, expert_count, groups, arrived)
+    rows_per = gate_weight.shape[1]
+    moved = (moved[:, :rows_per], moved[:, rows_per : 2 * rows_per], moved[:, 2 * rows_per :])
+    weights = tuple(
+        (jnp.where(own_flag == 1, fresh, stay) for fresh, stay in zip(moved, weights))
+    )
     x_rows, dy_rows = dp_gather(arrived, groups, quarter)
     gate_rows = arrived[:, 2 * quarter]
     w_gate = weights[0][0]

time: 821 us -> 811 us (0.988); the launches traced: 820 us -> 801 us
  Pallas kernels: 428 us -> 466 us
  waiting for transfers between devices: 255 us -> 226 us
  starting transfers between devices: 60.5 us -> 32.8 us
    ppermute x12 -> x4, waiting for transfers between devices: 205 us -> 91 us  [z_shift(): return lax.ppermute(value, ('expert', 'dp'), pairs)]
    all_to_all x1, waiting for transfers between devices: 0.01 us -> 97.5 us  [shards(): lax.all_to_all(outgoing, 'expert', split_axis=0, concat_axis=0, tiled=True)]
    pallas_call x1, Pallas kernels: 285 us -> 324 us  [dp_gather(): pl.pallas_call(lambda *refs: dp_gather_kernel(groups, width, *refs), out_...]
    all_to_all x1, starting transfers between devices: 25.1 us -> 10.3 us  [shards(): lax.all_to_all(reduced, 'expert', split_axis=0, concat_axis=0, tiled=True)]
    ppermute x12 -> x4, starting transfers between devices: 21 us -> 7.97 us  [z_shift(): return lax.ppermute(value, ('expert', 'dp'), pairs)]
    all_to_all x1, waiting for transfers between devices: 50 us -> 37.5 us  [shards(): lax.all_to_all(reduced, 'expert', split_axis=0, concat_axis=0, tiled=True)]
  transfers between devices with their start and end apart: 14 -> 6, of which waited for: 7 -> 3; matrix products, arithmetic and copies ran while one was open for 3% -> 2% of each run, Pallas kernels for 35% -> 40%
where the time goes in v10:
time: 811 us; the launch traced here: 801 us
  Pallas kernels  466 us (57%)
  waiting for transfers between devices  226 us (28%)
  local copies, waits for them, and re-layouts  36.1 us (4%)
  starting transfers between devices  32.8 us (4%)
  matrix products  23.1 us (3%)
  other arithmetic  15.3 us (2%)
    pallas_call x1, Pallas kernels, dp_gather(): pl.pallas_call(lambda *refs: dp_gather_kernel(groups, width, *refs), out_...  324 us
    pallas_call x1, Pallas kernels, dp_scatter(): pl.pallas_call(lambda *refs: dp_scatter_kernel(groups, *refs), out_shape=...  142 us
    all_to_all x1, waiting for transfers between devices, shards(): lax.all_to_all(outgoing, 'expert', split_axis=0, concat_axis=0, tiled=True)  97.5 us
    ppermute x4, waiting for transfers between devices, z_shift(): return lax.ppermute(value, ('expert', 'dp'), pairs)  91 us
    all_to_all x1, waiting for transfers between devices, shards(): lax.all_to_all(reduced, 'expert', split_axis=0, concat_axis=0, tiled=True)  37.5 us
  transfers between devices with their start and end apart: 6, of which 3 were waited for; matrix products, arithmetic and copies ran while one was open for 2% of the time, Pallas kernels for 40%

profile of v10, /device:TPU:35, one launch (start us, length us, event | category | flops | bytes accessed | tf_op | source)
XLA Modules:
  0.0 801.1 jit_solution(7651708103903400597)
XLA Ops:
  4.8 2.4 scatter_custom_fusion
  9.3 2.8 gather_fusion
  12.2 2.8 gather_fusion.1
  15.0 4.3 gather_fusion.2
  20.6 3.0 all_to_all.16
  23.6 14.5 %all-to-all-start = ((bf16[64,10,2176]{2,1,0:T(8,128)(2,1)}), bf16[64,10,2176]{2,1,0:T(8,128)(2,1)}, u32[]{:S(2)}, u32[]{:S(2)}) async-start(bf16[64,10,2176]{2,1,0:T(8,128)(2,1)} %all_to_all.16), calls=%async_computation | async-start | bytes 8912896 | tf_op jit(solution)/shard_map/all_to_all | solution.py:193
  38.1 3.5 pad_maximum_fusion
  42.8 3.2 collective-permute-start.1
  46.0 97.5 %all-to-all-done = bf16[64,10,2176]{2,1,0:T(8,128)(2,1)} async-done(((bf16[64,10,2176]{2,1,0:T(8,128)(2,1)}), bf16[64,10,2176]{2,1,0:T(8,128)(2,1)}, u32[]{:S(2)}, u32[]{:S(2)}) %all-to-all-start) | async-done | bytes 2785312 | tf_op jit(solution)/shard_map/all_to_all | solution.py:193
  143.5 5.6 all_to_all.18.refs_0_
  149.1 91.0 %collective-permute-done = bf16[1,288,4096]{2,1,0:T(8,128)(2,1)S(1)} collective-permute-done((bf16[1,288,4096]{2,1,0:T(8,128)(2,1)}, bf16[1,288,4096]{2,1,0:T(8,128)(2,1)S(1)}, u32[]{:S(2)}, u32[]{:S(2)}) %collective-permute-start) | collective-permute-done | bytes 2359328 | tf_op jit(solution)/shard_map/ppermute | solution.py:142
  241.5 3.6 collective-permute-start.2
  246.3 324.4 %shard_map.119 = (bf16[640,4096]{1,0:T(8,128)(2,1)}, bf16[640,4096]{1,0:T(8,128)(2,1)}) custom-call(bf16[640,2176]{1,0:T(8,128)(2,1)} %all_to_all.18.refs_0_), custom_call_target="tpu_custom_call" | custom-call | tf_op jit(solution)/shard_map/pallas_call | solution.py:113
  571.8 2.3 fusion.16
  578.9 3.5 multiply_reduce_fusion
  584.5 3.9 add_convert_fusion.refs_0_
  588.4 141.7 %shard_map.120 = (bf16[640,1024]{1,0:T(8,128)(2,1)}, f32[8,128]{1,0:T(8,128)}) custom-call(bf16[640,4096]{1,0:T(8,128)(2,1)} %add_convert_fusion.refs_0_, f32[8,128]{1,0:T(8,128)} %pad_bitcast_fusion.refs_1_), custom_call_target="tpu_custom_call" | custom-call | tf_op jit(solution)/shard_map/pallas_call | solution.py:59
  734.7 10.3 %all-to-all-start.1 = ((bf16[64,10,1152]{2,1,0:T(8,128)(2,1)}), bf16[64,10,1152]{2,1,0:T(8,128)(2,1)}, u32[]{:S(2)}, u32[]{:S(2)}) async-start(bf16[64,10,1152]{2,1,0:T(8,128)(2,1)} %all_to_all.19), calls=%async_computation.1 | async-start | bytes 4718592 | tf_op jit(solution)/shard_map/all_to_all | solution.py:234
  745.1 5.2 fusion.7
  750.3 2.5 fusion.6
  752.9 2.7 fusion.8
  755.5 37.5 %all-to-all-done.1 = bf16[64,10,1152]{2,1,0:T(8,128)(2,1)} async-done(((bf16[64,10,1152]{2,1,0:T(8,128)(2,1)}), bf16[64,10,1152]{2,1,0:T(8,128)(2,1)}, u32[]{:S(2)}, u32[]{:S(2)}) %all-to-all-start.1) | async-done | bytes 1474592 | tf_op jit(solution)/shard_map/all_to_all | solution.py:234
  793.1 2.7 all_to_all.21
  798.2 2.2 slice_reduce_fusion
  (78 shorter events, 26.3 us)
Async XLA Ops:
  23.6 14.5 %copy-start.1 = (bf16[1,192,4096]{2,1,0:T(8,128)(2,1)S(1)}, bf16[1,192,4096]{2,1,0:T(8,128)(2,1)}, u32[]{:S(2)}) copy-start(bf16[1,192,4096]{2,1,0:T(8,128)(2,1)} %param.16) | copy-start | bytes 4718596
  23.6 14.5 %copy-start.3 = (bf16[1,192,4096]{2,1,0:T(8,128)(2,1)S(1)}, bf16[1,192,4096]{2,1,0:T(8,128)(2,1)}, u32[]{:S(2)}) copy-start(bf16[1,192,4096]{2,1,0:T(8,128)(2,1)} %param.17) | copy-start | bytes 4718596
  23.6 119.9 %all-to-all-start = ((bf16[64,10,2176]{2,1,0:T(8,128)(2,1)}), bf16[64,10,2176]{2,1,0:T(8,128)(2,1)}, u32[]{:S(2)}, u32[]{:S(2)}) async-start(bf16[64,10,2176]{2,1,0:T(8,128)(2,1)} %all_to_all.16), calls=%async_computation | async-start | bytes 8912896 | tf_op jit(solution)/shard_map/all_to_all | solution.py:193
  41.6 198.5 %collective-permute-start = (bf16[1,288,4096]{2,1,0:T(8,128)(2,1)}, bf16[1,288,4096]{2,1,0:T(8,128)(2,1)S(1)}, u32[]{:S(2)}, u32[]{:S(2)}) collective-permute-start(bf16[1,288,4096]{2,1,0:T(8,128)(2,1)} %get-tuple-element.62), channel_id=1, source_target_pairs={{0,2},{1,3},{2,128},{3,129},{4,6},{5,7},{6,132},{7,133},{8,10},{9,... | collective-permute-start | bytes 7077896 | tf_op jit(solution)/shard_map/ppermute | solution.py:142
  42.8 202.3 %copy-start.5 = (s32[32]{0:T(128)S(1)}, s32[32]{0:T(128)}, u32[]{:S(2)}) copy-start(s32[32]{0:T(128)} %param.21) | copy-start | bytes 388
  42.8 198.7 %collective-permute-start.1 = (bf16[1,288,4096]{2,1,0:T(8,128)(2,1)}, bf16[1,288,4096]{2,1,0:T(8,128)(2,1)}, u32[]{:S(2)}, u32[]{:S(2)}) collective-permute-start(bf16[1,288,4096]{2,1,0:T(8,128)(2,1)} %get-tuple-element.61), channel_id=1, source_target_pairs={{0,130},{1,131},{2,0},{3,1},{4,134},{5,135},{6,4},{7,5},{8,138},{9... | collective-permute-start | bytes 7077896 | tf_op jit(solution)/shard_map/ppermute | solution.py:142
  240.1 1.4 copy-start.6
  241.5 330.4 %collective-permute-start.3 = (bf16[1,288,4096]{2,1,0:T(8,128)(2,1)}, bf16[1,288,4096]{2,1,0:T(8,128)(2,1)S(1)}, u32[]{:S(2)}, u32[]{:S(2)}) collective-permute-start(bf16[1,288,4096]{2,1,0:T(8,128)(2,1)} %copy-done.6), channel_id=1, source_target_pairs={{0,2},{1,3},{2,128},{3,129},{4,6},{5,7},{6,132},{7,133},{8,10},{9,... | collective-permute-start | bytes 7077896 | tf_op jit(solution)/shard_map/ppermute | solution.py:142
  241.5 330.4 %collective-permute-start.2 = (bf16[1,288,4096]{2,1,0:T(8,128)(2,1)}, bf16[1,288,4096]{2,1,0:T(8,128)(2,1)}, u32[]{:S(2)}, u32[]{:S(2)}) collective-permute-start(bf16[1,288,4096]{2,1,0:T(8,128)(2,1)} %collective-permute-done.1), channel_id=1, source_target_pairs={{0,130},{1,131},{2,0},{3,1},{4,134},{5,135},{6,4},{7,5},{8,138},{9... | collective-permute-start | bytes 7077896 | tf_op jit(solution)/shard_map/ppermute | solution.py:142
  571.8 3.2 copy-start
  575.0 1.9 copy-start.2
  575.0 3.8 slice-start.2
  576.9 1.9 copy-start.4
  576.9 1.9 slice-start.3
  734.7 15.6 %slice-start = ((s8[5242880]{0:T(1024)(128)(4,1)}), s8[1048576]{0:T(1024)(128)(4,1)S(1)}, s32[]{:S(2)}) async-start(s8[5242880]{0:T(1024)(128)(4,1)} %bitcast.64), calls=%async_computation.2 | async-start | bytes 2097152
  734.7 58.3 %all-to-all-start.1 = ((bf16[64,10,1152]{2,1,0:T(8,128)(2,1)}), bf16[64,10,1152]{2,1,0:T(8,128)(2,1)}, u32[]{:S(2)}, u32[]{:S(2)}) async-start(bf16[64,10,1152]{2,1,0:T(8,128)(2,1)} %all_to_all.19), calls=%async_computation.1 | async-start | bytes 4718592 | tf_op jit(solution)/shard_map/all_to_all | solution.py:234
  745.1 5.2 slice-start.1
  745.1 7.7 slice-start.4
  750.3 2.6 slice-start.5

commit v11 on v6

--- a/solution.py
+++ b/solution.py
@@ -129,6 +129,16 @@
     return lax.ppermute(value, axis, [(i, (i + by) % devices) for i in range(devices)])
 
 
+def mirror_swap(value, expert_count, groups):
+    half_axis = expert_count // 2
+    pairs = [
+        (slot * groups + group, ((slot + half_axis) % expert_count) * groups + groups - 1 - group)
+        for slot in range(expert_count)
+        for group in range(groups)
+    ]
+    return lax.ppermute(value, ("expert", "dp"), pairs)
+
+
 def pair_lookup(experts, pair_flags, half_axis):
     match = experts[:, None] % half_axis == jnp.arange(half_axis, dtype=jnp.int32)[None, :]
     return jnp.sum(jnp.where(match, pair_flags[None, :], 0), axis=1)
@@ -146,7 +156,7 @@
     own_flag = pair_lookup(jnp.reshape(my_slot, (1,)), swap_flags, half_axis)[0]
     flat_ids = expert_ids.reshape(-1)
     weights = (gate_weight, up_weight, down_weight)
-    arrived = from_behind((gate_weight, up_weight, down_weight), "expert", half_axis)
+    arrived = mirror_swap((gate_weight, up_weight, down_weight), expert_count, groups)
     weights = tuple(
         (jnp.where(own_flag == 1, fresh, stay) for fresh, stay in zip(arrived, weights))
     )
@@ -194,11 +204,14 @@
     input_part = input_part + jnp.dot(grad_up, w_up, preferred_element_type=jnp.float32)
     scaled = gate_rows[:, None] * dy_rows
     contract_rows = (((0,), (0,)), ((), ()))
+    computed = (grad_gate, grad_up, hidden)
+    mirrored = lax.ppermute(computed, "dp", [(g, groups - 1 - g) for g in range(groups)])
+    mine = tuple(jnp.where(own_flag == 1, far, near) for far, near in zip(mirrored, computed))
     grad_wgate = lax.dot_general(
-        grad_gate, x_rows, contract_rows, preferred_element_type=jnp.float32
-    )
-    grad_wup = lax.dot_general(grad_up, x_rows, contract_rows, preferred_element_type=jnp.float32)
-    grad_wdown = lax.dot_general(hidden, scaled, contract_rows, preferred_element_type=jnp.float32)
+        mine[0], x_rows, contract_rows, preferred_element_type=jnp.float32
+    )
+    grad_wup = lax.dot_general(mine[1], x_rows, contract_rows, preferred_element_type=jnp.float32)
+    grad_wdown = lax.dot_general(mine[2], scaled, contract_rows, preferred_element_type=jnp.float32)
     slots = capacity * expert_count
     score_tile = jnp.zeros((8 * 128,), jnp.float32).at[:slots].set(score_part).reshape(8, 128)
     share, score_sum = dp_scatter(input_part.astype(jnp.bfloat16), score_tile, groups)

time: 811 us -> 774 us (0.954)
  Pallas kernels: 528 us -> 493 us
    ppermute x3 -> x6, waiting for transfers between devices: 0.01 us -> 74.4 us  [the longest x3 74.4 us: shards(): lax.ppermute(computed, 'dp', [(g, groups - 1 - g) for g in range(groups)])]
    pallas_call x1, Pallas kernels: 384 us -> 327 us  [dp_gather(): pl.pallas_call(lambda *refs: dp_gather_kernel(groups, width, *refs), out_...]
    all_to_all x1, waiting for transfers between devices: 37.7 us -> 0.01 us  [shards(): lax.all_to_all(reduced, 'expert', split_axis=0, concat_axis=0, tiled=True)]
    all_to_all x1, waiting for transfers between devices: 125 us -> 92 us  [shards(): lax.all_to_all(outgoing, 'expert', split_axis=0, concat_axis=0, tiled=True)]
    pallas_call x1, Pallas kernels: 144 us -> 166 us  [dp_scatter(): pl.pallas_call(lambda *refs: dp_scatter_kernel(groups, *refs), out_shape=...]
  transfers between devices with their start and end apart: 5 -> 8, of which waited for: 2 -> 4; matrix products, arithmetic and copies ran while one was open for 2% -> 3% of each run, Pallas kernels for 48% -> 42%
where the time goes in v11:
time: 774 us; the launch traced here: 772 us
  Pallas kernels  493 us (64%)
  waiting for transfers between devices  166 us (21%)
  starting transfers between devices  36.7 us (5%)
  local copies, waits for them, and re-layouts  34 us (4%)
  matrix products  31.5 us (4%)
  other arithmetic  9.53 us (1%)
    pallas_call x1, Pallas kernels, dp_gather(): pl.pallas_call(lambda *refs: dp_gather_kernel(groups, width, *refs), out_...  327 us
    pallas_call x1, Pallas kernels, dp_scatter(): pl.pallas_call(lambda *refs: dp_scatter_kernel(groups, *refs), out_shape=...  166 us
    all_to_all x1, waiting for transfers between devices, shards(): lax.all_to_all(outgoing, 'expert', split_axis=0, concat_axis=0, tiled=True)  92 us
    ppermute x3, waiting for transfers between devices, shards(): lax.ppermute(computed, 'dp', [(g, groups - 1 - g) for g in range(groups)])  74.4 us
  transfers between devices with their start and end apart: 8, of which 4 were waited for; matrix products, arithmetic and copies ran while one was open for 3% of the time, Pallas kernels for 42%

profile of v11, /device:TPU:35, one launch (start us, length us, event | category | flops | bytes accessed | tf_op | source)
XLA Modules:
  0.0 772.4 jit_solution(5934879325837172908)
XLA Ops:
  4.8 2.4 scatter_custom_fusion
  9.3 2.8 gather_fusion
  12.2 2.8 gather_fusion.1
  15.0 4.3 gather_fusion.2
  20.6 3.0 all_to_all.15
  23.6 14.5 %all-to-all-start = ((bf16[64,10,2176]{2,1,0:T(8,128)(2,1)}), bf16[64,10,2176]{2,1,0:T(8,128)(2,1)}, u32[]{:S(2)}, u32[]{:S(2)}) async-start(bf16[64,10,2176]{2,1,0:T(8,128)(2,1)} %all_to_all.15), calls=%async_computation | async-start | bytes 8912896 | tf_op jit(solution)/shard_map/all_to_all | solution.py:185
  38.1 4.8 collective-permute-start.2
  43.1 4.4 collective-permute-start
  48.7 92.0 %all-to-all-done = bf16[64,10,2176]{2,1,0:T(8,128)(2,1)} async-done(((bf16[64,10,2176]{2,1,0:T(8,128)(2,1)}), bf16[64,10,2176]{2,1,0:T(8,128)(2,1)}, u32[]{:S(2)}, u32[]{:S(2)}) %all-to-all-start) | async-done | bytes 2785312 | tf_op jit(solution)/shard_map/all_to_all | solution.py:185
  140.7 5.7 all_to_all.17.refs_0_
  146.3 326.9 %shard_map.119 = (bf16[640,4096]{1,0:T(8,128)(2,1)}, bf16[640,4096]{1,0:T(8,128)(2,1)}) custom-call(bf16[640,2176]{1,0:T(8,128)(2,1)} %all_to_all.17.refs_0_), custom_call_target="tpu_custom_call" | custom-call | tf_op jit(solution)/shard_map/pallas_call | solution.py:113
  474.4 5.0 fusion.15
  479.4 3.5 fusion.19
  483.0 4.1 multiply_reduce_fusion
  487.8 3.0 fusion.17
  490.8 5.4 add_convert_fusion.refs_0_
  496.2 165.8 %shard_map.120 = (bf16[640,1024]{1,0:T(8,128)(2,1)}, f32[8,128]{1,0:T(8,128)}) custom-call(bf16[640,4096]{1,0:T(8,128)(2,1)} %add_convert_fusion.refs_0_, f32[8,128]{1,0:T(8,128)} %pad_bitcast_fusion.refs_1_), custom_call_target="tpu_custom_call" | custom-call | tf_op jit(solution)/shard_map/pallas_call | solution.py:59
  666.6 11.0 %all-to-all-start.1 = ((bf16[64,10,1152]{2,1,0:T(8,128)(2,1)}), bf16[64,10,1152]{2,1,0:T(8,128)(2,1)}, u32[]{:S(2)}, u32[]{:S(2)}) async-start(bf16[64,10,1152]{2,1,0:T(8,128)(2,1)} %all_to_all.18), calls=%async_computation.1 | async-start | bytes 4718592 | tf_op jit(solution)/shard_map/all_to_all | solution.py:222
  679.6 71.6 %collective-permute-done.4 = bf16[640,192]{0,1:T(8,128)(2,1)S(1)} collective-permute-done((bf16[640,192]{0,1:T(8,128)(2,1)S(1)}, bf16[640,192]{0,1:T(8,128)(2,1)S(1)}, u32[]{:S(2)}, u32[]{:S(2)}) %collective-permute-start.4) | collective-permute-done | bytes 245792 | tf_op jit(solution)/shard_map/ppermute | solution.py:208
  751.2 5.2 fusion.7
  756.5 2.6 fusion.6
  759.0 2.7 collective-permute-done.5
  761.7 2.7 fusion.8
  764.4 2.7 all_to_all.20
  (82 shorter events, 21.9 us)
Async XLA Ops:
  23.6 14.5 %copy-start.1 = (bf16[1,192,4096]{2,1,0:T(8,128)(2,1)S(1)}, bf16[1,192,4096]{2,1,0:T(8,128)(2,1)}, u32[]{:S(2)}) copy-start(bf16[1,192,4096]{2,1,0:T(8,128)(2,1)} %param.16) | copy-start | bytes 4718596
  23.6 19.4 %copy-start = (bf16[1,192,4096]{2,1,0:T(8,128)(2,1)S(1)}, bf16[1,192,4096]{2,1,0:T(8,128)(2,1)}, u32[]{:S(2)}) copy-start(bf16[1,192,4096]{2,1,0:T(8,128)(2,1)} %param.17) | copy-start | bytes 4718596
  23.6 23.8 %copy-start.4 = (s32[32]{0:T(128)S(1)}, s32[32]{0:T(128)}, u32[]{:S(2)}) copy-start(s32[32]{0:T(128)} %param.21) | copy-start | bytes 388
  23.6 117.1 %all-to-all-start = ((bf16[64,10,2176]{2,1,0:T(8,128)(2,1)}), bf16[64,10,2176]{2,1,0:T(8,128)(2,1)}, u32[]{:S(2)}, u32[]{:S(2)}) async-start(bf16[64,10,2176]{2,1,0:T(8,128)(2,1)} %all_to_all.15), calls=%async_computation | async-start | bytes 8912896 | tf_op jit(solution)/shard_map/all_to_all | solution.py:185
  38.1 436.2 %collective-permute-start.2 = (bf16[1,192,4096]{2,1,0:T(8,128)(2,1)S(1)}, bf16[1,192,4096]{2,1,0:T(8,128)(2,1)}, u32[]{:S(2)}, u32[]{:S(2)}) collective-permute-start(bf16[1,192,4096]{2,1,0:T(8,128)(2,1)S(1)} %copy-done.1), channel_id=1, source_target_pairs={{0,131},{1,130},{2,129},{3,128},{4,135},{5,134},{6,133},{7,132},{8... | collective-permute-start | bytes 4718600 | tf_op jit(solution)/shard_map/ppermute | solution.py:139
  43.0 436.5 %collective-permute-start.1 = (bf16[1,192,4096]{2,1,0:T(8,128)(2,1)S(1)}, bf16[1,192,4096]{2,1,0:T(8,128)(2,1)}, u32[]{:S(2)}, u32[]{:S(2)}) collective-permute-start(bf16[1,192,4096]{2,1,0:T(8,128)(2,1)S(1)} %copy-done), channel_id=1, source_target_pairs={{0,131},{1,130},{2,129},{3,128},{4,135},{5,134},{6,133},{7,132},{8... | collective-permute-start | bytes 4718600 | tf_op jit(solution)/shard_map/ppermute | solution.py:139
  43.1 439.9 %collective-permute-start = (bf16[1,192,4096]{2,1,0:T(8,128)(2,1)}, bf16[1,192,4096]{2,1,0:T(8,128)(2,1)}, u32[]{:S(2)}, u32[]{:S(2)}) collective-permute-start(bf16[1,192,4096]{2,1,0:T(8,128)(2,1)} %param.18), channel_id=1, source_target_pairs={{0,131},{1,130},{2,129},{3,128},{4,135},{5,134},{6,133},{7,132},{8... | collective-permute-start | bytes 4718600 | tf_op jit(solution)/shard_map/ppermute | solution.py:139
  474.4 5.1 copy-start.5
  474.4 8.6 %slice-start = ((s8[5242880]{0:T(1024)(128)(4,1)}), s8[4194304]{0:T(1024)(128)(4,1)S(1)}, s32[]{:S(2)}) async-start(s8[5242880]{0:T(1024)(128)(4,1)} %bitcast.69), calls=%async_computation.2 | async-start | bytes 8388608
  479.4 3.6 slice-start.1
  479.4 3.6 copy-start.6
  487.1 3.7 copy-start.2
  666.6 11.1 %copy-start.3 = (bf16[640,192]{0,1:T(8,128)(2,1)S(1)}, bf16[640,192]{0,1:T(8,128)(2,1)}, u32[]{:S(2)}) copy-start(bf16[640,192]{0,1:T(8,128)(2,1)} %copy-done.2) | copy-start | bytes 737284
  666.6 12.6 %copy-start.7 = (bf16[640,192]{0,1:T(8,128)(2,1)S(1)}, bf16[640,192]{0,1:T(8,128)(2,1)}, u32[]{:S(2)}) copy-start(bf16[640,192]{0,1:T(8,128)(2,1)} %get-tuple-element.50) | copy-start | bytes 737284
  666.6 97.8 %all-to-all-start.1 = ((bf16[64,10,1152]{2,1,0:T(8,128)(2,1)}), bf16[64,10,1152]{2,1,0:T(8,128)(2,1)}, u32[]{:S(2)}, u32[]{:S(2)}) async-start(bf16[64,10,1152]{2,1,0:T(8,128)(2,1)} %all_to_all.18), calls=%async_computation.1 | async-start | bytes 4718592 | tf_op jit(solution)/shard_map/all_to_all | solution.py:222
  677.6 73.6 %collective-permute-start.4 = (bf16[640,192]{0,1:T(8,128)(2,1)S(1)}, bf16[640,192]{0,1:T(8,128)(2,1)S(1)}, u32[]{:S(2)}, u32[]{:S(2)}) collective-permute-start(bf16[640,192]{0,1:T(8,128)(2,1)S(1)} %get-tuple-element.56), channel_id=1, source_target_pairs={{0,3},{1,2},{2,1},{3,0},{4,7},{5,6},{6,5},{7,4},{8,11},{9,10},{10,... | collective-permute-start | bytes 737288 | tf_op jit(solution)/shard_map/ppermute | solution.py:208
  677.7 78.8 %collective-permute-start.3 = (bf16[640,192]{0,1:T(8,128)(2,1)S(1)}, bf16[640,192]{0,1:T(8,128)(2,1)S(1)}, u32[]{:S(2)}, u32[]{:S(2)}) collective-permute-start(bf16[640,192]{0,1:T(8,128)(2,1)S(1)} %copy-done.3), channel_id=1, source_target_pairs={{0,3},{1,2},{2,1},{3,0},{4,7},{5,6},{6,5},{7,4},{8,11},{9,10},{10,... | collective-permute-start | bytes 737288 | tf_op jit(solution)/shard_map/ppermute | solution.py:208
  679.2 77.2 %slice-start.4 = ((s8[5242880]{0:T(1024)(128)(4,1)}), s8[4194304]{0:T(1024)(128)(4,1)S(1)}, s32[]{:S(2)}) async-start(s8[5242880]{0:T(1024)(128)(4,1)} %bitcast.73), calls=%async_computation.6 | async-start | bytes 8388608
  679.2 77.2 %slice-start.5 = ((s8[5242880]{0:T(1024)(128)(4,1)}), s8[1048576]{0:T(1024)(128)(4,1)S(1)}, s32[]{:S(2)}) async-start(s8[5242880]{0:T(1024)(128)(4,1)} %bitcast.73), calls=%async_computation.7 | async-start | bytes 2097152
  679.2 82.5 %collective-permute-start.5 = (bf16[640,192]{0,1:T(8,128)(2,1)S(1)}, bf16[640,192]{0,1:T(8,128)(2,1)S(1)}, u32[]{:S(2)}, u32[]{:S(2)}) collective-permute-start(bf16[640,192]{0,1:T(8,128)(2,1)S(1)} %copy-done.7), channel_id=1, source_target_pairs={{0,3},{1,2},{2,1},{3,0},{4,7},{5,6},{6,5},{7,4},{8,11},{9,10},{10,... | collective-permute-start | bytes 737288 | tf_op jit(solution)/shard_map/ppermute | solution.py:208
  751.2 10.5 %slice-start.2 = ((s8[5242880]{0:T(1024)(128)(4,1)}), s8[4194304]{0:T(1024)(128)(4,1)S(1)}, s32[]{:S(2)}) async-start(s8[5242880]{0:T(1024)(128)(4,1)} %bitcast.71), calls=%async_computation.4 | async-start | bytes 8388608
  756.4 5.3 slice-start.3

commit v12 on v11

--- a/solution.py
+++ b/solution.py
@@ -206,6 +206,7 @@
     contract_rows = (((0,), (0,)), ((), ()))
     computed = (grad_gate, grad_up, hidden)
     mirrored = lax.ppermute(computed, "dp", [(g, groups - 1 - g) for g in range(groups)])
+    mirrored, input_part, score_part = lax.optimization_barrier((mirrored, input_part, score_part))
     mine = tuple(jnp.where(own_flag == 1, far, near) for far, near in zip(mirrored, computed))
     grad_wgate = lax.dot_general(
         mine[0], x_rows, contract_rows, preferred_element_type=jnp.float32

time: 774 us -> 768 us (level); the launches traced: 772 us -> 758 us
  waiting for transfers between devices: 166 us -> 148 us
    ppermute x3, waiting for transfers between devices: 74.4 us -> 21.5 us  [shards(): lax.ppermute(computed, 'dp', [(g, groups - 1 - g) for g in range(groups)])]
    all_to_all x1, waiting for transfers between devices: 0.01 us -> 34.9 us  [shards(): lax.all_to_all(reduced, 'expert', split_axis=0, concat_axis=0, tiled=True)]
  transfers between devices with their start and end apart: 8 -> 8, of which waited for: 4 -> 5; matrix products, arithmetic and copies ran while one was open for 3% -> 4% of each run, Pallas kernels for 42% -> 43%
where the time goes in v12:
time: 768 us; the launch traced here: 758 us
  Pallas kernels  495 us (64%)
  waiting for transfers between devices  148 us (19%)
  starting transfers between devices  35.5 us (5%)
  local copies, waits for them, and re-layouts  34.6 us (5%)
  matrix products  33.4 us (4%)
  other arithmetic  9.53 us (1%)
    pallas_call x1, Pallas kernels, dp_gather(): pl.pallas_call(lambda *refs: dp_gather_kernel(groups, width, *refs), out_...  327 us
    pallas_call x1, Pallas kernels, dp_scatter(): pl.pallas_call(lambda *refs: dp_scatter_kernel(groups, *refs), out_shape=...  168 us
    all_to_all x1, waiting for transfers between devices, shards(): lax.all_to_all(outgoing, 'expert', split_axis=0, concat_axis=0, tiled=True)  92 us
    all_to_all x1, waiting for transfers between devices, shards(): lax.all_to_all(reduced, 'expert', split_axis=0, concat_axis=0, tiled=True)  34.9 us
    ppermute x3, waiting for transfers between devices, shards(): lax.ppermute(computed, 'dp', [(g, groups - 1 - g) for g in range(groups)])  21.5 us
  transfers between devices with their start and end apart: 8, of which 5 were waited for; matrix products, arithmetic and copies ran while one was open for 4% of the time, Pallas kernels for 43%

profile of v12, /device:TPU:35, one launch (start us, length us, event | category | flops | bytes accessed | tf_op | source)
XLA Modules:
  0.0 758.1 jit_solution(3103522226863437215)
XLA Ops:
  9.3 2.8 gather_fusion
  12.2 2.8 gather_fusion.1
  15.0 4.3 gather_fusion.2
  20.6 3.0 all_to_all.15
  23.6 14.5 %all-to-all-start = ((bf16[64,10,2176]{2,1,0:T(8,128)(2,1)}), bf16[64,10,2176]{2,1,0:T(8,128)(2,1)}, u32[]{:S(2)}, u32[]{:S(2)}) async-start(bf16[64,10,2176]{2,1,0:T(8,128)(2,1)} %all_to_all.15), calls=%async_computation | async-start | bytes 8912896 | tf_op jit(solution)/shard_map/all_to_all | solution.py:185
  38.1 4.8 collective-permute-start.2
  43.1 4.4 collective-permute-start
  48.7 92.0 %all-to-all-done = bf16[64,10,2176]{2,1,0:T(8,128)(2,1)} async-done(((bf16[64,10,2176]{2,1,0:T(8,128)(2,1)}), bf16[64,10,2176]{2,1,0:T(8,128)(2,1)}, u32[]{:S(2)}, u32[]{:S(2)}) %all-to-all-start) | async-done | bytes 2785312 | tf_op jit(solution)/shard_map/all_to_all | solution.py:185
  140.7 5.6 all_to_all.17.refs_0_
  146.3 326.9 %shard_map.119 = (bf16[640,4096]{1,0:T(8,128)(2,1)}, bf16[640,4096]{1,0:T(8,128)(2,1)}) custom-call(bf16[640,2176]{1,0:T(8,128)(2,1)} %all_to_all.17.refs_0_), custom_call_target="tpu_custom_call" | custom-call | tf_op jit(solution)/shard_map/pallas_call | solution.py:113
  474.4 5.0 fusion.15
  479.4 3.5 fusion.19
  483.0 3.5 multiply_reduce_fusion
  488.1 3.0 fusion.17
  491.1 5.4 convolution_add_fusion.refs_0_
  496.6 12.0 %collective-permute-done.3 = bf16[640,192]{0,1:T(8,128)(2,1)S(1)} collective-permute-done((bf16[640,192]{0,1:T(8,128)(2,1)S(1)}, bf16[640,192]{0,1:T(8,128)(2,1)S(1)}, u32[]{:S(2)}, u32[]{:S(2)}) %collective-permute-start.3) | collective-permute-done | bytes 245792 | tf_op jit(solution)/shard_map/ppermute | solution.py:208
  508.6 5.3 collective-permute-done.4
  513.8 4.2 collective-permute-done.5
  519.3 168.1 %shard_map.120 = (bf16[640,1024]{1,0:T(8,128)(2,1)}, f32[8,128]{1,0:T(8,128)}) custom-call(bf16[640,4096]{1,0:T(8,128)(2,1)} %convolution_add_fusion.refs_0_, f32[8,128]{1,0:T(8,128)} %pad_bitcast_fusion.refs_1_), custom_call_target="tpu_custom_call" | custom-call | tf_op jit(solution)/shard_map/pallas_call | solution.py:59
  692.1 10.1 %all-to-all-start.1 = ((bf16[64,10,1152]{2,1,0:T(8,128)(2,1)}), bf16[64,10,1152]{2,1,0:T(8,128)(2,1)}, u32[]{:S(2)}, u32[]{:S(2)}) async-start(bf16[64,10,1152]{2,1,0:T(8,128)(2,1)} %all_to_all.18), calls=%async_computation.1 | async-start | bytes 4718592 | tf_op jit(solution)/shard_map/all_to_all | solution.py:223
  702.2 5.2 fusion.7
  707.4 5.2 fusion.6
  712.6 2.7 fusion.8
  715.3 34.9 %all-to-all-done.1 = bf16[64,10,1152]{2,1,0:T(8,128)(2,1)} async-done(((bf16[64,10,1152]{2,1,0:T(8,128)(2,1)}), bf16[64,10,1152]{2,1,0:T(8,128)(2,1)}, u32[]{:S(2)}, u32[]{:S(2)}) %all-to-all-start.1) | async-done | bytes 1474592 | tf_op jit(solution)/shard_map/all_to_all | solution.py:223
  (91 shorter events, 27.3 us)
Async XLA Ops:
  23.6 14.5 %copy-start.1 = (bf16[1,192,4096]{2,1,0:T(8,128)(2,1)S(1)}, bf16[1,192,4096]{2,1,0:T(8,128)(2,1)}, u32[]{:S(2)}) copy-start(bf16[1,192,4096]{2,1,0:T(8,128)(2,1)} %param.16) | copy-start | bytes 4718596
  23.6 19.4 %copy-start = (bf16[1,192,4096]{2,1,0:T(8,128)(2,1)S(1)}, bf16[1,192,4096]{2,1,0:T(8,128)(2,1)}, u32[]{:S(2)}) copy-start(bf16[1,192,4096]{2,1,0:T(8,128)(2,1)} %param.17) | copy-start | bytes 4718596
  23.6 23.8 %copy-start.4 = (s32[32]{0:T(128)S(1)}, s32[32]{0:T(128)}, u32[]{:S(2)}) copy-start(s32[32]{0:T(128)} %param.21) | copy-start | bytes 388
  23.6 117.1 %all-to-all-start = ((bf16[64,10,2176]{2,1,0:T(8,128)(2,1)}), bf16[64,10,2176]{2,1,0:T(8,128)(2,1)}, u32[]{:S(2)}, u32[]{:S(2)}) async-start(bf16[64,10,2176]{2,1,0:T(8,128)(2,1)} %all_to_all.15), calls=%async_computation | async-start | bytes 8912896 | tf_op jit(solution)/shard_map/all_to_all | solution.py:185
  38.1 436.2 %collective-permute-start.2 = (bf16[1,192,4096]{2,1,0:T(8,128)(2,1)S(1)}, bf16[1,192,4096]{2,1,0:T(8,128)(2,1)}, u32[]{:S(2)}, u32[]{:S(2)}) collective-permute-start(bf16[1,192,4096]{2,1,0:T(8,128)(2,1)S(1)} %copy-done.1), channel_id=1, source_target_pairs={{0,131},{1,130},{2,129},{3,128},{4,135},{5,134},{6,133},{7,132},{8... | collective-permute-start | bytes 4718600 | tf_op jit(solution)/shard_map/ppermute | solution.py:139
  43.0 436.4 %collective-permute-start.1 = (bf16[1,192,4096]{2,1,0:T(8,128)(2,1)S(1)}, bf16[1,192,4096]{2,1,0:T(8,128)(2,1)}, u32[]{:S(2)}, u32[]{:S(2)}) collective-permute-start(bf16[1,192,4096]{2,1,0:T(8,128)(2,1)S(1)} %copy-done), channel_id=1, source_target_pairs={{0,131},{1,130},{2,129},{3,128},{4,135},{5,134},{6,133},{7,132},{8... | collective-permute-start | bytes 4718600 | tf_op jit(solution)/shard_map/ppermute | solution.py:139
  43.1 439.8 %collective-permute-start = (bf16[1,192,4096]{2,1,0:T(8,128)(2,1)}, bf16[1,192,4096]{2,1,0:T(8,128)(2,1)}, u32[]{:S(2)}, u32[]{:S(2)}) collective-permute-start(bf16[1,192,4096]{2,1,0:T(8,128)(2,1)} %param.18), channel_id=1, source_target_pairs={{0,131},{1,130},{2,129},{3,128},{4,135},{5,134},{6,133},{7,132},{8... | collective-permute-start | bytes 4718600 | tf_op jit(solution)/shard_map/ppermute | solution.py:139
  474.3 5.1 copy-start.5
  474.3 8.6 %slice-start = ((s8[5242880]{0:T(1024)(128)(4,1)}), s8[4194304]{0:T(1024)(128)(4,1)S(1)}, s32[]{:S(2)}) async-start(s8[5242880]{0:T(1024)(128)(4,1)} %bitcast.69), calls=%async_computation.2 | async-start | bytes 8388608
  486.4 4.7 copy-start.2
  486.4 4.7 copy-start.7
  486.4 22.1 %collective-permute-start.3 = (bf16[640,192]{0,1:T(8,128)(2,1)S(1)}, bf16[640,192]{0,1:T(8,128)(2,1)S(1)}, u32[]{:S(2)}, u32[]{:S(2)}) collective-permute-start(bf16[640,192]{0,1:T(8,128)(2,1)S(1)} %get-tuple-element.65), channel_id=1, source_target_pairs={{0,3},{1,2},{2,1},{3,0},{4,7},{5,6},{6,5},{7,4},{8,11},{9,10},{10,... | collective-permute-start | bytes 737288 | tf_op jit(solution)/shard_map/ppermute | solution.py:208
  486.5 27.3 %collective-permute-start.4 = (bf16[640,192]{0,1:T(8,128)(2,1)S(1)}, bf16[640,192]{0,1:T(8,128)(2,1)S(1)}, u32[]{:S(2)}, u32[]{:S(2)}) collective-permute-start(bf16[640,192]{0,1:T(8,128)(2,1)S(1)} %get-tuple-element.66), channel_id=1, source_target_pairs={{0,3},{1,2},{2,1},{3,0},{4,7},{5,6},{6,5},{7,4},{8,11},{9,10},{10,... | collective-permute-start | bytes 737288 | tf_op jit(solution)/shard_map/ppermute | solution.py:208
  488.0 30.1 %collective-permute-start.5 = (bf16[640,192]{0,1:T(8,128)(2,1)S(1)}, bf16[640,192]{0,1:T(8,128)(2,1)S(1)}, u32[]{:S(2)}, u32[]{:S(2)}) collective-permute-start(bf16[640,192]{0,1:T(8,128)(2,1)S(1)} %get-tuple-element.60), channel_id=1, source_target_pairs={{0,3},{1,2},{2,1},{3,0},{4,7},{5,6},{6,5},{7,4},{8,11},{9,10},{10,... | collective-permute-start | bytes 737288 | tf_op jit(solution)/shard_map/ppermute | solution.py:208
  508.6 9.5 %copy-start.9 = (bf16[640,192]{0,1:T(8,128)(2,1)}, bf16[640,192]{0,1:T(8,128)(2,1)S(1)}, u32[]{:S(2)}) copy-start(bf16[640,192]{0,1:T(8,128)(2,1)S(1)} %collective-permute-done.3) | copy-start | bytes 737284
  513.8 4.2 copy-start.13
  692.1 10.1 %copy-start.14 = (bf16[640,192]{0,1:T(8,128)(2,1)S(1)}, bf16[640,192]{0,1:T(8,128)(2,1)}, u32[]{:S(2)}) copy-start(bf16[640,192]{0,1:T(8,128)(2,1)} %copy-done.13) | copy-start | bytes 737284
  692.1 58.1 %all-to-all-start.1 = ((bf16[64,10,1152]{2,1,0:T(8,128)(2,1)}), bf16[64,10,1152]{2,1,0:T(8,128)(2,1)}, u32[]{:S(2)}, u32[]{:S(2)}) async-start(bf16[64,10,1152]{2,1,0:T(8,128)(2,1)} %all_to_all.18), calls=%async_computation.1 | async-start | bytes 4718592 | tf_op jit(solution)/shard_map/all_to_all | solution.py:223
  702.2 5.2 copy-start.3
  702.2 5.2 copy-start.10
  702.2 10.4 %slice-start.2 = ((s8[5242880]{0:T(1024)(128)(4,1)}), s8[4194304]{0:T(1024)(128)(4,1)S(1)}, s32[]{:S(2)}) async-start(s8[5242880]{0:T(1024)(128)(4,1)} %bitcast.71), calls=%async_computation.4 | async-start | bytes 8388608
  707.4 5.2 slice-start.3
  707.4 5.2 copy-start.8
  707.4 5.2 copy-start.12
  (3 other events, 7.8 us)

commit v13 on v11

--- a/solution.py
+++ b/solution.py
@@ -8,7 +8,9 @@
 MESH_IDS = pl.DeviceIdType.MESH
 
 
-def dp_scatter_kernel(groups, src_ref, score_ref, out_ref, score_out, landing, score_in, send_sem, recv_sem):
+def dp_scatter_kernel(
+    groups, src_ref, score_ref, grads_ref, out_ref, score_out, mirror_out, landing, score_in, send_sem, recv_sem, mirror_sem
+):
     me = lax.axis_index("dp")
     home = lax.axis_index("expert")
     width = landing.shape[2]
@@ -33,6 +35,16 @@
             )
             copy.start()
             copies.append(copy)
+    mirror = pltpu.make_async_remote_copy(
+        src_ref=grads_ref,
+        dst_ref=mirror_out,
+        send_sem=mirror_sem.at[0],
+        recv_sem=mirror_sem.at[1],
+        device_id=(home, groups - 1 - me),
+        device_id_type=MESH_IDS,
+    )
+    mirror.start()
+    copies.append(mirror)
     for copy in copies:
         copy.wait()
     own = pl.multiple_of(me * width, 128)
@@ -53,7 +65,7 @@
     score_out[...] = score
 
 
-def dp_scatter(partial, score, groups):
+def dp_scatter(partial, score, grads, groups):
     rows, full = partial.shape
     width = full // groups
     return pl.pallas_call(
@@ -61,17 +73,19 @@
         out_shape=(
             jax.ShapeDtypeStruct((rows, width), partial.dtype),
             jax.ShapeDtypeStruct(score.shape, score.dtype),
+            jax.ShapeDtypeStruct(grads.shape, grads.dtype),
         ),
-        in_specs=[pl.BlockSpec(memory_space=pltpu.VMEM)] * 2,
-        out_specs=(pl.BlockSpec(memory_space=pltpu.VMEM), pl.BlockSpec(memory_space=pltpu.VMEM)),
+        in_specs=[pl.BlockSpec(memory_space=pltpu.VMEM)] * 3,
+        out_specs=tuple(pl.BlockSpec(memory_space=pltpu.VMEM) for _ in range(3)),
         scratch_shapes=[
             pltpu.VMEM((groups, rows, width), partial.dtype),
             pltpu.VMEM((groups,) + score.shape, score.dtype),
             pltpu.SemaphoreType.DMA((groups, 2)),
             pltpu.SemaphoreType.DMA((groups, 2)),
+            pltpu.SemaphoreType.DMA((2,)),
         ],
         compiler_params=pltpu.CompilerParams(collective_id=0, has_side_effects=True),
-    )(partial, score)
+    )(partial, score, grads)
 
 
 def dp_gather_kernel(groups, width, src_ref, x_ref, dy_ref, local_sem, send_sem, recv_sem):
@@ -205,16 +219,17 @@
     scaled = gate_rows[:, None] * dy_rows
     contract_rows = (((0,), (0,)), ((), ()))
     computed = (grad_gate, grad_up, hidden)
-    mirrored = lax.ppermute(computed, "dp", [(g, groups - 1 - g) for g in range(groups)])
-    mine = tuple(jnp.where(own_flag == 1, far, near) for far, near in zip(mirrored, computed))
+    slots = capacity * expert_count
+    score_tile = jnp.zeros((8 * 128,), jnp.float32).at[:slots].set(score_part).reshape(8, 128)
+    share, score_sum, mirrored = dp_scatter(
+        input_part.astype(jnp.bfloat16), score_tile, jnp.stack(computed), groups
+    )
+    mine = tuple(jnp.where(own_flag == 1, mirrored[k], computed[k]) for k in range(3))
     grad_wgate = lax.dot_general(
         mine[0], x_rows, contract_rows, preferred_element_type=jnp.float32
     )
     grad_wup = lax.dot_general(mine[1], x_rows, contract_rows, preferred_element_type=jnp.float32)
     grad_wdown = lax.dot_general(mine[2], scaled, contract_rows, preferred_element_type=jnp.float32)
-    slots = capacity * expert_count
-    score_tile = jnp.zeros((8 * 128,), jnp.float32).at[:slots].set(score_part).reshape(8, 128)
-    share, score_sum = dp_scatter(input_part.astype(jnp.bfloat16), score_tile, groups)
     score_col = jnp.zeros((slots, 128), jnp.bfloat16).at[:, 0].set(
         score_sum.reshape(-1)[:slots].astype(jnp.bfloat16)
     )

time: 774 us -> 746 us (0.964)
  waiting for transfers between devices: 166 us -> 127 us
  Pallas kernels: 493 us -> 512 us
    ppermute x3 -> x0, waiting for transfers between devices: 74.4 us -> none  [shards(): lax.ppermute(computed, 'dp', [(g, groups - 1 - g) for g in range(groups)])]
    all_to_all x1, waiting for transfers between devices: 0.01 us -> 34.9 us  [shards(): lax.all_to_all(reduced, 'expert', split_axis=0, concat_axis=0, tiled=True)]
    pallas_call x1, Pallas kernels: 166 us -> 185 us  [dp_scatter(): pl.pallas_call(lambda *refs: dp_scatter_kernel(groups, *refs), out_shape=...]
  transfers between devices with their start and end apart: 8 -> 5, of which waited for: 4 -> 2; matrix products, arithmetic and copies ran while one was open for 3% -> 3% of each run, Pallas kernels for 42% -> 44%
where the time goes in v13:
time: 746 us; the launch traced here: 745 us
  Pallas kernels  512 us (69%)
  waiting for transfers between devices  127 us (17%)
  local copies, waits for them, and re-layouts  34.1 us (5%)
  starting transfers between devices  31.3 us (4%)
  matrix products  28.6 us (4%)
  other arithmetic  10.7 us (1%)
    pallas_call x1, Pallas kernels, dp_gather(): pl.pallas_call(lambda *refs: dp_gather_kernel(groups, width, *refs), out_...  327 us
    pallas_call x1, Pallas kernels, dp_scatter(): pl.pallas_call(lambda *refs: dp_scatter_kernel(groups, *refs), out_shape=...  185 us
    all_to_all x1, waiting for transfers between devices, shards(): lax.all_to_all(outgoing, 'expert', split_axis=0, concat_axis=0, tiled=True)  91.9 us
    all_to_all x1, waiting for transfers between devices, shards(): lax.all_to_all(reduced, 'expert', split_axis=0, concat_axis=0, tiled=True)  34.9 us
  transfers between devices with their start and end apart: 5, of which 2 were waited for; matrix products, arithmetic and copies ran while one was open for 3% of the time, Pallas kernels for 44%

profile of v13, /device:TPU:35, one launch (start us, length us, event | category | flops | bytes accessed | tf_op | source)
XLA Modules:
  0.0 744.8 jit_solution(4823946226138356063)
XLA Ops:
  5.8 2.4 scatter_custom_fusion
  8.3 4.3 gather_fusion.2
  14.5 2.8 gather_fusion
  17.3 2.8 gather_fusion.1
  20.6 3.0 all_to_all.15
  23.6 14.4 %all-to-all-start = ((bf16[64,10,2176]{2,1,0:T(8,128)(2,1)}), bf16[64,10,2176]{2,1,0:T(8,128)(2,1)}, u32[]{:S(2)}, u32[]{:S(2)}) async-start(bf16[64,10,2176]{2,1,0:T(8,128)(2,1)} %all_to_all.15), calls=%async_computation | async-start | bytes 8912896 | tf_op jit(solution)/shard_map/all_to_all | solution.py:199
  38.0 4.8 collective-permute-start.1
  42.9 4.4 collective-permute-start
  48.6 91.9 %all-to-all-done = bf16[64,10,2176]{2,1,0:T(8,128)(2,1)} async-done(((bf16[64,10,2176]{2,1,0:T(8,128)(2,1)}), bf16[64,10,2176]{2,1,0:T(8,128)(2,1)}, u32[]{:S(2)}, u32[]{:S(2)}) %all-to-all-start) | async-done | bytes 2785312 | tf_op jit(solution)/shard_map/all_to_all | solution.py:199
  140.5 5.6 all_to_all.17.refs_0_
  146.1 327.1 %shard_map.119 = (bf16[640,4096]{1,0:T(8,128)(2,1)}, bf16[640,4096]{1,0:T(8,128)(2,1)}) custom-call(bf16[640,2176]{1,0:T(8,128)(2,1)} %all_to_all.17.refs_0_), custom_call_target="tpu_custom_call" | custom-call | tf_op jit(solution)/shard_map/pallas_call | solution.py:127
  474.5 4.7 fusion.19
  479.3 3.2 fusion.15
  482.6 3.4 multiply_reduce_fusion
  489.3 5.3 add_convert_fusion.refs_0_
  494.6 184.5 %shard_map.120 = (bf16[640,1024]{1,0:T(8,128)(2,1)}, f32[8,128]{1,0:T(8,128)}, bf16[3,640,192]{2,1,0:T(8,128)(2,1)}) custom-call(bf16[640,4096]{1,0:T(8,128)(2,1)} %add_convert_fusion.refs_0_, f32[8,128]{1,0:T(8,128)} %pad_bitcast_fusion.refs_1_, bf16[3,640,192]{2,1,0:T(8,128)(2,1)} %pad_maximum_fusion.refs_2_), custom_call_target="tpu_custom_call" | custom-call | tf_op jit(solution)/shard_map/pallas_call | solution.py:71
  683.8 7.7 %all-to-all-start.1 = ((bf16[64,10,1152]{2,1,0:T(8,128)(2,1)}), bf16[64,10,1152]{2,1,0:T(8,128)(2,1)}, u32[]{:S(2)}, u32[]{:S(2)}) async-start(bf16[64,10,1152]{2,1,0:T(8,128)(2,1)} %all_to_all.18), calls=%async_computation.1 | async-start | bytes 4718592 | tf_op jit(solution)/shard_map/all_to_all | solution.py:237
  691.5 5.2 fusion.6
  696.7 2.6 fusion.7
  699.3 2.6 fusion.8
  701.9 34.9 %all-to-all-done.1 = bf16[64,10,1152]{2,1,0:T(8,128)(2,1)} async-done(((bf16[64,10,1152]{2,1,0:T(8,128)(2,1)}), bf16[64,10,1152]{2,1,0:T(8,128)(2,1)}, u32[]{:S(2)}, u32[]{:S(2)}) %all-to-all-start.1) | async-done | bytes 1474592 | tf_op jit(solution)/shard_map/all_to_all | solution.py:237
  736.8 2.7 all_to_all.20
  739.5 2.1 gather_fusion.3
  741.9 2.2 slice_reduce_fusion
  (82 shorter events, 18.4 us)
Async XLA Ops:
  23.6 14.4 %copy-start = (bf16[1,192,4096]{2,1,0:T(8,128)(2,1)S(1)}, bf16[1,192,4096]{2,1,0:T(8,128)(2,1)}, u32[]{:S(2)}) copy-start(bf16[1,192,4096]{2,1,0:T(8,128)(2,1)} %param.17) | copy-start | bytes 4718596
  23.6 23.7 %copy-start.6 = (s32[32]{0:T(128)S(1)}, s32[32]{0:T(128)}, u32[]{:S(2)}) copy-start(s32[32]{0:T(128)} %param.21) | copy-start | bytes 388
  23.6 116.9 %all-to-all-start = ((bf16[64,10,2176]{2,1,0:T(8,128)(2,1)}), bf16[64,10,2176]{2,1,0:T(8,128)(2,1)}, u32[]{:S(2)}, u32[]{:S(2)}) async-start(bf16[64,10,2176]{2,1,0:T(8,128)(2,1)} %all_to_all.15), calls=%async_computation | async-start | bytes 8912896 | tf_op jit(solution)/shard_map/all_to_all | solution.py:199
  38.0 436.5 %collective-permute-start.1 = (bf16[1,192,4096]{2,1,0:T(8,128)(2,1)S(1)}, bf16[1,192,4096]{2,1,0:T(8,128)(2,1)S(1)}, u32[]{:S(2)}, u32[]{:S(2)}) collective-permute-start(bf16[1,192,4096]{2,1,0:T(8,128)(2,1)S(1)} %copy-done), channel_id=1, source_target_pairs={{0,131},{1,130},{2,129},{3,128},{4,135},{5,134},{6,133},{7,132},{8... | collective-permute-start | bytes 4718600 | tf_op jit(solution)/shard_map/ppermute | solution.py:153
  42.8 436.4 %collective-permute-start.2 = (bf16[1,192,4096]{2,1,0:T(8,128)(2,1)}, bf16[1,192,4096]{2,1,0:T(8,128)(2,1)}, u32[]{:S(2)}, u32[]{:S(2)}) collective-permute-start(bf16[1,192,4096]{2,1,0:T(8,128)(2,1)} %param.16), channel_id=1, source_target_pairs={{0,131},{1,130},{2,129},{3,128},{4,135},{5,134},{6,133},{7,132},{8... | collective-permute-start | bytes 4718600 | tf_op jit(solution)/shard_map/ppermute | solution.py:153
  42.9 439.6 %collective-permute-start = (bf16[1,192,4096]{2,1,0:T(8,128)(2,1)}, bf16[1,192,4096]{2,1,0:T(8,128)(2,1)}, u32[]{:S(2)}, u32[]{:S(2)}) collective-permute-start(bf16[1,192,4096]{2,1,0:T(8,128)(2,1)} %param.18), channel_id=1, source_target_pairs={{0,131},{1,130},{2,129},{3,128},{4,135},{5,134},{6,133},{7,132},{8... | collective-permute-start | bytes 4718600 | tf_op jit(solution)/shard_map/ppermute | solution.py:153
  473.2 6.0 slice-start
  474.5 4.8 copy-start.2
  474.5 4.8 slice-start.1
  474.5 4.8 copy-start.4
  474.5 8.1 %slice-start.4 = ((s8[5242880]{0:T(1024)(128)(4,1)}), s8[4194304]{0:T(1024)(128)(4,1)S(1)}, s32[]{:S(2)}) async-start(s8[5242880]{0:T(1024)(128)(4,1)} %bitcast.88), calls=%async_computation.6 | async-start | bytes 8388608
  479.2 3.3 slice-start.5
  479.3 3.3 copy-start.7
  482.6 5.2 copy-start.3
  486.0 1.8 copy-start.1
  683.8 7.7 %copy-start.5 = (bf16[3,640,192]{2,1,0:T(8,128)(2,1)S(1)}, bf16[3,640,192]{2,1,0:T(8,128)(2,1)}, u32[]{:S(2)}) copy-start(bf16[3,640,192]{2,1,0:T(8,128)(2,1)} %get-tuple-element.50) | copy-start | bytes 2211844
  683.8 12.9 %slice-start.2 = ((s8[5242880]{0:T(1024)(128)(4,1)}), s8[1048576]{0:T(1024)(128)(4,1)S(1)}, s32[]{:S(2)}) async-start(s8[5242880]{0:T(1024)(128)(4,1)} %bitcast.77), calls=%async_computation.4 | async-start | bytes 2097152
  683.8 53.0 %all-to-all-start.1 = ((bf16[64,10,1152]{2,1,0:T(8,128)(2,1)}), bf16[64,10,1152]{2,1,0:T(8,128)(2,1)}, u32[]{:S(2)}, u32[]{:S(2)}) async-start(bf16[64,10,1152]{2,1,0:T(8,128)(2,1)} %all_to_all.18), calls=%async_computation.1 | async-start | bytes 4718592 | tf_op jit(solution)/shard_map/all_to_all | solution.py:237
  691.5 5.2 slice-start.3
  691.5 7.8 %slice-start.6 = ((s8[5242880]{0:T(1024)(128)(4,1)}), s8[4194304]{0:T(1024)(128)(4,1)S(1)}, s32[]{:S(2)}) async-start(s8[5242880]{0:T(1024)(128)(4,1)} %bitcast.90), calls=%async_computation.8 | async-start | bytes 8388608
  696.7 2.6 slice-start.7

commit v14 on v13

--- a/solution.py
+++ b/solution.py
@@ -169,11 +169,6 @@
     quarter = model_width // groups
     own_flag = pair_lookup(jnp.reshape(my_slot, (1,)), swap_flags, half_axis)[0]
     flat_ids = expert_ids.reshape(-1)
-    weights = (gate_weight, up_weight, down_weight)
-    arrived = mirror_swap((gate_weight, up_weight, down_weight), expert_count, groups)
-    weights = tuple(
-        (jnp.where(own_flag == 1, fresh, stay) for fresh, stay in zip(arrived, weights))
-    )
     flipped = pair_lookup(flat_ids, swap_flags, half_axis)
     target = jnp.where(flipped == 1, (flat_ids + half_axis) % expert_count, flat_ids)
     copies = row_count * routed
@@ -197,6 +192,12 @@
     gate_cols = jnp.zeros((expert_count * capacity, 128), jnp.bfloat16).at[:, 0].set(gate_buffer)
     outgoing = jnp.concatenate([x_buffer, dy_buffer, gate_cols], axis=1)
     arrived = lax.all_to_all(outgoing, "expert", split_axis=0, concat_axis=0, tiled=True)
+    weights = (gate_weight, up_weight, down_weight)
+    held, arrived = lax.optimization_barrier((weights, arrived))
+    moved = mirror_swap(held, expert_count, groups)
+    weights = tuple(
+        (jnp.where(own_flag == 1, fresh, stay) for fresh, stay in zip(moved, weights))
+    )
     x_rows, dy_rows = dp_gather(arrived, groups, quarter)
     gate_rows = arrived[:, 2 * quarter]
     w_gate = weights[0][0]

time: 746 us -> 695 us (0.932)
  blocking collectives: 0 us -> 119 us
  waiting for transfers between devices: 127 us -> 31.5 us
  Pallas kernels: 512 us -> 456 us
  starting transfers between devices: 31.3 us -> 16.1 us
    all_to_all x0 -> x1, blocking collectives: none -> 119 us  [shards(): lax.all_to_all(outgoing, 'expert', split_axis=0, concat_axis=0, tiled=True)]
    all_to_all x1 -> x0, waiting for transfers between devices: 91.9 us -> none  [shards(): lax.all_to_all(outgoing, 'expert', split_axis=0, concat_axis=0, tiled=True)]
    pallas_call x1, Pallas kernels: 327 us -> 264 us  [dp_gather(): pl.pallas_call(lambda *refs: dp_gather_kernel(groups, width, *refs), out_...]
    all_to_all x1 -> x0, starting transfers between devices: 14.4 us -> none  [shards(): lax.all_to_all(outgoing, 'expert', split_axis=0, concat_axis=0, tiled=True)]
    pallas_call x1, Pallas kernels: 185 us -> 193 us  [dp_scatter(): pl.pallas_call(lambda *refs: dp_scatter_kernel(groups, *refs), out_shape=...]
  transfers between devices with their start and end apart: 5 -> 4, of which waited for: 2 -> 1; matrix products, arithmetic and copies ran while one was open for 3% -> 3% of each run, Pallas kernels for 44% -> 38%
where the time goes in v14:
time: 695 us; the launch traced here: 694 us
  Pallas kernels  456 us (66%)
  blocking collectives  119 us (17%)
  local copies, waits for them, and re-layouts  34.3 us (5%)
  waiting for transfers between devices  31.5 us (5%)
  matrix products  24.1 us (3%)
  starting transfers between devices  16.1 us (2%)
  other arithmetic  10.7 us (2%)
    pallas_call x1, Pallas kernels, dp_gather(): pl.pallas_call(lambda *refs: dp_gather_kernel(groups, width, *refs), out_...  264 us
    pallas_call x1, Pallas kernels, dp_scatter(): pl.pallas_call(lambda *refs: dp_scatter_kernel(groups, *refs), out_shape=...  193 us
    all_to_all x1, blocking collectives, shards(): lax.all_to_all(outgoing, 'expert', split_axis=0, concat_axis=0, tiled=True)  119 us
    all_to_all x1, waiting for transfers between devices, shards(): lax.all_to_all(reduced, 'expert', split_axis=0, concat_axis=0, tiled=True)  31.5 us
  transfers between devices with their start and end apart: 4, of which 1 were waited for; matrix products, arithmetic and copies ran while one was open for 3% of the time, Pallas kernels for 38%

profile of v14, /device:TPU:35, one launch (start us, length us, event | category | flops | bytes accessed | tf_op | source)
XLA Modules:
  0.0 693.7 jit_solution(16479464338638612856)
XLA Ops:
  5.8 2.4 scatter_custom_fusion
  8.3 4.3 gather_fusion.2
  14.5 2.8 gather_fusion
  17.3 2.8 gather_fusion.1
  20.6 3.0 all_to_all.16
  23.6 118.9 %all_to_all.24 = bf16[64,10,2176]{2,1,0:T(8,128)(2,1)} all-to-all(bf16[64,10,2176]{2,1,0:T(8,128)(2,1)} %all_to_all.16), channel_id=1, replica_groups=mesh['expert'=64,'dp'=4] {'expert'}, dimensions={0} | all-to-all | bytes 5570560 | tf_op jit(solution)/shard_map/all_to_all | solution.py:194
  142.5 5.7 all_to_all.18.refs_0_
  148.4 4.3 collective-permute-start.2
  154.1 263.7 %shard_map.119 = (bf16[640,4096]{1,0:T(8,128)(2,1)}, bf16[640,4096]{1,0:T(8,128)(2,1)}) custom-call(bf16[640,2176]{1,0:T(8,128)(2,1)} %all_to_all.18.refs_0_), custom_call_target="tpu_custom_call" | custom-call | tf_op jit(solution)/shard_map/pallas_call | solution.py:127
  419.2 4.7 fusion.19
  424.0 1.7 fusion.15
  425.8 1.9 multiply_reduce_fusion
  429.4 1.5 fusion.17
  430.9 3.9 add_convert_fusion.refs_0_
  434.8 192.7 %shard_map.120 = (bf16[640,1024]{1,0:T(8,128)(2,1)}, f32[8,128]{1,0:T(8,128)}, bf16[3,640,192]{2,1,0:T(8,128)(2,1)}) custom-call(bf16[640,4096]{1,0:T(8,128)(2,1)} %add_convert_fusion.refs_0_, f32[8,128]{1,0:T(8,128)} %pad_bitcast_fusion.refs_1_, bf16[3,640,192]{2,1,0:T(8,128)(2,1)} %pad_maximum_fusion.refs_2_), custom_call_target="tpu_custom_call" | custom-call | tf_op jit(solution)/shard_map/pallas_call | solution.py:71
  630.6 1.7 all_to_all.19
  632.2 11.4 %all-to-all-start.1 = ((bf16[64,10,1152]{2,1,0:T(8,128)(2,1)}), bf16[64,10,1152]{2,1,0:T(8,128)(2,1)}, u32[]{:S(2)}, u32[]{:S(2)}) async-start(bf16[64,10,1152]{2,1,0:T(8,128)(2,1)} %all_to_all.19), calls=%async_computation.1 | async-start | bytes 4718592 | tf_op jit(solution)/shard_map/all_to_all | solution.py:238
  643.7 5.2 fusion.6
  648.9 2.6 fusion.7
  651.5 2.6 fusion.8
  654.2 31.5 %all-to-all-done.1 = bf16[64,10,1152]{2,1,0:T(8,128)(2,1)} async-done(((bf16[64,10,1152]{2,1,0:T(8,128)(2,1)}), bf16[64,10,1152]{2,1,0:T(8,128)(2,1)}, u32[]{:S(2)}, u32[]{:S(2)}) %all-to-all-start.1) | async-done | bytes 1474592 | tf_op jit(solution)/shard_map/all_to_all | solution.py:238
  685.6 2.7 all_to_all.21
  688.3 2.1 gather_fusion.3
  690.8 2.2 slice_reduce_fusion
  (81 shorter events, 15.5 us)
Async XLA Ops:
  142.5 5.8 copy-start
  142.5 10.4 %copy-start.6 = (s32[32]{0:T(128)S(1)}, s32[32]{0:T(128)}, u32[]{:S(2)}) copy-start(s32[32]{0:T(128)} %param.21) | copy-start | bytes 388
  148.2 270.9 %collective-permute-start.1 = (bf16[1,192,4096]{2,1,0:T(8,128)(2,1)S(1)}, bf16[1,192,4096]{2,1,0:T(8,128)(2,1)S(1)}, u32[]{:S(2)}, u32[]{:S(2)}) collective-permute-start(bf16[1,192,4096]{2,1,0:T(8,128)(2,1)S(1)} %copy-done), channel_id=1, source_target_pairs={{0,131},{1,130},{2,129},{3,128},{4,135},{5,134},{6,133},{7,132},{8... | collective-permute-start | bytes 4718600 | tf_op jit(solution)/shard_map/ppermute | solution.py:153
  148.4 275.5 %collective-permute-start.2 = (bf16[1,192,4096]{2,1,0:T(8,128)(2,1)}, bf16[1,192,4096]{2,1,0:T(8,128)(2,1)}, u32[]{:S(2)}, u32[]{:S(2)}) collective-permute-start(bf16[1,192,4096]{2,1,0:T(8,128)(2,1)} %param.16), channel_id=1, source_target_pairs={{0,131},{1,130},{2,129},{3,128},{4,135},{5,134},{6,133},{7,132},{8... | collective-permute-start | bytes 4718600 | tf_op jit(solution)/shard_map/ppermute | solution.py:153
  152.7 273.0 %collective-permute-start = (bf16[1,192,4096]{2,1,0:T(8,128)(2,1)}, bf16[1,192,4096]{2,1,0:T(8,128)(2,1)}, u32[]{:S(2)}, u32[]{:S(2)}) collective-permute-start(bf16[1,192,4096]{2,1,0:T(8,128)(2,1)} %param.18), channel_id=1, source_target_pairs={{0,131},{1,130},{2,129},{3,128},{4,135},{5,134},{6,133},{7,132},{8... | collective-permute-start | bytes 4718600 | tf_op jit(solution)/shard_map/ppermute | solution.py:153
  417.9 6.0 slice-start
  419.1 4.8 copy-start.2
  419.1 4.8 slice-start.1
  419.1 4.8 copy-start.4
  419.1 6.5 slice-start.4
  423.9 1.8 slice-start.5
  423.9 1.9 copy-start.7
  425.8 3.6 copy-start.3
  427.6 1.8 copy-start.1
  632.2 11.5 %copy-start.5 = (bf16[3,640,192]{2,1,0:T(8,128)(2,1)S(1)}, bf16[3,640,192]{2,1,0:T(8,128)(2,1)}, u32[]{:S(2)}) copy-start(bf16[3,640,192]{2,1,0:T(8,128)(2,1)} %get-tuple-element.58) | copy-start | bytes 2211844
  632.2 16.7 %slice-start.2 = ((s8[5242880]{0:T(1024)(128)(4,1)}), s8[1048576]{0:T(1024)(128)(4,1)S(1)}, s32[]{:S(2)}) async-start(s8[5242880]{0:T(1024)(128)(4,1)} %bitcast.77), calls=%async_computation.4 | async-start | bytes 2097152
  632.2 53.4 %all-to-all-start.1 = ((bf16[64,10,1152]{2,1,0:T(8,128)(2,1)}), bf16[64,10,1152]{2,1,0:T(8,128)(2,1)}, u32[]{:S(2)}, u32[]{:S(2)}) async-start(bf16[64,10,1152]{2,1,0:T(8,128)(2,1)} %all_to_all.19), calls=%async_computation.1 | async-start | bytes 4718592 | tf_op jit(solution)/shard_map/all_to_all | solution.py:238
  643.7 5.2 slice-start.3
  643.7 7.8 %slice-start.6 = ((s8[5242880]{0:T(1024)(128)(4,1)}), s8[4194304]{0:T(1024)(128)(4,1)S(1)}, s32[]{:S(2)}) async-start(s8[5242880]{0:T(1024)(128)(4,1)} %bitcast.90), calls=%async_computation.8 | async-start | bytes 8388608
  648.9 2.6 slice-start.7

commit v15 on v14

--- a/solution.py
+++ b/solution.py
@@ -20,8 +20,10 @@
         pl.semaphore_signal(barrier, 1, device_id=(home, peer), device_id_type=MESH_IDS)
     pl.semaphore_wait(barrier, groups - 1)
     copies = []
-    for step in range(1, groups):
-        peer = lax.rem(me + step, groups)
+    far = (groups - 1) * (1 - me // 2)
+    middle = lax.rem(3 * me + 2, 5)
+    for peer in (far, middle, groups * (groups - 1) // 2 - me - far - middle):
+        step = lax.rem(peer - me + groups, groups)
         for part, (source, target) in enumerate(
             ((src_ref.at[:, pl.ds(pl.multiple_of(peer * width, 128), width)], landing), (score_ref, score_in))
         ):

time: 695 us -> 689 us (level)
  no operation moved by 1% of the time
where the time goes in v15:
time: 689 us
  Pallas kernels  455 us (66%)
  blocking collectives  119 us (17%)
  local copies, waits for them, and re-layouts  34.2 us (5%)
  matrix products  28.6 us (4%)
  waiting for transfers between devices  25.6 us (4%)
  starting transfers between devices  14.5 us (2%)
  other arithmetic  10.7 us (2%)
    pallas_call x1, Pallas kernels, dp_gather(): pl.pallas_call(lambda *refs: dp_gather_kernel(groups, width, *refs), out_...  264 us
    pallas_call x1, Pallas kernels, dp_scatter(): pl.pallas_call(lambda *refs: dp_scatter_kernel(groups, *refs), out_shape=...  191 us
    all_to_all x1, blocking collectives, shards(): lax.all_to_all(outgoing, 'expert', split_axis=0, concat_axis=0, tiled=True)  119 us
    all_to_all x1, waiting for transfers between devices, shards(): lax.all_to_all(reduced, 'expert', split_axis=0, concat_axis=0, tiled=True)  25.6 us
  transfers between devices with their start and end apart: 4, of which 1 were waited for; matrix products, arithmetic and copies ran while one was open for 3% of the time, Pallas kernels for 38%

profile of v15, /device:TPU:35, one launch (start us, length us, event | category | flops | bytes accessed | tf_op | source)
XLA Modules:
  0.0 688.7 jit_solution(12669994275169672033)
XLA Ops:
  5.8 2.4 scatter_custom_fusion
  8.3 4.3 gather_fusion.2
  14.5 2.8 gather_fusion
  17.3 2.8 gather_fusion.1
  20.6 3.0 all_to_all.16
  23.6 118.9 %all_to_all.24 = bf16[64,10,2176]{2,1,0:T(8,128)(2,1)} all-to-all(bf16[64,10,2176]{2,1,0:T(8,128)(2,1)} %all_to_all.16), channel_id=1, replica_groups=mesh['expert'=64,'dp'=4] {'expert'}, dimensions={0} | all-to-all | bytes 5570560 | tf_op jit(solution)/shard_map/all_to_all | solution.py:196
  142.5 5.7 all_to_all.18.refs_0_
  148.4 4.3 collective-permute-start.2
  154.1 263.7 %shard_map.119 = (bf16[640,4096]{1,0:T(8,128)(2,1)}, bf16[640,4096]{1,0:T(8,128)(2,1)}) custom-call(bf16[640,2176]{1,0:T(8,128)(2,1)} %all_to_all.18.refs_0_), custom_call_target="tpu_custom_call" | custom-call | tf_op jit(solution)/shard_map/pallas_call | solution.py:129
  419.2 4.7 fusion.19
  424.0 3.2 fusion.15
  427.3 3.4 multiply_reduce_fusion
  432.4 1.5 fusion.17
  434.0 5.3 add_convert_fusion.refs_0_
  439.3 190.8 %shard_map.120 = (bf16[640,1024]{1,0:T(8,128)(2,1)}, f32[8,128]{1,0:T(8,128)}, bf16[3,640,192]{2,1,0:T(8,128)(2,1)}) custom-call(bf16[640,4096]{1,0:T(8,128)(2,1)} %add_convert_fusion.refs_0_, f32[8,128]{1,0:T(8,128)} %pad_bitcast_fusion.refs_1_, bf16[3,640,192]{2,1,0:T(8,128)(2,1)} %pad_maximum_fusion.refs_2_), custom_call_target="tpu_custom_call" | custom-call | tf_op jit(solution)/shard_map/pallas_call | solution.py:73
  633.1 1.7 all_to_all.19
  634.7 9.9 %all-to-all-start.1 = ((bf16[64,10,1152]{2,1,0:T(8,128)(2,1)}), bf16[64,10,1152]{2,1,0:T(8,128)(2,1)}, u32[]{:S(2)}, u32[]{:S(2)}) async-start(bf16[64,10,1152]{2,1,0:T(8,128)(2,1)} %all_to_all.19), calls=%async_computation.1 | async-start | bytes 4718592 | tf_op jit(solution)/shard_map/all_to_all | solution.py:240
  644.7 5.2 fusion.6
  649.9 2.6 fusion.7
  652.5 2.6 fusion.8
  655.1 25.6 %all-to-all-done.1 = bf16[64,10,1152]{2,1,0:T(8,128)(2,1)} async-done(((bf16[64,10,1152]{2,1,0:T(8,128)(2,1)}), bf16[64,10,1152]{2,1,0:T(8,128)(2,1)}, u32[]{:S(2)}, u32[]{:S(2)}) %all-to-all-start.1) | async-done | bytes 1474592 | tf_op jit(solution)/shard_map/all_to_all | solution.py:240
  680.7 2.7 all_to_all.21
  683.3 2.1 gather_fusion.3
  685.8 2.2 slice_reduce_fusion
  (81 shorter events, 15.5 us)
Async XLA Ops:
  142.5 5.8 copy-start
  142.5 10.4 %copy-start.6 = (s32[32]{0:T(128)S(1)}, s32[32]{0:T(128)}, u32[]{:S(2)}) copy-start(s32[32]{0:T(128)} %param.21) | copy-start | bytes 388
  148.2 270.9 %collective-permute-start.1 = (bf16[1,192,4096]{2,1,0:T(8,128)(2,1)S(1)}, bf16[1,192,4096]{2,1,0:T(8,128)(2,1)S(1)}, u32[]{:S(2)}, u32[]{:S(2)}) collective-permute-start(bf16[1,192,4096]{2,1,0:T(8,128)(2,1)S(1)} %copy-done), channel_id=1, source_target_pairs={{0,131},{1,130},{2,129},{3,128},{4,135},{5,134},{6,133},{7,132},{8... | collective-permute-start | bytes 4718600 | tf_op jit(solution)/shard_map/ppermute | solution.py:155
  148.4 275.5 %collective-permute-start.2 = (bf16[1,192,4096]{2,1,0:T(8,128)(2,1)}, bf16[1,192,4096]{2,1,0:T(8,128)(2,1)}, u32[]{:S(2)}, u32[]{:S(2)}) collective-permute-start(bf16[1,192,4096]{2,1,0:T(8,128)(2,1)} %param.16), channel_id=1, source_target_pairs={{0,131},{1,130},{2,129},{3,128},{4,135},{5,134},{6,133},{7,132},{8... | collective-permute-start | bytes 4718600 | tf_op jit(solution)/shard_map/ppermute | solution.py:155
  152.7 274.5 %collective-permute-start = (bf16[1,192,4096]{2,1,0:T(8,128)(2,1)}, bf16[1,192,4096]{2,1,0:T(8,128)(2,1)}, u32[]{:S(2)}, u32[]{:S(2)}) collective-permute-start(bf16[1,192,4096]{2,1,0:T(8,128)(2,1)} %param.18), channel_id=1, source_target_pairs={{0,131},{1,130},{2,129},{3,128},{4,135},{5,134},{6,133},{7,132},{8... | collective-permute-start | bytes 4718600 | tf_op jit(solution)/shard_map/ppermute | solution.py:155
  417.9 6.0 slice-start
  419.1 4.8 copy-start.2
  419.1 4.8 slice-start.1
  419.1 4.8 copy-start.4
  419.1 8.1 %slice-start.4 = ((s8[5242880]{0:T(1024)(128)(4,1)}), s8[4194304]{0:T(1024)(128)(4,1)S(1)}, s32[]{:S(2)}) async-start(s8[5242880]{0:T(1024)(128)(4,1)} %bitcast.88), calls=%async_computation.6 | async-start | bytes 8388608
  423.9 3.3 slice-start.5
  423.9 3.3 copy-start.7
  427.2 5.2 copy-start.3
  430.7 1.8 copy-start.1
  634.7 9.9 %copy-start.5 = (bf16[3,640,192]{2,1,0:T(8,128)(2,1)S(1)}, bf16[3,640,192]{2,1,0:T(8,128)(2,1)}, u32[]{:S(2)}) copy-start(bf16[3,640,192]{2,1,0:T(8,128)(2,1)} %get-tuple-element.58) | copy-start | bytes 2211844
  634.7 15.2 %slice-start.2 = ((s8[5242880]{0:T(1024)(128)(4,1)}), s8[1048576]{0:T(1024)(128)(4,1)S(1)}, s32[]{:S(2)}) async-start(s8[5242880]{0:T(1024)(128)(4,1)} %bitcast.77), calls=%async_computation.4 | async-start | bytes 2097152
  634.7 46.0 %all-to-all-start.1 = ((bf16[64,10,1152]{2,1,0:T(8,128)(2,1)}), bf16[64,10,1152]{2,1,0:T(8,128)(2,1)}, u32[]{:S(2)}, u32[]{:S(2)}) async-start(bf16[64,10,1152]{2,1,0:T(8,128)(2,1)} %all_to_all.19), calls=%async_computation.1 | async-start | bytes 4718592 | tf_op jit(solution)/shard_map/all_to_all | solution.py:240
  644.6 5.2 slice-start.3
  644.6 7.8 %slice-start.6 = ((s8[5242880]{0:T(1024)(128)(4,1)}), s8[4194304]{0:T(1024)(128)(4,1)S(1)}, s32[]{:S(2)}) async-start(s8[5242880]{0:T(1024)(128)(4,1)} %bitcast.90), calls=%async_computation.8 | async-start | bytes 8388608
  649.9 2.6 slice-start.7

commit v16 on v15

--- a/solution.py
+++ b/solution.py
@@ -100,8 +100,10 @@
     pl.semaphore_wait(barrier, groups - 1)
     mine = pl.ds(pl.multiple_of(me * width, 128), width)
     copies = []
-    for step in range(1, groups):
-        peer = lax.rem(me + step, groups)
+    far = (groups - 1) * (1 - me // 2)
+    middle = lax.rem(3 * me + 2, 5)
+    for peer in (far, middle, groups * (groups - 1) // 2 - me - far - middle):
+        step = lax.rem(peer - me + groups, groups)
         for part, dst in enumerate((x_ref, dy_ref)):
             copy = pltpu.make_async_remote_copy(
                 src_ref=src_ref.at[:, pl.ds(part * width, width)],

time: 689 us -> 689 us (level)
  transfers between devices with their start and end apart: 4 -> 4, of which waited for: 1 -> 1; matrix products, arithmetic and copies ran while one was open for 3% -> 3% of each run, Pallas kernels for 38% -> 39%
where the time goes in v16:
time: 689 us; the launch traced here: 687 us
  Pallas kernels  454 us (66%)
  blocking collectives  119 us (17%)
  local copies, waits for them, and re-layouts  34.2 us (5%)
  matrix products  28.6 us (4%)
  waiting for transfers between devices  25.6 us (4%)
  starting transfers between devices  13.9 us (2%)
  other arithmetic  10.7 us (2%)
    pallas_call x1, Pallas kernels, dp_gather(): pl.pallas_call(lambda *refs: dp_gather_kernel(groups, width, *refs), out_...  270 us
    pallas_call x1, Pallas kernels, dp_scatter(): pl.pallas_call(lambda *refs: dp_scatter_kernel(groups, *refs), out_shape=...  184 us
    all_to_all x1, blocking collectives, shards(): lax.all_to_all(outgoing, 'expert', split_axis=0, concat_axis=0, tiled=True)  119 us
    all_to_all x1, waiting for transfers between devices, shards(): lax.all_to_all(reduced, 'expert', split_axis=0, concat_axis=0, tiled=True)  25.6 us
  transfers between devices with their start and end apart: 4, of which 1 were waited for; matrix products, arithmetic and copies ran while one was open for 3% of the time, Pallas kernels for 39%

profile of v16, /device:TPU:35, one launch (start us, length us, event | category | flops | bytes accessed | tf_op | source)
XLA Modules:
  0.0 687.4 jit_solution(3056597664240790252)
XLA Ops:
  5.8 2.4 scatter_custom_fusion
  8.3 4.3 gather_fusion.2
  14.5 2.8 gather_fusion
  17.3 2.8 gather_fusion.1
  20.6 3.0 all_to_all.16
  23.6 118.9 %all_to_all.24 = bf16[64,10,2176]{2,1,0:T(8,128)(2,1)} all-to-all(bf16[64,10,2176]{2,1,0:T(8,128)(2,1)} %all_to_all.16), channel_id=1, replica_groups=mesh['expert'=64,'dp'=4] {'expert'}, dimensions={0} | all-to-all | bytes 5570560 | tf_op jit(solution)/shard_map/all_to_all | solution.py:198
  142.5 5.7 all_to_all.18.refs_0_
  148.4 4.3 collective-permute-start.2
  154.1 269.8 %shard_map.119 = (bf16[640,4096]{1,0:T(8,128)(2,1)}, bf16[640,4096]{1,0:T(8,128)(2,1)}) custom-call(bf16[640,2176]{1,0:T(8,128)(2,1)} %all_to_all.18.refs_0_), custom_call_target="tpu_custom_call" | custom-call | tf_op jit(solution)/shard_map/pallas_call | solution.py:131
  425.2 4.7 fusion.19
  430.0 3.2 fusion.15
  433.3 3.4 multiply_reduce_fusion
  438.5 1.5 fusion.17
  440.0 5.3 add_convert_fusion.refs_0_
  445.3 184.1 %shard_map.120 = (bf16[640,1024]{1,0:T(8,128)(2,1)}, f32[8,128]{1,0:T(8,128)}, bf16[3,640,192]{2,1,0:T(8,128)(2,1)}) custom-call(bf16[640,4096]{1,0:T(8,128)(2,1)} %add_convert_fusion.refs_0_, f32[8,128]{1,0:T(8,128)} %pad_bitcast_fusion.refs_1_, bf16[3,640,192]{2,1,0:T(8,128)(2,1)} %pad_maximum_fusion.refs_2_), custom_call_target="tpu_custom_call" | custom-call | tf_op jit(solution)/shard_map/pallas_call | solution.py:73
  632.4 1.7 all_to_all.19
  634.0 9.3 %all-to-all-start.1 = ((bf16[64,10,1152]{2,1,0:T(8,128)(2,1)}), bf16[64,10,1152]{2,1,0:T(8,128)(2,1)}, u32[]{:S(2)}, u32[]{:S(2)}) async-start(bf16[64,10,1152]{2,1,0:T(8,128)(2,1)} %all_to_all.19), calls=%async_computation.1 | async-start | bytes 4718592 | tf_op jit(solution)/shard_map/all_to_all | solution.py:242
  643.4 5.2 fusion.6
  648.6 2.6 fusion.7
  651.2 2.6 fusion.8
  653.8 25.6 %all-to-all-done.1 = bf16[64,10,1152]{2,1,0:T(8,128)(2,1)} async-done(((bf16[64,10,1152]{2,1,0:T(8,128)(2,1)}), bf16[64,10,1152]{2,1,0:T(8,128)(2,1)}, u32[]{:S(2)}, u32[]{:S(2)}) %all-to-all-start.1) | async-done | bytes 1474592 | tf_op jit(solution)/shard_map/all_to_all | solution.py:242
  679.4 2.7 all_to_all.21
  682.1 2.1 gather_fusion.3
  684.5 2.2 slice_reduce_fusion
  (81 shorter events, 15.5 us)
Async XLA Ops:
  142.5 5.8 copy-start
  142.5 10.4 %copy-start.6 = (s32[32]{0:T(128)S(1)}, s32[32]{0:T(128)}, u32[]{:S(2)}) copy-start(s32[32]{0:T(128)} %param.21) | copy-start | bytes 388
  148.2 276.9 %collective-permute-start.1 = (bf16[1,192,4096]{2,1,0:T(8,128)(2,1)S(1)}, bf16[1,192,4096]{2,1,0:T(8,128)(2,1)S(1)}, u32[]{:S(2)}, u32[]{:S(2)}) collective-permute-start(bf16[1,192,4096]{2,1,0:T(8,128)(2,1)S(1)} %copy-done), channel_id=1, source_target_pairs={{0,131},{1,130},{2,129},{3,128},{4,135},{5,134},{6,133},{7,132},{8... | collective-permute-start | bytes 4718600 | tf_op jit(solution)/shard_map/ppermute | solution.py:157
  148.4 281.6 %collective-permute-start.2 = (bf16[1,192,4096]{2,1,0:T(8,128)(2,1)}, bf16[1,192,4096]{2,1,0:T(8,128)(2,1)}, u32[]{:S(2)}, u32[]{:S(2)}) collective-permute-start(bf16[1,192,4096]{2,1,0:T(8,128)(2,1)} %param.16), channel_id=1, source_target_pairs={{0,131},{1,130},{2,129},{3,128},{4,135},{5,134},{6,133},{7,132},{8... | collective-permute-start | bytes 4718600 | tf_op jit(solution)/shard_map/ppermute | solution.py:157
  152.7 280.5 %collective-permute-start = (bf16[1,192,4096]{2,1,0:T(8,128)(2,1)}, bf16[1,192,4096]{2,1,0:T(8,128)(2,1)}, u32[]{:S(2)}, u32[]{:S(2)}) collective-permute-start(bf16[1,192,4096]{2,1,0:T(8,128)(2,1)} %param.18), channel_id=1, source_target_pairs={{0,131},{1,130},{2,129},{3,128},{4,135},{5,134},{6,133},{7,132},{8... | collective-permute-start | bytes 4718600 | tf_op jit(solution)/shard_map/ppermute | solution.py:157
  423.9 6.0 slice-start
  425.1 4.8 copy-start.2
  425.2 4.8 slice-start.1
  425.2 4.8 copy-start.4
  425.2 8.1 %slice-start.4 = ((s8[5242880]{0:T(1024)(128)(4,1)}), s8[4194304]{0:T(1024)(128)(4,1)S(1)}, s32[]{:S(2)}) async-start(s8[5242880]{0:T(1024)(128)(4,1)} %bitcast.88), calls=%async_computation.6 | async-start | bytes 8388608
  429.9 3.3 slice-start.5
  429.9 3.3 copy-start.7
  433.3 5.2 copy-start.3
  436.7 1.8 copy-start.1
  634.0 9.3 %copy-start.5 = (bf16[3,640,192]{2,1,0:T(8,128)(2,1)S(1)}, bf16[3,640,192]{2,1,0:T(8,128)(2,1)}, u32[]{:S(2)}) copy-start(bf16[3,640,192]{2,1,0:T(8,128)(2,1)} %get-tuple-element.58) | copy-start | bytes 2211844
  634.0 14.6 %slice-start.2 = ((s8[5242880]{0:T(1024)(128)(4,1)}), s8[1048576]{0:T(1024)(128)(4,1)S(1)}, s32[]{:S(2)}) async-start(s8[5242880]{0:T(1024)(128)(4,1)} %bitcast.77), calls=%async_computation.4 | async-start | bytes 2097152
  634.0 45.4 %all-to-all-start.1 = ((bf16[64,10,1152]{2,1,0:T(8,128)(2,1)}), bf16[64,10,1152]{2,1,0:T(8,128)(2,1)}, u32[]{:S(2)}, u32[]{:S(2)}) async-start(bf16[64,10,1152]{2,1,0:T(8,128)(2,1)} %all_to_all.19), calls=%async_computation.1 | async-start | bytes 4718592 | tf_op jit(solution)/shard_map/all_to_all | solution.py:242
  643.4 5.2 slice-start.3
  643.4 7.8 %slice-start.6 = ((s8[5242880]{0:T(1024)(128)(4,1)}), s8[4194304]{0:T(1024)(128)(4,1)S(1)}, s32[]{:S(2)}) async-start(s8[5242880]{0:T(1024)(128)(4,1)} %bitcast.90), calls=%async_computation.8 | async-start | bytes 8388608
  648.6 2.6 slice-start.7
